TPU v7x, 32 devices: a whole 2x2x4 slice. The times are simulated.
32 devices in a mesh: groups: 2 (over x), row: 16 (over z, y, core).
Axes of the slice: x: 2, y: 2, z: 4, core: 2. Of those that a mesh axis runs over, the one named last changes fastest.
Arguments:
- homolog_embedding: bfloat16 [128, 256, 64], P('groups', 'row'), parts along dimension 0, may hold values from -6 to 6
- pair_state_tiles: bfloat16 [512, 256, 128], P(('groups', 'row')), parts along dimension 0, may hold values from -6 to 6
- alignment_mask: int32 [128, 256], P('groups', 'row'), parts along dimension 0, may hold values 0 or 1
- token_real_mask: int32 [512], P('groups'), parts along dimension 0, may hold values 0 or 1
- lineup_standardize_scaling: float32 [64], replicated, may hold values from 0.1 to 1.9
- former_factor_proj: bfloat16 [64, 32], replicated, may hold values from -0.75 to 0.75
- latter_factor_proj: bfloat16 [64, 32], replicated, may hold values from -0.75 to 0.75
- outer_output_weight: bfloat16 [1024, 128], replicated, may hold values from -0.1875 to 0.1875
- pair_norm_gain: float32 [128], replicated, may hold values from 0.1 to 1.9
- pair_logit_weight: float32 [128, 8], replicated
- content_vector_proj: bfloat16 [64, 256], replicated, may hold values from -0.75 to 0.75
- sigmoid_switch_proj: bfloat16 [64, 256], replicated, may hold values from -0.75 to 0.75
- final_result_proj: bfloat16 [256, 64], replicated, may hold values from -0.375 to 0.375
Outputs:
- alignment_updated: bfloat16 [128, 256, 64], P('groups', 'row'), parts along dimension 0
- pair_updated: bfloat16 [512, 256, 128], P(('groups', 'row')), parts along dimension 0
There are 2 independent parts, one for each index of `groups`. A program takes and returns all parts, laid end to end along the dimension named above; an argument that names none is the same for every part. Nothing has to cross between parts.
All inputs are finite; a program needn't handle non-finite values. No bound on the sum of `alignment_mask` on one device may be relied on, other than what follows from the above.
Results may differ from a plain program's by a relative error of at most 0.007.
Values may be sent and summed in bfloat16 or wider, within the bound.
No kernel may reach another device: no remote copies, remote signals or barrier semaphores. Data moves between devices by JAX's collectives and lax.ppermute only.
A program may use at most 128 MiB of HBM per device.

v0:
```python
import functools

import jax
import jax.numpy as jnp
from jax import lax
from jax.experimental import pallas as pl
from jax.experimental.pallas import tpu as pltpu
from jax.sharding import PartitionSpec as P


F32 = jnp.float32
BF16 = jnp.bfloat16
VM = pl.BlockSpec(memory_space=pltpu.VMEM)
HB = pl.BlockSpec(memory_space=pltpu.HBM)


def dot(a, b):
    return jnp.dot(a, b, preferred_element_type=F32)


def dot_nt(a, b):
    return lax.dot_general(a, b, (((1,), (1,)), ((), ())), preferred_element_type=F32)


def iota(shape, axis):
    return lax.broadcasted_iota(jnp.int32, shape, axis)


def split(x):
    high = x.astype(BF16)
    return high, (x - high.astype(F32)).astype(BF16)


def twice(block):
    zero = jnp.zeros_like(block)
    return jnp.concatenate(
        [jnp.concatenate([block, zero], 1), jnp.concatenate([zero, block], 1)], 0
    )


def fetch(sources, targets, sems):
    copies = [pltpu.make_async_copy(a, b, sems.at[n]) for n, (a, b) in enumerate(zip(sources, targets))]
    for copy in copies:
        copy.start()
    return copies


def pack_kernel(rows_hbm, mask_hbm, gain_hbm, real_hbm, out_ref, rows_ref, mask_ref, gain_ref, real_ref, sems):
    copies = fetch(
        (rows_hbm, mask_hbm, gain_hbm, real_hbm), (rows_ref, mask_ref, gain_ref, real_ref), sems
    )
    for copy in copies:
        copy.wait()
    seqs, toks, width = rows_ref.shape
    outer = seqs // 8
    x = rows_ref[...].reshape(outer, 2, 4, toks, width)
    x = jnp.concatenate([x[:, 0], x[:, 1]], axis=-1).reshape(seqs // 2 * toks, 2 * width)
    lanes = 2 * width
    same = (iota((lanes, lanes), 0) // width) == (iota((lanes, lanes), 1) // width)
    mean_of = jnp.where(same, 1.0 / width, 0.0).astype(BF16)
    centered = x.astype(F32) - dot(x, mean_of)
    high, low = split(centered * centered)
    spread = dot(high, mean_of) + dot(low, mean_of)
    gain = jnp.concatenate([gain_ref[...], gain_ref[...]], axis=-1)
    normed = centered * lax.rsqrt(spread + 1e-05) * gain
    out_ref[: seqs // 2] = normed.astype(BF16).reshape(seqs // 2, toks, lanes)
    real = real_ref[...].astype(F32)
    tokens = real.shape[1]
    here = iota((toks, tokens), 1) == lax.axis_index("row") * toks + iota((toks, tokens), 0)
    mine = jnp.sum(jnp.where(here, real, 0.0), axis=1, keepdims=True)
    mask = mask_ref[...].astype(F32)
    mask = jnp.concatenate([mask, jnp.zeros((toks, lanes - seqs), F32)], axis=-1)
    mask = jnp.where(iota(mask.shape, 1) == seqs, mine, mask)
    out_ref[seqs // 2] = mask.astype(BF16)


def fold_kernel(
    seqs,
    heads,
    pack_ref,
    former_hbm,
    latter_hbm,
    outer_hbm,
    content_hbm,
    switch_hbm,
    final_hbm,
    folded_ref,
    gate_ref,
    right_ref,
    value_ref,
    result_ref,
    former_ref,
    latter_ref,
    outer_ref,
    content_ref,
    switch_ref,
    final_ref,
    weight_scr,
    left_scr,
    lhs_scr,
    sems,
):
    copies = fetch(
        (former_hbm, outer_hbm, latter_hbm, content_hbm, switch_hbm, final_hbm),
        (former_ref, outer_ref, latter_ref, content_ref, switch_ref, final_ref),
        sems,
    )
    half, toks, lanes = seqs // 2, pack_ref.shape[1], pack_ref.shape[2]
    factor, width = former_ref.shape
    outer = seqs // 8
    rows = pack_ref[:half].reshape(half * toks, lanes)
    copies[0].wait()
    left = dot_nt(rows, twice(former_ref[...]))
    for so in range(outer):
        for s2 in range(2):
            left_scr[pl.ds((so * 8 + s2 * 4) * toks, 4 * toks), :factor] = left[
                so * 4 * toks : (so + 1) * 4 * toks, s2 * factor : (s2 + 1) * factor
            ]
    eye = iota((seqs, seqs), 0) == iota((seqs, seqs), 1)
    mask = pack_ref[half].astype(F32)[:, :seqs]
    for i in range(toks):
        picked = jnp.where(eye, jnp.broadcast_to(mask[i : i + 1], (seqs, seqs)), 0.0)
        rows_i = left_scr[pl.ds(i, seqs, stride=toks), :][:, :factor].astype(BF16)
        lhs_scr[i * seqs : (i + 1) * seqs, :] = dot(picked.astype(BF16), rows_i).astype(BF16)
    copies[1].wait()
    weight_scr[...] = outer_ref[...].astype(F32)
    channels = outer_ref.shape[1]

    def step(m, carry):
        even = weight_scr[pl.ds(2 * m, factor, stride=factor), :]
        odd = weight_scr[pl.ds(2 * m + 1, factor, stride=factor), :]
        pair = jnp.concatenate([even, odd], axis=1).astype(BF16)
        for i in range(toks):
            block = dot(lhs_scr[i * seqs : (i + 1) * seqs, :], pair)
            block = block.reshape(outer, 8, 2 * channels)
            block = jnp.concatenate([block[:, :, :channels], block[:, :, channels:]], axis=1)
            first = i % 2 * channels
            folded_ref[
                i // 2, :, pl.ds(pl.multiple_of(16 * m, 16), 16), first : first + channels
            ] = block.astype(BF16)
        return carry

    lax.fori_loop(0, factor // 2, step, 0)
    for copy in copies[2:]:
        copy.wait()
    spread = jnp.where(
        iota((factor, 8 * factor), 0) == iota((factor, 8 * factor), 1) // 8, 1.0, 0.0
    ).astype(BF16)
    wide = dot(latter_ref[...].astype(F32).T.astype(BF16), spread)
    lane = iota(wide.shape, 1) % 8
    for rest in range(4):
        for s2 in range(2):
            base = (rest * 2 + s2) * width
            right_ref[base : base + width, :] = jnp.where(lane == s2 * 4 + rest, wide, 0.0).astype(
                BF16
            )
    column = content_ref.shape[1] // heads
    for hp in range(heads // 2):
        cols = slice(2 * column * hp, 2 * column * (hp + 1))
        gate_ref[hp] = jax.nn.sigmoid(dot(rows, twice(switch_ref[:, cols])))
        piece = content_ref[:, cols].astype(F32)
        which = iota(piece.shape, 1) // column
        zero = jnp.zeros_like(piece)
        for h2 in range(2):
            mine = jnp.where(which == h2, piece, 0.0)
            for s2 in range(2):
                base = (h2 * 2 + s2) * width
                row = [mine, zero] if s2 == 0 else [zero, mine]
                value_ref[hp, base : base + width, :] = jnp.concatenate(row, 1).astype(BF16)
        result_ref[hp] = twice(final_ref[:, cols])


def main_kernel(seqs, heads, shifts, *refs):
    blocks = refs[: len(shifts)]
    (
        rows_hbm,
        state_hbm,
        weight_hbm,
        gain_hbm,
        folded_ref,
        gate_ref,
        right_ref,
        value_ref,
        result_ref,
        out_ref,
        pair_hbm,
        rows_ref,
        state_ref,
        weight_ref,
        gain_ref,
        pair_ref,
        wide_scr,
        rhs_scr,
        logits_scr,
        mixed_scr,
        sems,
        pair_sem,
    ) = refs[len(shifts) :]
    copies = fetch(
        (weight_hbm, gain_hbm, state_hbm, rows_hbm),
        (weight_ref, gain_ref, state_ref, rows_ref),
        sems,
    )
    half = seqs // 2
    outer = seqs // 8
    devs = len(shifts)
    _, toks, lanes = blocks[0].shape
    tokens = devs * toks
    me = lax.axis_index("row")

    def place(shift):
        where = 0
        bit = 1
        while bit < devs:
            mine = (me // bit) % 2
            where = where + bit * ((1 - mine) if shift & bit else mine)
            bit *= 2
        return pl.multiple_of(where * toks, toks)

    spots = [place(k) for k in shifts]

    def gathered(n):
        return jnp.concatenate([block[n] for block in blocks], axis=0)

    mask = gathered(half)
    inverse = 1.0 / (1.0 + dot_nt(mask, jnp.where(iota((toks, lanes), 1) < seqs, blocks[0][half], 0)))
    real = dot_nt(jnp.where(iota((8, lanes), 1) == seqs, 1.0, 0.0).astype(BF16), mask)
    wide = right_ref.shape[1]
    which = iota((lanes, wide), 0) - iota((lanes, wide), 1) % 8
    for so in range(outer):
        pick = jnp.where(which == 8 * so, 1.0, 0.0).astype(BF16)
        wide_scr[:, so * wide : (so + 1) * wide] = dot(mask, pick).astype(BF16)
    for so in range(outer):
        rows = jnp.concatenate([gathered(so * 4 + r) for r in range(4)], axis=1)
        cols = slice(so * wide, (so + 1) * wide)
        rhs_scr[:, cols] = (dot(rows, right_ref[...]) * wide_scr[:, cols].astype(F32)).astype(BF16)
    for copy in copies:
        copy.wait()
    w_high, w_low = split(weight_ref[...] * gain_ref[...])
    lhs = jnp.concatenate(
        [
            jnp.concatenate([w_high, w_high], axis=1),
            jnp.concatenate([w_low, jnp.zeros_like(w_low)], axis=1),
        ],
        axis=0,
    )
    channels = state_ref.shape[-1]

    def product(ip):
        return dot(rhs_scr[...], folded_ref[ip].reshape(outer * wide, 2 * channels))

    acc = product(0)
    for ip in range(toks // 2):
        later = product(ip + 1) if ip + 1 < toks // 2 else None
        for i2 in range(2):
            i = 2 * ip + i2
            x = jnp.concatenate([state_ref[i, pl.ds(spot, toks), :] for spot in spots], axis=0)
            x = x.astype(F32) + acc[:, i2 * channels : (i2 + 1) * channels] * inverse[:, i : i + 1]
            x = x.astype(BF16)
            for n, spot in enumerate(spots):
                pair_ref[i, pl.ds(spot, toks), :] = x[n * toks : (n + 1) * toks]
            pltpu.make_async_copy(pair_ref.at[i], pair_hbm.at[i], pair_sem.at[i]).start()
            x = x.astype(F32)
            x = x - jnp.mean(x, axis=-1, keepdims=True)
            spread = jnp.mean(x * x, axis=-1, keepdims=True)
            high, low = split(x * lax.rsqrt(spread + 1e-05))
            logits = dot_nt(lhs, jnp.concatenate([high, low], axis=1))
            logits = logits[:heads] + logits[heads:]
            for jb in range(tokens // 128):
                logits_scr[jb, pl.ds(i, heads, stride=toks), :] = logits[
                    :, jb * 128 : jb * 128 + 128
                ]
        acc = later
    logits = jnp.concatenate([logits_scr[jb] for jb in range(tokens // 128)], axis=1)
    logits = jnp.where(real[:1] > 0.5, logits, -1000000000.0)
    top = jnp.max(logits, axis=-1, keepdims=True)
    power = jnp.exp(logits - top)
    probs = (power / jnp.sum(power, axis=-1, keepdims=True)).astype(BF16)
    for b in range(0, half, 2):
        mixed = dot(probs, jnp.concatenate([gathered(b), gathered(b + 1)], axis=1)).astype(BF16)
        mixed_scr[b] = mixed[:, :lanes]
        mixed_scr[b + 1] = mixed[:, lanes:]
    total = None
    for hp in range(heads // 2):
        pair = jnp.concatenate(
            [
                mixed_scr[:, (2 * hp + h2) * toks : (2 * hp + h2 + 1) * toks, :].reshape(
                    half * toks, lanes
                )
                for h2 in range(2)
            ],
            axis=1,
        )
        average = dot(pair, value_ref[hp])
        gated = (gate_ref[hp] * average).astype(BF16)
        part = dot_nt(gated, result_ref[hp])
        total = part if total is None else total + part
    width = rows_ref.shape[2]
    total = total.reshape(outer, 4, toks, lanes)
    base = rows_ref[...].astype(F32).reshape(outer, 2, 4, toks, width)
    for s2 in range(2):
        piece = base[:, s2] + total[..., s2 * width : (s2 + 1) * width]
        for so in range(outer):
            out_ref[so * 8 + s2 * 4 : so * 8 + s2 * 4 + 4] = piece[so].astype(BF16)
    for i in range(toks):
        pltpu.make_async_copy(pair_ref.at[i], pair_hbm.at[i], pair_sem.at[i]).wait()


def shards(
    homolog_embedding,
    pair_state_tiles,
    alignment_mask,
    token_real_mask,
    lineup_standardize_scaling,
    former_factor_proj,
    latter_factor_proj,
    outer_output_weight,
    pair_norm_gain,
    pair_logit_weight,
    content_vector_proj,
    sigmoid_switch_proj,
    final_result_proj,
    *,
    devs,
):
    seqs, toks, width = homolog_embedding.shape
    tokens = devs * toks
    heads = pair_logit_weight.shape[1]
    factor = former_factor_proj.shape[1]
    channels = outer_output_weight.shape[1]
    lanes = 2 * width
    half, outer = seqs // 2, seqs // 8
    params = pltpu.CompilerParams(vmem_limit_bytes=28 << 20)

    def keep(*arrays):
        return [pltpu.with_memory_space_constraint(a, pltpu.HBM) for a in arrays]

    def room(*arrays):
        return [pltpu.VMEM(a.shape, a.dtype) for a in arrays]

    arrays = (
        homolog_embedding,
        alignment_mask.T,
        lineup_standardize_scaling[None],
        token_real_mask[None],
    )
    packed = pl.pallas_call(
        pack_kernel,
        out_shape=jax.ShapeDtypeStruct((half + 1, toks, lanes), BF16),
        in_specs=[HB] * 4,
        out_specs=VM,
        scratch_shapes=room(*arrays) + [pltpu.SemaphoreType.DMA((4,))],
        compiler_params=params,
        name="pack",
    )(*keep(*arrays))

    def swap(block, shift):
        return lax.ppermute(block, "row", [(n, n ^ shift) for n in range(devs)])

    held = {0: packed}
    for shift in sorted(range(4, devs, 4), reverse=True):
        held[shift] = swap(packed, shift)
    for bit in (2, 1):
        for shift in sorted(held):
            held[shift ^ bit] = swap(held[shift], bit)
    shifts = tuple(sorted(held))

    arrays = (
        former_factor_proj.T,
        latter_factor_proj.T,
        outer_output_weight,
        content_vector_proj,
        sigmoid_switch_proj,
        final_result_proj.T,
    )
    folded, gate, right, value, result = pl.pallas_call(
        functools.partial(fold_kernel, seqs, heads),
        out_shape=(
            jax.ShapeDtypeStruct((toks // 2, outer, 8 * factor, 2 * channels), BF16),
            jax.ShapeDtypeStruct((heads // 2, half * toks, lanes), F32),
            jax.ShapeDtypeStruct((8 * width, 8 * factor), BF16),
            jax.ShapeDtypeStruct((heads // 2, 4 * width, lanes), BF16),
            jax.ShapeDtypeStruct((heads // 2, lanes, lanes), BF16),
        ),
        in_specs=[VM] + [HB] * 6,
        out_specs=(VM,) * 5,
        scratch_shapes=room(*arrays)
        + [
            pltpu.VMEM(outer_output_weight.shape, F32),
            pltpu.VMEM((seqs * toks, 128), F32),
            pltpu.VMEM((seqs * toks, factor), BF16),
            pltpu.SemaphoreType.DMA((6,)),
        ],
        compiler_params=params,
        cost_estimate=pl.CostEstimate(
            flops=10**9, bytes_accessed=10**7, transcendentals=10**6
        ),
        name="fold",
    )(packed, *keep(*arrays))
    arrays = (homolog_embedding, pair_state_tiles, pair_logit_weight.T, pair_norm_gain[None])
    out, pair = pl.pallas_call(
        functools.partial(main_kernel, seqs, heads, shifts),
        out_shape=(
            jax.ShapeDtypeStruct(homolog_embedding.shape, BF16),
            jax.ShapeDtypeStruct(pair_state_tiles.shape, BF16),
        ),
        in_specs=[VM] * devs + [HB] * 4 + [VM] * 5,
        out_specs=(VM, HB),
        scratch_shapes=room(*arrays)
        + [
            pltpu.VMEM(pair_state_tiles.shape, BF16),
            pltpu.VMEM((tokens, outer * 8 * factor), BF16),
            pltpu.VMEM((tokens, outer * 8 * factor), BF16),
            pltpu.VMEM((tokens // 128, heads * toks, 128), F32),
            pltpu.VMEM((half, heads * toks, lanes), BF16),
            pltpu.SemaphoreType.DMA((4,)),
            pltpu.SemaphoreType.DMA((toks,)),
        ],
        compiler_params=params,
        cost_estimate=pl.CostEstimate(flops=4 * 10**9, bytes_accessed=10**7, transcendentals=10**6),
        name="main",
    )(*[held[shift] for shift in shifts], *keep(*arrays), folded, gate, right, value, result)
    return out, pair


def solution(mesh):
    placed = (
        P("groups", "row", None),
        P(("groups", "row"), None, None),
        P("groups", "row"),
        P("groups"),
        P(),
        P(),
        P(),
        P(),
        P(),
        P(),
        P(),
        P(),
        P(),
    )
    devs = mesh.shape["row"]

    def body(*arrays):
        return shards(*arrays, devs=devs)

    return jax.shard_map(
        body,
        mesh=mesh,
        in_specs=placed,
        out_specs=(P("groups", "row", None), P(("groups", "row"), None, None)),
        check_vma=False,
    )
```

profile of v0, /device:TPU:0, one launch (start us, length us, event | category | flops | bytes accessed | tf_op | source)
XLA Modules:
  0.0 43.6 jit_solution(13230870172539380056)
XLA Ops:
  0.6 1.4 %pack.1.pack_ref.refs_0_ = bf16[33,16,128]{2,1,0:T(8,128)(2,1)S(1)} custom-call(bf16[64,16,64]{2,1,0:T(8,128)(2,1)} %refs_16_.1, s32[16,64]{1,0:T(8,128)} %bitcast.8, f32[1,64]{1,0:T(1,128)} %bitcast.10, s32[1,256]{1,0:T(1,128)} %bitcast.9), custom_call_target="tpu_custom_call" | custom-call | tf_op jit(solution)/shard_map/pack/pallas_call | solution.py:347
  2.1 5.1 %collective-permute-start.11 = (bf16[33,16,128]{2,1,0:T(8,128)(2,1)S(1)}, bf16[33,16,128]{2,1,0:T(8,128)(2,1)S(1)}, u32[]{:S(2)}, u32[]{:S(2)}) collective-permute-start(bf16[33,16,128]{2,1,0:T(8,128)(2,1)S(1)} %pack.1.pack_ref.refs_0_), channel_id=1, source_target_pairs={{0,12},{1,13},{2,14},{3,15},{4,8},{5,9},{6,10},{7,11},{8,4},{9,5},... | collective-permute-start | bytes 405512 | tf_op jit(solution)/shard_map/ppermute | solution.py:358
  7.2 0.0 collective-permute-start.7
  7.2 0.6 %collective-permute-start.3 = (bf16[33,16,128]{2,1,0:T(8,128)(2,1)S(1)}, bf16[33,16,128]{2,1,0:T(8,128)(2,1)S(1)}, u32[]{:S(2)}, u32[]{:S(2)}) collective-permute-start(bf16[33,16,128]{2,1,0:T(8,128)(2,1)S(1)} %pack.1.pack_ref.refs_0_), channel_id=1, source_target_pairs={{0,4},{1,5},{2,6},{3,7},{4,0},{5,1},{6,2},{7,3},{8,12},{9,13},{10,... | collective-permute-start | bytes 405512 | tf_op jit(solution)/shard_map/ppermute | solution.py:358
  7.9 1.7 %collective-permute-start.1 = (bf16[33,16,128]{2,1,0:T(8,128)(2,1)S(1)}, bf16[33,16,128]{2,1,0:T(8,128)(2,1)S(1)}, u32[]{:S(2)}, u32[]{:S(2)}) collective-permute-start(bf16[33,16,128]{2,1,0:T(8,128)(2,1)S(1)} %pack.1.pack_ref.refs_0_), channel_id=1, source_target_pairs={{0,2},{1,3},{2,0},{3,1},{4,6},{5,7},{6,4},{7,5},{8,10},{9,11},{10,... | collective-permute-start | bytes 405512 | tf_op jit(solution)/shard_map/ppermute | solution.py:358
  9.5 0.0 collective-permute-start
  9.5 2.2 %collective-permute-done.11.refs_12_ = bf16[33,16,128]{2,1,0:T(8,128)(2,1)S(1)} collective-permute-done((bf16[33,16,128]{2,1,0:T(8,128)(2,1)S(1)}, bf16[33,16,128]{2,1,0:T(8,128)(2,1)S(1)}, u32[]{:S(2)}, u32[]{:S(2)}) %collective-permute-start.11) | collective-permute-done | bytes 135200 | tf_op jit(solution)/shard_map/ppermute | solution.py:358
  11.8 1.7 %collective-permute-start.13 = (bf16[33,16,128]{2,1,0:T(8,128)(2,1)S(1)}, bf16[33,16,128]{2,1,0:T(8,128)(2,1)S(1)}, u32[]{:S(2)}, u32[]{:S(2)}) collective-permute-start(bf16[33,16,128]{2,1,0:T(8,128)(2,1)S(1)} %collective-permute-done.11.refs_12_), channel_id=1, source_target_pairs={{0,2},{1,3},{2,0},{3,1},{4,6},{5,7},{6,4},{7,5},{8,10},{9,11},{10,... | collective-permute-start | bytes 405512 | tf_op jit(solution)/shard_map/ppermute | solution.py:358
  13.5 5.2 %collective-permute-done.7.refs_8_ = bf16[33,16,128]{2,1,0:T(8,128)(2,1)S(1)} collective-permute-done((bf16[33,16,128]{2,1,0:T(8,128)(2,1)S(1)}, bf16[33,16,128]{2,1,0:T(8,128)(2,1)S(1)}, u32[]{:S(2)}, u32[]{:S(2)}) %collective-permute-start.7) | collective-permute-done | bytes 135200 | tf_op jit(solution)/shard_map/ppermute | solution.py:358
  18.7 0.0 collective-permute-start.12
  18.7 0.0 collective-permute-done.3.refs_4_
  18.7 1.5 %collective-permute-start.9 = (bf16[33,16,128]{2,1,0:T(8,128)(2,1)S(1)}, bf16[33,16,128]{2,1,0:T(8,128)(2,1)S(1)}, u32[]{:S(2)}, u32[]{:S(2)}) collective-permute-start(bf16[33,16,128]{2,1,0:T(8,128)(2,1)S(1)} %collective-permute-done.7.refs_8_), channel_id=1, source_target_pairs={{0,2},{1,3},{2,0},{3,1},{4,6},{5,7},{6,4},{7,5},{8,10},{9,11},{10,... | collective-permute-start | bytes 405512 | tf_op jit(solution)/shard_map/ppermute | solution.py:358
  20.2 0.0 collective-permute-done.1.refs_2_
  20.2 0.2 collective-permute-start.8
  20.4 0.0 collective-permute-done.refs_1_
  20.4 0.5 %collective-permute-start.5 = (bf16[33,16,128]{2,1,0:T(8,128)(2,1)S(1)}, bf16[33,16,128]{2,1,0:T(8,128)(2,1)S(1)}, u32[]{:S(2)}, u32[]{:S(2)}) collective-permute-start(bf16[33,16,128]{2,1,0:T(8,128)(2,1)S(1)} %collective-permute-done.3.refs_4_), channel_id=1, source_target_pairs={{0,2},{1,3},{2,0},{3,1},{4,6},{5,7},{6,4},{7,5},{8,10},{9,11},{10,... | collective-permute-start | bytes 405512 | tf_op jit(solution)/shard_map/ppermute | solution.py:358
  20.9 0.0 collective-permute-done.13.refs_14_
  20.9 0.0 collective-permute-start.4
  20.9 0.0 collective-permute-done.12.refs_13_
  20.9 0.5 %collective-permute-start.2 = (bf16[33,16,128]{2,1,0:T(8,128)(2,1)S(1)}, bf16[33,16,128]{2,1,0:T(8,128)(2,1)S(1)}, u32[]{:S(2)}, u32[]{:S(2)}) collective-permute-start(bf16[33,16,128]{2,1,0:T(8,128)(2,1)S(1)} %collective-permute-done.1.refs_2_), channel_id=1, source_target_pairs={{0,1},{1,0},{2,3},{3,2},{4,5},{5,4},{6,7},{7,6},{8,9},{9,8},{10,11... | collective-permute-start | bytes 405512 | tf_op jit(solution)/shard_map/ppermute | solution.py:358
  21.4 3.7 %collective-permute-done.9.refs_10_ = bf16[33,16,128]{2,1,0:T(8,128)(2,1)S(1)} collective-permute-done((bf16[33,16,128]{2,1,0:T(8,128)(2,1)S(1)}, bf16[33,16,128]{2,1,0:T(8,128)(2,1)S(1)}, u32[]{:S(2)}, u32[]{:S(2)}) %collective-permute-start.9) | collective-permute-done | bytes 135200 | tf_op jit(solution)/shard_map/ppermute | solution.py:358
  25.1 0.0 collective-permute-start.14
  25.1 0.0 collective-permute-done.8.refs_9_
  25.1 0.5 %collective-permute-start.10 = (bf16[33,16,128]{2,1,0:T(8,128)(2,1)S(1)}, bf16[33,16,128]{2,1,0:T(8,128)(2,1)S(1)}, u32[]{:S(2)}, u32[]{:S(2)}) collective-permute-start(bf16[33,16,128]{2,1,0:T(8,128)(2,1)S(1)} %collective-permute-done.9.refs_10_), channel_id=1, source_target_pairs={{0,1},{1,0},{2,3},{3,2},{4,5},{5,4},{6,7},{7,6},{8,9},{9,8},{10,11... | collective-permute-start | bytes 405512 | tf_op jit(solution)/shard_map/ppermute | solution.py:358
  25.6 1.9 %collective-permute-done.5.refs_6_ = bf16[33,16,128]{2,1,0:T(8,128)(2,1)S(1)} collective-permute-done((bf16[33,16,128]{2,1,0:T(8,128)(2,1)S(1)}, bf16[33,16,128]{2,1,0:T(8,128)(2,1)S(1)}, u32[]{:S(2)}, u32[]{:S(2)}) %collective-permute-start.5) | collective-permute-done | bytes 135200 | tf_op jit(solution)/shard_map/ppermute | solution.py:358
  27.6 0.0 collective-permute-start.6
  27.6 6.4 %fold.1 = (bf16[8,8,256,256]{3,2,1,0:T(8,128)(2,1)S(1)}, f32[4,512,128]{2,1,0:T(8,128)S(1)}, bf16[512,256]{1,0:T(8,128)(2,1)S(1)}, bf16[4,256,128]{2,1,0:T(8,128)(2,1)S(1)}, bf16[4,128,128]{2,1,0:T(8,128)(2,1)S(1)}) custom-call(bf16[33,16,128]{2,1,0:T(8,128)(2,1)S(1)} %pack.1.pack_ref.refs_0_, bf16[32,64]{1,0:T(8,128)(2,1)} %bitcast.12, ...), custom_call_target="tpu_custom_call" | custom-call | flops 1000000000 | bytes 10000000 | tf_op jit(solution)/shard_map/fold/pallas_call | solution.py:376
  34.0 0.0 collective-permute-done.4.refs_5_
  34.0 0.0 collective-permute-done.2.refs_3_
  34.0 0.0 collective-permute-done.14.refs_15_
  34.0 0.0 collective-permute-done.10.refs_11_
  34.0 0.0 collective-permute-done.6.refs_7_
  34.0 9.5 %main.1 = (bf16[64,16,64]{2,1,0:T(8,128)(2,1)}, bf16[16,256,128]{2,1,0:T(8,128)(2,1)}) custom-call(bf16[33,16,128]{2,1,0:T(8,128)(2,1)S(1)} %pack.1.pack_ref.refs_0_, bf16[33,16,128]{2,1,0:T(8,128)(2,1)S(1)} %collective-permute-done.refs_1_, bf16[33,16,128]{2,1,0:T(8,128)(2,1)S(1)} %collective-permute-done.1.refs_2_, ...), custom_call_target="tpu_custom_call" | custom-call | flops 4000000000 | bytes 10000000 | tf_op jit(solution)/shard_map/main/pallas_call | solution.py:401
Async XLA Ops:
  2.1 9.7 %collective-permute-start.11 = (bf16[33,16,128]{2,1,0:T(8,128)(2,1)S(1)}, bf16[33,16,128]{2,1,0:T(8,128)(2,1)S(1)}, u32[]{:S(2)}, u32[]{:S(2)}) collective-permute-start(bf16[33,16,128]{2,1,0:T(8,128)(2,1)S(1)} %pack.1.pack_ref.refs_0_), channel_id=1, source_target_pairs={{0,12},{1,13},{2,14},{3,15},{4,8},{5,9},{6,10},{7,11},{8,4},{9,5},... | collective-permute-start | bytes 405512 | tf_op jit(solution)/shard_map/ppermute | solution.py:358
  7.2 11.4 %collective-permute-start.7 = (bf16[33,16,128]{2,1,0:T(8,128)(2,1)S(1)}, bf16[33,16,128]{2,1,0:T(8,128)(2,1)S(1)}, u32[]{:S(2)}, u32[]{:S(2)}) collective-permute-start(bf16[33,16,128]{2,1,0:T(8,128)(2,1)S(1)} %pack.1.pack_ref.refs_0_), channel_id=1, source_target_pairs={{0,8},{1,9},{2,10},{3,11},{4,12},{5,13},{6,14},{7,15},{8,0},{9,1},... | collective-permute-start | bytes 405512 | tf_op jit(solution)/shard_map/ppermute | solution.py:358
  7.2 11.4 %collective-permute-start.3 = (bf16[33,16,128]{2,1,0:T(8,128)(2,1)S(1)}, bf16[33,16,128]{2,1,0:T(8,128)(2,1)S(1)}, u32[]{:S(2)}, u32[]{:S(2)}) collective-permute-start(bf16[33,16,128]{2,1,0:T(8,128)(2,1)S(1)} %pack.1.pack_ref.refs_0_), channel_id=1, source_target_pairs={{0,4},{1,5},{2,6},{3,7},{4,0},{5,1},{6,2},{7,3},{8,12},{9,13},{10,... | collective-permute-start | bytes 405512 | tf_op jit(solution)/shard_map/ppermute | solution.py:358
  7.9 12.3 %collective-permute-start.1 = (bf16[33,16,128]{2,1,0:T(8,128)(2,1)S(1)}, bf16[33,16,128]{2,1,0:T(8,128)(2,1)S(1)}, u32[]{:S(2)}, u32[]{:S(2)}) collective-permute-start(bf16[33,16,128]{2,1,0:T(8,128)(2,1)S(1)} %pack.1.pack_ref.refs_0_), channel_id=1, source_target_pairs={{0,2},{1,3},{2,0},{3,1},{4,6},{5,7},{6,4},{7,5},{8,10},{9,11},{10,... | collective-permute-start | bytes 405512 | tf_op jit(solution)/shard_map/ppermute | solution.py:358
  9.5 10.9 %collective-permute-start = (bf16[33,16,128]{2,1,0:T(8,128)(2,1)S(1)}, bf16[33,16,128]{2,1,0:T(8,128)(2,1)S(1)}, u32[]{:S(2)}, u32[]{:S(2)}) collective-permute-start(bf16[33,16,128]{2,1,0:T(8,128)(2,1)S(1)} %pack.1.pack_ref.refs_0_), channel_id=1, source_target_pairs={{0,1},{1,0},{2,3},{3,2},{4,5},{5,4},{6,7},{7,6},{8,9},{9,8},{10,11... | collective-permute-start | bytes 405512 | tf_op jit(solution)/shard_map/ppermute | solution.py:358
  11.8 9.2 %collective-permute-start.13 = (bf16[33,16,128]{2,1,0:T(8,128)(2,1)S(1)}, bf16[33,16,128]{2,1,0:T(8,128)(2,1)S(1)}, u32[]{:S(2)}, u32[]{:S(2)}) collective-permute-start(bf16[33,16,128]{2,1,0:T(8,128)(2,1)S(1)} %collective-permute-done.11.refs_12_), channel_id=1, source_target_pairs={{0,2},{1,3},{2,0},{3,1},{4,6},{5,7},{6,4},{7,5},{8,10},{9,11},{10,... | collective-permute-start | bytes 405512 | tf_op jit(solution)/shard_map/ppermute | solution.py:358
  18.7 2.3 %collective-permute-start.12 = (bf16[33,16,128]{2,1,0:T(8,128)(2,1)S(1)}, bf16[33,16,128]{2,1,0:T(8,128)(2,1)S(1)}, u32[]{:S(2)}, u32[]{:S(2)}) collective-permute-start(bf16[33,16,128]{2,1,0:T(8,128)(2,1)S(1)} %collective-permute-done.11.refs_12_), channel_id=1, source_target_pairs={{0,1},{1,0},{2,3},{3,2},{4,5},{5,4},{6,7},{7,6},{8,9},{9,8},{10,11... | collective-permute-start | bytes 405512 | tf_op jit(solution)/shard_map/ppermute | solution.py:358
  18.7 6.5 %collective-permute-start.9 = (bf16[33,16,128]{2,1,0:T(8,128)(2,1)S(1)}, bf16[33,16,128]{2,1,0:T(8,128)(2,1)S(1)}, u32[]{:S(2)}, u32[]{:S(2)}) collective-permute-start(bf16[33,16,128]{2,1,0:T(8,128)(2,1)S(1)} %collective-permute-done.7.refs_8_), channel_id=1, source_target_pairs={{0,2},{1,3},{2,0},{3,1},{4,6},{5,7},{6,4},{7,5},{8,10},{9,11},{10,... | collective-permute-start | bytes 405512 | tf_op jit(solution)/shard_map/ppermute | solution.py:358
  20.2 4.9 %collective-permute-start.8 = (bf16[33,16,128]{2,1,0:T(8,128)(2,1)S(1)}, bf16[33,16,128]{2,1,0:T(8,128)(2,1)S(1)}, u32[]{:S(2)}, u32[]{:S(2)}) collective-permute-start(bf16[33,16,128]{2,1,0:T(8,128)(2,1)S(1)} %collective-permute-done.7.refs_8_), channel_id=1, source_target_pairs={{0,1},{1,0},{2,3},{3,2},{4,5},{5,4},{6,7},{7,6},{8,9},{9,8},{10,11... | collective-permute-start | bytes 405512 | tf_op jit(solution)/shard_map/ppermute | solution.py:358
  20.4 7.1 %collective-permute-start.5 = (bf16[33,16,128]{2,1,0:T(8,128)(2,1)S(1)}, bf16[33,16,128]{2,1,0:T(8,128)(2,1)S(1)}, u32[]{:S(2)}, u32[]{:S(2)}) collective-permute-start(bf16[33,16,128]{2,1,0:T(8,128)(2,1)S(1)} %collective-permute-done.3.refs_4_), channel_id=1, source_target_pairs={{0,2},{1,3},{2,0},{3,1},{4,6},{5,7},{6,4},{7,5},{8,10},{9,11},{10,... | collective-permute-start | bytes 405512 | tf_op jit(solution)/shard_map/ppermute | solution.py:358
  20.9 13.0 %collective-permute-start.4 = (bf16[33,16,128]{2,1,0:T(8,128)(2,1)S(1)}, bf16[33,16,128]{2,1,0:T(8,128)(2,1)S(1)}, u32[]{:S(2)}, u32[]{:S(2)}) collective-permute-start(bf16[33,16,128]{2,1,0:T(8,128)(2,1)S(1)} %collective-permute-done.3.refs_4_), channel_id=1, source_target_pairs={{0,1},{1,0},{2,3},{3,2},{4,5},{5,4},{6,7},{7,6},{8,9},{9,8},{10,11... | collective-permute-start | bytes 405512 | tf_op jit(solution)/shard_map/ppermute | solution.py:358
  20.9 13.1 %collective-permute-start.2 = (bf16[33,16,128]{2,1,0:T(8,128)(2,1)S(1)}, bf16[33,16,128]{2,1,0:T(8,128)(2,1)S(1)}, u32[]{:S(2)}, u32[]{:S(2)}) collective-permute-start(bf16[33,16,128]{2,1,0:T(8,128)(2,1)S(1)} %collective-permute-done.1.refs_2_), channel_id=1, source_target_pairs={{0,1},{1,0},{2,3},{3,2},{4,5},{5,4},{6,7},{7,6},{8,9},{9,8},{10,11... | collective-permute-start | bytes 405512 | tf_op jit(solution)/shard_map/ppermute | solution.py:358
  25.1 8.9 %collective-permute-start.14 = (bf16[33,16,128]{2,1,0:T(8,128)(2,1)S(1)}, bf16[33,16,128]{2,1,0:T(8,128)(2,1)S(1)}, u32[]{:S(2)}, u32[]{:S(2)}) collective-permute-start(bf16[33,16,128]{2,1,0:T(8,128)(2,1)S(1)} %collective-permute-done.13.refs_14_), channel_id=1, source_target_pairs={{0,1},{1,0},{2,3},{3,2},{4,5},{5,4},{6,7},{7,6},{8,9},{9,8},{10,11... | collective-permute-start | bytes 405512 | tf_op jit(solution)/shard_map/ppermute | solution.py:358
  25.1 8.9 %collective-permute-start.10 = (bf16[33,16,128]{2,1,0:T(8,128)(2,1)S(1)}, bf16[33,16,128]{2,1,0:T(8,128)(2,1)S(1)}, u32[]{:S(2)}, u32[]{:S(2)}) collective-permute-start(bf16[33,16,128]{2,1,0:T(8,128)(2,1)S(1)} %collective-permute-done.9.refs_10_), channel_id=1, source_target_pairs={{0,1},{1,0},{2,3},{3,2},{4,5},{5,4},{6,7},{7,6},{8,9},{9,8},{10,11... | collective-permute-start | bytes 405512 | tf_op jit(solution)/shard_map/ppermute | solution.py:358
  27.6 6.5 %collective-permute-start.6 = (bf16[33,16,128]{2,1,0:T(8,128)(2,1)S(1)}, bf16[33,16,128]{2,1,0:T(8,128)(2,1)S(1)}, u32[]{:S(2)}, u32[]{:S(2)}) collective-permute-start(bf16[33,16,128]{2,1,0:T(8,128)(2,1)S(1)} %collective-permute-done.5.refs_6_), channel_id=1, source_target_pairs={{0,1},{1,0},{2,3},{3,2},{4,5},{5,4},{6,7},{7,6},{8,9},{9,8},{10,11... | collective-permute-start | bytes 405512 | tf_op jit(solution)/shard_map/ppermute | solution.py:358
where the time goes:
time: 43.8 us; the launch traced here: 43.6 us
  Pallas kernels  17.4 us (40%)
  waiting for transfers between devices  13 us (30%)
  starting transfers between devices  12.4 us (28%)
  between operations  0.7 us (2%)
    ppermute x15, waiting for transfers between devices, swap(): return lax.ppermute(block, 'row', [(n, n ^ shift) for n in range(devs)])  13 us
    ppermute x15, starting transfers between devices, swap(): return lax.ppermute(block, 'row', [(n, n ^ shift) for n in range(devs)])  12.4 us
    pallas_call x1, Pallas kernels, shards(): pl.pallas_call(functools.partial(main_kernel, seqs, heads, shifts), out_s...  9.54 us
    pallas_call x1, Pallas kernels, shards(): pl.pallas_call(functools.partial(fold_kernel, seqs, heads), out_shape=(ja...  6.41 us
    pallas_call x1, Pallas kernels, shards(): pl.pallas_call(pack_kernel, out_shape=jax.ShapeDtypeStruct((half + 1, tok...  1.45 us
  transfers between devices with their start and end apart: 15, of which 4 were waited for; matrix products, arithmetic and copies ran while one was open for 0% of the time, Pallas kernels for 15%

commit v1 on v0

--- a/solution.py
+++ b/solution.py
@@ -11,6 +11,7 @@
 F32 = jnp.float32
 BF16 = jnp.bfloat16
 VM = pl.BlockSpec(memory_space=pltpu.VMEM)
+UNROLL = 4
 HB = pl.BlockSpec(memory_space=pltpu.HBM)
 
 
@@ -127,20 +128,22 @@
     channels = outer_ref.shape[1]
 
     def step(m, carry):
-        even = weight_scr[pl.ds(2 * m, factor, stride=factor), :]
-        odd = weight_scr[pl.ds(2 * m + 1, factor, stride=factor), :]
-        pair = jnp.concatenate([even, odd], axis=1).astype(BF16)
-        for i in range(toks):
-            block = dot(lhs_scr[i * seqs : (i + 1) * seqs, :], pair)
-            block = block.reshape(outer, 8, 2 * channels)
-            block = jnp.concatenate([block[:, :, :channels], block[:, :, channels:]], axis=1)
-            first = i % 2 * channels
-            folded_ref[
-                i // 2, :, pl.ds(pl.multiple_of(16 * m, 16), 16), first : first + channels
-            ] = block.astype(BF16)
+        for u in range(UNROLL):
+            e = 2 * (m * UNROLL + u)
+            even = weight_scr[pl.ds(e, factor, stride=factor), :]
+            odd = weight_scr[pl.ds(e + 1, factor, stride=factor), :]
+            pair = jnp.concatenate([even, odd], axis=1).astype(BF16)
+            product = dot(lhs_scr[...], pair)
+            for i in range(toks):
+                block = product[i * seqs : (i + 1) * seqs].reshape(outer, 8, 2 * channels)
+                block = jnp.concatenate([block[:, :, :channels], block[:, :, channels:]], axis=1)
+                first = i % 2 * channels
+                folded_ref[
+                    i // 2, :, pl.ds(pl.multiple_of(8 * e, 16), 16), first : first + channels
+                ] = block.astype(BF16)
         return carry
 
-    lax.fori_loop(0, factor // 2, step, 0)
+    lax.fori_loop(0, factor // 2 // UNROLL, step, 0)
     for copy in copies[2:]:
         copy.wait()
     spread = jnp.where(
@@ -193,6 +196,11 @@
         rhs_scr,
         logits_scr,
         mixed_scr,
+        inverse_scr,
+        lhs_scr,
+        even_scr,
+        odd_scr,
+        both_scr,
         sems,
         pair_sem,
     ) = refs[len(shifts) :]
@@ -230,6 +238,8 @@
     for so in range(outer):
         pick = jnp.where(which == 8 * so, 1.0, 0.0).astype(BF16)
         wide_scr[:, so * wide : (so + 1) * wide] = dot(mask, pick).astype(BF16)
+    for i in range(toks):
+        inverse_scr[i] = jnp.broadcast_to(inverse[:, i : i + 1], inverse_scr.shape[1:])
     for so in range(outer):
         rows = jnp.concatenate([gathered(so * 4 + r) for r in range(4)], axis=1)
         cols = slice(so * wide, (so + 1) * wide)
@@ -237,7 +247,7 @@
     for copy in copies:
         copy.wait()
     w_high, w_low = split(weight_ref[...] * gain_ref[...])
-    lhs = jnp.concatenate(
+    lhs_scr[...] = jnp.concatenate(
         [
             jnp.concatenate([w_high, w_high], axis=1),
             jnp.concatenate([w_low, jnp.zeros_like(w_low)], axis=1),
@@ -246,31 +256,38 @@
     )
     channels = state_ref.shape[-1]
 
-    def product(ip):
-        return dot(rhs_scr[...], folded_ref[ip].reshape(outer * wide, 2 * channels))
-
-    acc = product(0)
-    for ip in range(toks // 2):
-        later = product(ip + 1) if ip + 1 < toks // 2 else None
+    def product(ip, acc_scr):
+        acc_scr[...] = dot(rhs_scr[...], folded_ref[ip].reshape(outer * wide, 2 * channels))
+
+    def finish(ip, acc_scr):
         for i2 in range(2):
             i = 2 * ip + i2
-            x = jnp.concatenate([state_ref[i, pl.ds(spot, toks), :] for spot in spots], axis=0)
-            x = x.astype(F32) + acc[:, i2 * channels : (i2 + 1) * channels] * inverse[:, i : i + 1]
-            x = x.astype(BF16)
             for n, spot in enumerate(spots):
-                pair_ref[i, pl.ds(spot, toks), :] = x[n * toks : (n + 1) * toks]
+                here = slice(n * toks, (n + 1) * toks)
+                x = state_ref[i, pl.ds(spot, toks), :].astype(F32) + (
+                    acc_scr[here, i2 * channels : (i2 + 1) * channels] * inverse_scr[i, here, :]
+                )
+                x = x.astype(BF16)
+                pair_ref[i, pl.ds(spot, toks), :] = x
+                x = x.astype(F32)
+                x = x - jnp.mean(x, axis=-1, keepdims=True)
+                spread = jnp.mean(x * x, axis=-1, keepdims=True)
+                high, low = split(x * lax.rsqrt(spread + 1e-05))
+                both_scr[i2, here, :channels] = high
+                both_scr[i2, here, channels:] = low
             pltpu.make_async_copy(pair_ref.at[i], pair_hbm.at[i], pair_sem.at[i]).start()
-            x = x.astype(F32)
-            x = x - jnp.mean(x, axis=-1, keepdims=True)
-            spread = jnp.mean(x * x, axis=-1, keepdims=True)
-            high, low = split(x * lax.rsqrt(spread + 1e-05))
-            logits = dot_nt(lhs, jnp.concatenate([high, low], axis=1))
+            logits = dot_nt(lhs_scr[...], both_scr[i2])
             logits = logits[:heads] + logits[heads:]
             for jb in range(tokens // 128):
                 logits_scr[jb, pl.ds(i, heads, stride=toks), :] = logits[
                     :, jb * 128 : jb * 128 + 128
                 ]
-        acc = later
+
+    product(0, even_scr)
+    for ip in range(toks // 2):
+        if ip + 1 < toks // 2:
+            product(ip + 1, odd_scr if ip % 2 == 0 else even_scr)
+        finish(ip, even_scr if ip % 2 == 0 else odd_scr)
     logits = jnp.concatenate([logits_scr[jb] for jb in range(tokens // 128)], axis=1)
     logits = jnp.where(real[:1] > 0.5, logits, -1000000000.0)
     top = jnp.max(logits, axis=-1, keepdims=True)
@@ -306,6 +323,11 @@
         pltpu.make_async_copy(pair_ref.at[i], pair_hbm.at[i], pair_sem.at[i]).wait()
 
 
+def far_order(devs):
+    far = list(range(4, devs, 4))
+    return far[:1] + far[:0:-1]
+
+
 def shards(
     homolog_embedding,
     pair_state_tiles,
@@ -358,10 +380,11 @@
         return lax.ppermute(block, "row", [(n, n ^ shift) for n in range(devs)])
 
     held = {0: packed}
-    for shift in sorted(range(4, devs, 4), reverse=True):
+    far = far_order(devs)
+    for shift in far:
         held[shift] = swap(packed, shift)
     for bit in (2, 1):
-        for shift in sorted(held):
+        for shift in list(held):
             held[shift ^ bit] = swap(held[shift], bit)
     shifts = tuple(sorted(held))
 
@@ -413,6 +436,11 @@
             pltpu.VMEM((tokens, outer * 8 * factor), BF16),
             pltpu.VMEM((tokens // 128, heads * toks, 128), F32),
             pltpu.VMEM((half, heads * toks, lanes), BF16),
+            pltpu.VMEM((toks, tokens, channels), F32),
+            pltpu.VMEM((2 * heads, 2 * channels), BF16),
+            pltpu.VMEM((tokens, 2 * channels), F32),
+            pltpu.VMEM((tokens, 2 * channels), F32),
+            pltpu.VMEM((2, tokens, 2 * channels), BF16),
             pltpu.SemaphoreType.DMA((4,)),
             pltpu.SemaphoreType.DMA((toks,)),
         ],

time: 43.8 us -> 41.2 us (0.941)
  Pallas kernels: 17.4 us -> 14.8 us
    pallas_call x1, Pallas kernels: 9.54 us -> 8.07 us  [shards(): pl.pallas_call(functools.partial(main_kernel, seqs, heads, shifts), out_s...]
    pallas_call x1, Pallas kernels: 6.41 us -> 5.29 us  [shards(): pl.pallas_call(functools.partial(fold_kernel, seqs, heads), out_shape=(ja...]
  transfers between devices with their start and end apart: 15 -> 15, of which waited for: 4 -> 4; matrix products, arithmetic and copies ran while one was open for 0% -> 0% of each run, Pallas kernels for 15% -> 13%
where the time goes in v1:
time: 41.2 us; the launch traced here: 41 us
  Pallas kernels  14.8 us (36%)
  waiting for transfers between devices  13 us (32%)
  starting transfers between devices  12.4 us (30%)
  between operations  0.7 us (2%)
    ppermute x15, waiting for transfers between devices, swap(): return lax.ppermute(block, 'row', [(n, n ^ shift) for n in range(devs)])  13 us
    ppermute x15, starting transfers between devices, swap(): return lax.ppermute(block, 'row', [(n, n ^ shift) for n in range(devs)])  12.4 us
    pallas_call x1, Pallas kernels, shards(): pl.pallas_call(functools.partial(main_kernel, seqs, heads, shifts), out_s...  8.07 us
    pallas_call x1, Pallas kernels, shards(): pl.pallas_call(functools.partial(fold_kernel, seqs, heads), out_shape=(ja...  5.29 us
    pallas_call x1, Pallas kernels, shards(): pl.pallas_call(pack_kernel, out_shape=jax.ShapeDtypeStruct((half + 1, tok...  1.45 us
  transfers between devices with their start and end apart: 15, of which 4 were waited for; matrix products, arithmetic and copies ran while one was open for 0% of the time, Pallas kernels for 13%

profile of v1, /device:TPU:0, one launch (start us, length us, event | category | flops | bytes accessed | tf_op | source)
XLA Modules:
  0.0 41.0 jit_solution(9097531213769934663)
XLA Ops:
  0.6 1.4 %pack.1.pack_ref.refs_0_ = bf16[33,16,128]{2,1,0:T(8,128)(2,1)S(1)} custom-call(bf16[64,16,64]{2,1,0:T(8,128)(2,1)} %refs_16_.1, s32[16,64]{1,0:T(8,128)} %bitcast.8, f32[1,64]{1,0:T(1,128)} %bitcast.10, s32[1,256]{1,0:T(1,128)} %bitcast.9), custom_call_target="tpu_custom_call" | custom-call | tf_op jit(solution)/shard_map/pack/pallas_call | solution.py:369
  2.1 5.1 %collective-permute-start.11 = (bf16[33,16,128]{2,1,0:T(8,128)(2,1)S(1)}, bf16[33,16,128]{2,1,0:T(8,128)(2,1)S(1)}, u32[]{:S(2)}, u32[]{:S(2)}) collective-permute-start(bf16[33,16,128]{2,1,0:T(8,128)(2,1)S(1)} %pack.1.pack_ref.refs_0_), channel_id=1, source_target_pairs={{0,12},{1,13},{2,14},{3,15},{4,8},{5,9},{6,10},{7,11},{8,4},{9,5},... | collective-permute-start | bytes 405512 | tf_op jit(solution)/shard_map/ppermute | solution.py:380
  7.2 0.0 collective-permute-start.7
  7.2 0.6 %collective-permute-start.3 = (bf16[33,16,128]{2,1,0:T(8,128)(2,1)S(1)}, bf16[33,16,128]{2,1,0:T(8,128)(2,1)S(1)}, u32[]{:S(2)}, u32[]{:S(2)}) collective-permute-start(bf16[33,16,128]{2,1,0:T(8,128)(2,1)S(1)} %pack.1.pack_ref.refs_0_), channel_id=1, source_target_pairs={{0,4},{1,5},{2,6},{3,7},{4,0},{5,1},{6,2},{7,3},{8,12},{9,13},{10,... | collective-permute-start | bytes 405512 | tf_op jit(solution)/shard_map/ppermute | solution.py:380
  7.9 1.7 %collective-permute-start.1 = (bf16[33,16,128]{2,1,0:T(8,128)(2,1)S(1)}, bf16[33,16,128]{2,1,0:T(8,128)(2,1)S(1)}, u32[]{:S(2)}, u32[]{:S(2)}) collective-permute-start(bf16[33,16,128]{2,1,0:T(8,128)(2,1)S(1)} %pack.1.pack_ref.refs_0_), channel_id=1, source_target_pairs={{0,2},{1,3},{2,0},{3,1},{4,6},{5,7},{6,4},{7,5},{8,10},{9,11},{10,... | collective-permute-start | bytes 405512 | tf_op jit(solution)/shard_map/ppermute | solution.py:380
  9.5 0.0 collective-permute-start
  9.5 2.2 %collective-permute-done.11.refs_12_ = bf16[33,16,128]{2,1,0:T(8,128)(2,1)S(1)} collective-permute-done((bf16[33,16,128]{2,1,0:T(8,128)(2,1)S(1)}, bf16[33,16,128]{2,1,0:T(8,128)(2,1)S(1)}, u32[]{:S(2)}, u32[]{:S(2)}) %collective-permute-start.11) | collective-permute-done | bytes 135200 | tf_op jit(solution)/shard_map/ppermute | solution.py:380
  11.8 1.7 %collective-permute-start.13 = (bf16[33,16,128]{2,1,0:T(8,128)(2,1)S(1)}, bf16[33,16,128]{2,1,0:T(8,128)(2,1)S(1)}, u32[]{:S(2)}, u32[]{:S(2)}) collective-permute-start(bf16[33,16,128]{2,1,0:T(8,128)(2,1)S(1)} %collective-permute-done.11.refs_12_), channel_id=1, source_target_pairs={{0,2},{1,3},{2,0},{3,1},{4,6},{5,7},{6,4},{7,5},{8,10},{9,11},{10,... | collective-permute-start | bytes 405512 | tf_op jit(solution)/shard_map/ppermute | solution.py:380
  13.5 5.2 %collective-permute-done.7.refs_8_ = bf16[33,16,128]{2,1,0:T(8,128)(2,1)S(1)} collective-permute-done((bf16[33,16,128]{2,1,0:T(8,128)(2,1)S(1)}, bf16[33,16,128]{2,1,0:T(8,128)(2,1)S(1)}, u32[]{:S(2)}, u32[]{:S(2)}) %collective-permute-start.7) | collective-permute-done | bytes 135200 | tf_op jit(solution)/shard_map/ppermute | solution.py:380
  18.7 0.0 collective-permute-start.12
  18.7 0.0 collective-permute-done.3.refs_4_
  18.7 1.5 %collective-permute-start.9 = (bf16[33,16,128]{2,1,0:T(8,128)(2,1)S(1)}, bf16[33,16,128]{2,1,0:T(8,128)(2,1)S(1)}, u32[]{:S(2)}, u32[]{:S(2)}) collective-permute-start(bf16[33,16,128]{2,1,0:T(8,128)(2,1)S(1)} %collective-permute-done.7.refs_8_), channel_id=1, source_target_pairs={{0,2},{1,3},{2,0},{3,1},{4,6},{5,7},{6,4},{7,5},{8,10},{9,11},{10,... | collective-permute-start | bytes 405512 | tf_op jit(solution)/shard_map/ppermute | solution.py:380
  20.2 0.0 collective-permute-done.1.refs_2_
  20.2 0.2 collective-permute-start.8
  20.4 0.0 collective-permute-done.refs_1_
  20.4 0.5 %collective-permute-start.5 = (bf16[33,16,128]{2,1,0:T(8,128)(2,1)S(1)}, bf16[33,16,128]{2,1,0:T(8,128)(2,1)S(1)}, u32[]{:S(2)}, u32[]{:S(2)}) collective-permute-start(bf16[33,16,128]{2,1,0:T(8,128)(2,1)S(1)} %collective-permute-done.3.refs_4_), channel_id=1, source_target_pairs={{0,2},{1,3},{2,0},{3,1},{4,6},{5,7},{6,4},{7,5},{8,10},{9,11},{10,... | collective-permute-start | bytes 405512 | tf_op jit(solution)/shard_map/ppermute | solution.py:380
  20.9 0.0 collective-permute-done.13.refs_14_
  20.9 0.0 collective-permute-start.4
  20.9 0.0 collective-permute-done.12.refs_13_
  20.9 0.5 %collective-permute-start.2 = (bf16[33,16,128]{2,1,0:T(8,128)(2,1)S(1)}, bf16[33,16,128]{2,1,0:T(8,128)(2,1)S(1)}, u32[]{:S(2)}, u32[]{:S(2)}) collective-permute-start(bf16[33,16,128]{2,1,0:T(8,128)(2,1)S(1)} %collective-permute-done.1.refs_2_), channel_id=1, source_target_pairs={{0,1},{1,0},{2,3},{3,2},{4,5},{5,4},{6,7},{7,6},{8,9},{9,8},{10,11... | collective-permute-start | bytes 405512 | tf_op jit(solution)/shard_map/ppermute | solution.py:380
  21.4 3.7 %collective-permute-done.9.refs_10_ = bf16[33,16,128]{2,1,0:T(8,128)(2,1)S(1)} collective-permute-done((bf16[33,16,128]{2,1,0:T(8,128)(2,1)S(1)}, bf16[33,16,128]{2,1,0:T(8,128)(2,1)S(1)}, u32[]{:S(2)}, u32[]{:S(2)}) %collective-permute-start.9) | collective-permute-done | bytes 135200 | tf_op jit(solution)/shard_map/ppermute | solution.py:380
  25.1 0.0 collective-permute-start.14
  25.1 0.0 collective-permute-done.8.refs_9_
  25.1 0.5 %collective-permute-start.10 = (bf16[33,16,128]{2,1,0:T(8,128)(2,1)S(1)}, bf16[33,16,128]{2,1,0:T(8,128)(2,1)S(1)}, u32[]{:S(2)}, u32[]{:S(2)}) collective-permute-start(bf16[33,16,128]{2,1,0:T(8,128)(2,1)S(1)} %collective-permute-done.9.refs_10_), channel_id=1, source_target_pairs={{0,1},{1,0},{2,3},{3,2},{4,5},{5,4},{6,7},{7,6},{8,9},{9,8},{10,11... | collective-permute-start | bytes 405512 | tf_op jit(solution)/shard_map/ppermute | solution.py:380
  25.6 1.9 %collective-permute-done.5.refs_6_ = bf16[33,16,128]{2,1,0:T(8,128)(2,1)S(1)} collective-permute-done((bf16[33,16,128]{2,1,0:T(8,128)(2,1)S(1)}, bf16[33,16,128]{2,1,0:T(8,128)(2,1)S(1)}, u32[]{:S(2)}, u32[]{:S(2)}) %collective-permute-start.5) | collective-permute-done | bytes 135200 | tf_op jit(solution)/shard_map/ppermute | solution.py:380
  27.6 0.0 collective-permute-start.6
  27.6 5.3 %fold.1 = (bf16[8,8,256,256]{3,2,1,0:T(8,128)(2,1)S(1)}, f32[4,512,128]{2,1,0:T(8,128)S(1)}, bf16[512,256]{1,0:T(8,128)(2,1)S(1)}, bf16[4,256,128]{2,1,0:T(8,128)(2,1)S(1)}, bf16[4,128,128]{2,1,0:T(8,128)(2,1)S(1)}) custom-call(bf16[33,16,128]{2,1,0:T(8,128)(2,1)S(1)} %pack.1.pack_ref.refs_0_, bf16[32,64]{1,0:T(8,128)(2,1)} %bitcast.12, ...), custom_call_target="tpu_custom_call" | custom-call | flops 1000000000 | bytes 10000000 | tf_op jit(solution)/shard_map/fold/pallas_call | solution.py:399
  32.9 0.0 collective-permute-done.4.refs_5_
  32.9 0.0 collective-permute-done.2.refs_3_
  32.9 0.0 collective-permute-done.14.refs_15_
  32.9 0.0 collective-permute-done.10.refs_11_
  32.9 0.0 collective-permute-done.6.refs_7_
  32.9 8.1 %main.1 = (bf16[64,16,64]{2,1,0:T(8,128)(2,1)}, bf16[16,256,128]{2,1,0:T(8,128)(2,1)}) custom-call(bf16[33,16,128]{2,1,0:T(8,128)(2,1)S(1)} %pack.1.pack_ref.refs_0_, bf16[33,16,128]{2,1,0:T(8,128)(2,1)S(1)} %collective-permute-done.refs_1_, bf16[33,16,128]{2,1,0:T(8,128)(2,1)S(1)} %collective-permute-done.1.refs_2_, ...), custom_call_target="tpu_custom_call" | custom-call | flops 4000000000 | bytes 10000000 | tf_op jit(solution)/shard_map/main/pallas_call | solution.py:424
Async XLA Ops:
  2.1 9.7 %collective-permute-start.11 = (bf16[33,16,128]{2,1,0:T(8,128)(2,1)S(1)}, bf16[33,16,128]{2,1,0:T(8,128)(2,1)S(1)}, u32[]{:S(2)}, u32[]{:S(2)}) collective-permute-start(bf16[33,16,128]{2,1,0:T(8,128)(2,1)S(1)} %pack.1.pack_ref.refs_0_), channel_id=1, source_target_pairs={{0,12},{1,13},{2,14},{3,15},{4,8},{5,9},{6,10},{7,11},{8,4},{9,5},... | collective-permute-start | bytes 405512 | tf_op jit(solution)/shard_map/ppermute | solution.py:380
  7.2 11.4 %collective-permute-start.7 = (bf16[33,16,128]{2,1,0:T(8,128)(2,1)S(1)}, bf16[33,16,128]{2,1,0:T(8,128)(2,1)S(1)}, u32[]{:S(2)}, u32[]{:S(2)}) collective-permute-start(bf16[33,16,128]{2,1,0:T(8,128)(2,1)S(1)} %pack.1.pack_ref.refs_0_), channel_id=1, source_target_pairs={{0,8},{1,9},{2,10},{3,11},{4,12},{5,13},{6,14},{7,15},{8,0},{9,1},... | collective-permute-start | bytes 405512 | tf_op jit(solution)/shard_map/ppermute | solution.py:380
  7.2 11.4 %collective-permute-start.3 = (bf16[33,16,128]{2,1,0:T(8,128)(2,1)S(1)}, bf16[33,16,128]{2,1,0:T(8,128)(2,1)S(1)}, u32[]{:S(2)}, u32[]{:S(2)}) collective-permute-start(bf16[33,16,128]{2,1,0:T(8,128)(2,1)S(1)} %pack.1.pack_ref.refs_0_), channel_id=1, source_target_pairs={{0,4},{1,5},{2,6},{3,7},{4,0},{5,1},{6,2},{7,3},{8,12},{9,13},{10,... | collective-permute-start | bytes 405512 | tf_op jit(solution)/shard_map/ppermute | solution.py:380
  7.9 12.3 %collective-permute-start.1 = (bf16[33,16,128]{2,1,0:T(8,128)(2,1)S(1)}, bf16[33,16,128]{2,1,0:T(8,128)(2,1)S(1)}, u32[]{:S(2)}, u32[]{:S(2)}) collective-permute-start(bf16[33,16,128]{2,1,0:T(8,128)(2,1)S(1)} %pack.1.pack_ref.refs_0_), channel_id=1, source_target_pairs={{0,2},{1,3},{2,0},{3,1},{4,6},{5,7},{6,4},{7,5},{8,10},{9,11},{10,... | collective-permute-start | bytes 405512 | tf_op jit(solution)/shard_map/ppermute | solution.py:380
  9.5 10.9 %collective-permute-start = (bf16[33,16,128]{2,1,0:T(8,128)(2,1)S(1)}, bf16[33,16,128]{2,1,0:T(8,128)(2,1)S(1)}, u32[]{:S(2)}, u32[]{:S(2)}) collective-permute-start(bf16[33,16,128]{2,1,0:T(8,128)(2,1)S(1)} %pack.1.pack_ref.refs_0_), channel_id=1, source_target_pairs={{0,1},{1,0},{2,3},{3,2},{4,5},{5,4},{6,7},{7,6},{8,9},{9,8},{10,11... | collective-permute-start | bytes 405512 | tf_op jit(solution)/shard_map/ppermute | solution.py:380
  11.8 9.2 %collective-permute-start.13 = (bf16[33,16,128]{2,1,0:T(8,128)(2,1)S(1)}, bf16[33,16,128]{2,1,0:T(8,128)(2,1)S(1)}, u32[]{:S(2)}, u32[]{:S(2)}) collective-permute-start(bf16[33,16,128]{2,1,0:T(8,128)(2,1)S(1)} %collective-permute-done.11.refs_12_), channel_id=1, source_target_pairs={{0,2},{1,3},{2,0},{3,1},{4,6},{5,7},{6,4},{7,5},{8,10},{9,11},{10,... | collective-permute-start | bytes 405512 | tf_op jit(solution)/shard_map/ppermute | solution.py:380
  18.7 2.3 %collective-permute-start.12 = (bf16[33,16,128]{2,1,0:T(8,128)(2,1)S(1)}, bf16[33,16,128]{2,1,0:T(8,128)(2,1)S(1)}, u32[]{:S(2)}, u32[]{:S(2)}) collective-permute-start(bf16[33,16,128]{2,1,0:T(8,128)(2,1)S(1)} %collective-permute-done.11.refs_12_), channel_id=1, source_target_pairs={{0,1},{1,0},{2,3},{3,2},{4,5},{5,4},{6,7},{7,6},{8,9},{9,8},{10,11... | collective-permute-start | bytes 405512 | tf_op jit(solution)/shard_map/ppermute | solution.py:380
  18.7 6.5 %collective-permute-start.9 = (bf16[33,16,128]{2,1,0:T(8,128)(2,1)S(1)}, bf16[33,16,128]{2,1,0:T(8,128)(2,1)S(1)}, u32[]{:S(2)}, u32[]{:S(2)}) collective-permute-start(bf16[33,16,128]{2,1,0:T(8,128)(2,1)S(1)} %collective-permute-done.7.refs_8_), channel_id=1, source_target_pairs={{0,2},{1,3},{2,0},{3,1},{4,6},{5,7},{6,4},{7,5},{8,10},{9,11},{10,... | collective-permute-start | bytes 405512 | tf_op jit(solution)/shard_map/ppermute | solution.py:380
  20.2 4.9 %collective-permute-start.8 = (bf16[33,16,128]{2,1,0:T(8,128)(2,1)S(1)}, bf16[33,16,128]{2,1,0:T(8,128)(2,1)S(1)}, u32[]{:S(2)}, u32[]{:S(2)}) collective-permute-start(bf16[33,16,128]{2,1,0:T(8,128)(2,1)S(1)} %collective-permute-done.7.refs_8_), channel_id=1, source_target_pairs={{0,1},{1,0},{2,3},{3,2},{4,5},{5,4},{6,7},{7,6},{8,9},{9,8},{10,11... | collective-permute-start | bytes 405512 | tf_op jit(solution)/shard_map/ppermute | solution.py:380
  20.4 7.1 %collective-permute-start.5 = (bf16[33,16,128]{2,1,0:T(8,128)(2,1)S(1)}, bf16[33,16,128]{2,1,0:T(8,128)(2,1)S(1)}, u32[]{:S(2)}, u32[]{:S(2)}) collective-permute-start(bf16[33,16,128]{2,1,0:T(8,128)(2,1)S(1)} %collective-permute-done.3.refs_4_), channel_id=1, source_target_pairs={{0,2},{1,3},{2,0},{3,1},{4,6},{5,7},{6,4},{7,5},{8,10},{9,11},{10,... | collective-permute-start | bytes 405512 | tf_op jit(solution)/shard_map/ppermute | solution.py:380
  20.9 11.9 %collective-permute-start.4 = (bf16[33,16,128]{2,1,0:T(8,128)(2,1)S(1)}, bf16[33,16,128]{2,1,0:T(8,128)(2,1)S(1)}, u32[]{:S(2)}, u32[]{:S(2)}) collective-permute-start(bf16[33,16,128]{2,1,0:T(8,128)(2,1)S(1)} %collective-permute-done.3.refs_4_), channel_id=1, source_target_pairs={{0,1},{1,0},{2,3},{3,2},{4,5},{5,4},{6,7},{7,6},{8,9},{9,8},{10,11... | collective-permute-start | bytes 405512 | tf_op jit(solution)/shard_map/ppermute | solution.py:380
  20.9 11.9 %collective-permute-start.2 = (bf16[33,16,128]{2,1,0:T(8,128)(2,1)S(1)}, bf16[33,16,128]{2,1,0:T(8,128)(2,1)S(1)}, u32[]{:S(2)}, u32[]{:S(2)}) collective-permute-start(bf16[33,16,128]{2,1,0:T(8,128)(2,1)S(1)} %collective-permute-done.1.refs_2_), channel_id=1, source_target_pairs={{0,1},{1,0},{2,3},{3,2},{4,5},{5,4},{6,7},{7,6},{8,9},{9,8},{10,11... | collective-permute-start | bytes 405512 | tf_op jit(solution)/shard_map/ppermute | solution.py:380
  25.1 7.8 %collective-permute-start.14 = (bf16[33,16,128]{2,1,0:T(8,128)(2,1)S(1)}, bf16[33,16,128]{2,1,0:T(8,128)(2,1)S(1)}, u32[]{:S(2)}, u32[]{:S(2)}) collective-permute-start(bf16[33,16,128]{2,1,0:T(8,128)(2,1)S(1)} %collective-permute-done.13.refs_14_), channel_id=1, source_target_pairs={{0,1},{1,0},{2,3},{3,2},{4,5},{5,4},{6,7},{7,6},{8,9},{9,8},{10,11... | collective-permute-start | bytes 405512 | tf_op jit(solution)/shard_map/ppermute | solution.py:380
  25.1 7.8 %collective-permute-start.10 = (bf16[33,16,128]{2,1,0:T(8,128)(2,1)S(1)}, bf16[33,16,128]{2,1,0:T(8,128)(2,1)S(1)}, u32[]{:S(2)}, u32[]{:S(2)}) collective-permute-start(bf16[33,16,128]{2,1,0:T(8,128)(2,1)S(1)} %collective-permute-done.9.refs_10_), channel_id=1, source_target_pairs={{0,1},{1,0},{2,3},{3,2},{4,5},{5,4},{6,7},{7,6},{8,9},{9,8},{10,11... | collective-permute-start | bytes 405512 | tf_op jit(solution)/shard_map/ppermute | solution.py:380
  27.6 5.3 %collective-permute-start.6 = (bf16[33,16,128]{2,1,0:T(8,128)(2,1)S(1)}, bf16[33,16,128]{2,1,0:T(8,128)(2,1)S(1)}, u32[]{:S(2)}, u32[]{:S(2)}) collective-permute-start(bf16[33,16,128]{2,1,0:T(8,128)(2,1)S(1)} %collective-permute-done.5.refs_6_), channel_id=1, source_target_pairs={{0,1},{1,0},{2,3},{3,2},{4,5},{5,4},{6,7},{7,6},{8,9},{9,8},{10,11... | collective-permute-start | bytes 405512 | tf_op jit(solution)/shard_map/ppermute | solution.py:380

commit v2 on v0

--- a/solution.py
+++ b/solution.py
@@ -11,6 +11,7 @@
 F32 = jnp.float32
 BF16 = jnp.bfloat16
 VM = pl.BlockSpec(memory_space=pltpu.VMEM)
+GROUP = 4
 HB = pl.BlockSpec(memory_space=pltpu.HBM)
 
 
@@ -74,13 +75,46 @@
     out_ref[seqs // 2] = mask.astype(BF16)
 
 
+def positions(devs, toks, shifts):
+    me = lax.axis_index("row")
+    spots = []
+    for shift in shifts:
+        where = 0
+        bit = 1
+        while bit < devs:
+            mine = (me // bit) % 2
+            where = where + bit * ((1 - mine) if shift & bit else mine)
+            bit *= 2
+        spots.append(pl.multiple_of(where * toks, toks))
+    return spots
+
+
+def turn_kernel(shifts, state_hbm, turned_ref, state_ref, sems):
+    toks = state_ref.shape[0]
+    copies = [
+        pltpu.make_async_copy(state_hbm.at[i], state_ref.at[i], sems.at[i]) for i in range(toks)
+    ]
+    for copy in copies:
+        copy.start()
+    spots = positions(len(shifts), toks, shifts)
+    group = 128 // toks
+    for i in range(toks):
+        copies[i].wait()
+        for jb in range(len(shifts) // group):
+            rows = [
+                state_ref[i, pl.ds(spot, toks), :] for spot in spots[jb * group : (jb + 1) * group]
+            ]
+            block = jnp.concatenate(rows, axis=0).astype(F32).T
+            turned_ref[i, :, jb * 128 : (jb + 1) * 128] = block.astype(BF16)
+
+
 def fold_kernel(
     seqs,
     heads,
     pack_ref,
     former_hbm,
+    outer_hbm,
     latter_hbm,
-    outer_hbm,
     content_hbm,
     switch_hbm,
     final_hbm,
@@ -90,14 +124,15 @@
     value_ref,
     result_ref,
     former_ref,
+    outer_ref,
     latter_ref,
-    outer_ref,
     content_ref,
     switch_ref,
     final_ref,
     weight_scr,
     left_scr,
     lhs_scr,
+    rhs_scr,
     sems,
 ):
     copies = fetch(
@@ -120,40 +155,40 @@
     mask = pack_ref[half].astype(F32)[:, :seqs]
     for i in range(toks):
         picked = jnp.where(eye, jnp.broadcast_to(mask[i : i + 1], (seqs, seqs)), 0.0)
-        rows_i = left_scr[pl.ds(i, seqs, stride=toks), :][:, :factor].astype(BF16)
-        lhs_scr[i * seqs : (i + 1) * seqs, :] = dot(picked.astype(BF16), rows_i).astype(BF16)
+        rows_i = left_scr[pl.ds(i, seqs, stride=toks), :][:, :factor].T.astype(BF16)
+        rhs_scr[i // 2, :, i % 2 * 2 * seqs : (i % 2 + 1) * 2 * seqs] = twice(
+            dot(rows_i, picked.astype(BF16))
+        ).astype(BF16)
     copies[1].wait()
     weight_scr[...] = outer_ref[...].astype(F32)
     channels = outer_ref.shape[1]
-
-    def step(m, carry):
-        even = weight_scr[pl.ds(2 * m, factor, stride=factor), :]
-        odd = weight_scr[pl.ds(2 * m + 1, factor, stride=factor), :]
-        pair = jnp.concatenate([even, odd], axis=1).astype(BF16)
-        for i in range(toks):
-            block = dot(lhs_scr[i * seqs : (i + 1) * seqs, :], pair)
-            block = block.reshape(outer, 8, 2 * channels)
-            block = jnp.concatenate([block[:, :, :channels], block[:, :, channels:]], axis=1)
-            first = i % 2 * channels
-            folded_ref[
-                i // 2, :, pl.ds(pl.multiple_of(16 * m, 16), 16), first : first + channels
-            ] = block.astype(BF16)
+    for ep in range(factor // 2):
+        even = weight_scr[pl.ds(2 * ep, factor, stride=factor), :]
+        odd = weight_scr[pl.ds(2 * ep + 1, factor, stride=factor), :]
+        lhs_scr[ep * channels : (ep + 1) * channels, :] = jnp.concatenate(
+            [even, odd], axis=0
+        ).T.astype(BF16)
+
+    def step(ip, carry):
+        product = dot(lhs_scr[...], rhs_scr[ip]).astype(BF16)
+        for ep in range(factor // 2):
+            for i2 in range(2):
+                folded_ref[2 * ip + i2, :, ep * 2 * seqs : (ep + 1) * 2 * seqs] = product[
+                    ep * channels : (ep + 1) * channels, i2 * 2 * seqs : (i2 + 1) * 2 * seqs
+                ]
         return carry
 
-    lax.fori_loop(0, factor // 2, step, 0)
+    lax.fori_loop(0, toks // 2, step, 0)
     for copy in copies[2:]:
         copy.wait()
     spread = jnp.where(
-        iota((factor, 8 * factor), 0) == iota((factor, 8 * factor), 1) // 8, 1.0, 0.0
+        iota((8 * factor, factor), 0) // 8 == iota((8 * factor, factor), 1), 1.0, 0.0
     ).astype(BF16)
-    wide = dot(latter_ref[...].astype(F32).T.astype(BF16), spread)
-    lane = iota(wide.shape, 1) % 8
-    for rest in range(4):
-        for s2 in range(2):
-            base = (rest * 2 + s2) * width
-            right_ref[base : base + width, :] = jnp.where(lane == s2 * 4 + rest, wide, 0.0).astype(
-                BF16
-            )
+    tall = dot(spread, latter_ref[...])
+    row = iota(tall.shape, 0) % 8
+    right_ref[...] = jnp.concatenate(
+        [jnp.where(row == s2 * 4 + rest, tall, 0.0) for rest in range(4) for s2 in range(2)], axis=1
+    ).astype(BF16)
     column = content_ref.shape[1] // heads
     for hp in range(heads // 2):
         cols = slice(2 * column * hp, 2 * column * (hp + 1))
@@ -174,9 +209,9 @@
     blocks = refs[: len(shifts)]
     (
         rows_hbm,
-        state_hbm,
         weight_hbm,
         gain_hbm,
+        turned_ref,
         folded_ref,
         gate_ref,
         right_ref,
@@ -185,20 +220,21 @@
         out_ref,
         pair_hbm,
         rows_ref,
-        state_ref,
         weight_ref,
         gain_ref,
         pair_ref,
-        wide_scr,
+        mask_scr,
         rhs_scr,
         logits_scr,
         mixed_scr,
+        even_scr,
+        odd_scr,
         sems,
         pair_sem,
     ) = refs[len(shifts) :]
     copies = fetch(
-        (weight_hbm, gain_hbm, state_hbm, rows_hbm),
-        (weight_ref, gain_ref, state_ref, rows_ref),
+        (weight_hbm, gain_hbm, rows_hbm),
+        (weight_ref, gain_ref, rows_ref),
         sems,
     )
     half = seqs // 2
@@ -206,73 +242,66 @@
     devs = len(shifts)
     _, toks, lanes = blocks[0].shape
     tokens = devs * toks
-    me = lax.axis_index("row")
-
-    def place(shift):
-        where = 0
-        bit = 1
-        while bit < devs:
-            mine = (me // bit) % 2
-            where = where + bit * ((1 - mine) if shift & bit else mine)
-            bit *= 2
-        return pl.multiple_of(where * toks, toks)
-
-    spots = [place(k) for k in shifts]
+    tiles = tokens // 128
+    spots = positions(devs, toks, shifts)
 
     def gathered(n):
         return jnp.concatenate([block[n] for block in blocks], axis=0)
 
     mask = gathered(half)
-    inverse = 1.0 / (1.0 + dot_nt(mask, jnp.where(iota((toks, lanes), 1) < seqs, blocks[0][half], 0)))
-    real = dot_nt(jnp.where(iota((8, lanes), 1) == seqs, 1.0, 0.0).astype(BF16), mask)
-    wide = right_ref.shape[1]
-    which = iota((lanes, wide), 0) - iota((lanes, wide), 1) % 8
-    for so in range(outer):
-        pick = jnp.where(which == 8 * so, 1.0, 0.0).astype(BF16)
-        wide_scr[:, so * wide : (so + 1) * wide] = dot(mask, pick).astype(BF16)
-    for so in range(outer):
-        rows = jnp.concatenate([gathered(so * 4 + r) for r in range(4)], axis=1)
-        cols = slice(so * wide, (so + 1) * wide)
-        rhs_scr[:, cols] = (dot(rows, right_ref[...]) * wide_scr[:, cols].astype(F32)).astype(BF16)
-    for copy in copies:
+    own = jnp.where(iota((toks, lanes), 1) < seqs, blocks[0][half], 0)
+    inverse = 1.0 / (1.0 + dot_nt(own, mask))
+    pick = jnp.where(iota((seqs + 8, lanes), 0) == iota((seqs + 8, lanes), 1), 1.0, 0.0)
+    mask_scr[...] = dot_nt(pick.astype(BF16), mask)
+    real = mask_scr[seqs : seqs + 1, :]
+    factor = rhs_scr.shape[0]
+    for so in range(0, outer, 2):
+        pieces = []
+        for n in (so, so + 1):
+            rows = jnp.concatenate([gathered(n * 4 + r) for r in range(4)], axis=1)
+            right = dot_nt(right_ref[...], rows).reshape(factor, 8, tokens)
+            pieces.append(right * mask_scr[n * 8 : n * 8 + 8, :])
+        rhs_scr[:, so * 8 : so * 8 + 16, :] = jnp.concatenate(pieces, axis=1).astype(BF16)
+    for copy in copies[:2]:
         copy.wait()
     w_high, w_low = split(weight_ref[...] * gain_ref[...])
-    lhs = jnp.concatenate(
-        [
-            jnp.concatenate([w_high, w_high], axis=1),
-            jnp.concatenate([w_low, jnp.zeros_like(w_low)], axis=1),
-        ],
-        axis=0,
-    )
-    channels = state_ref.shape[-1]
-
-    def product(ip):
-        return dot(rhs_scr[...], folded_ref[ip].reshape(outer * wide, 2 * channels))
-
-    acc = product(0)
-    for ip in range(toks // 2):
-        later = product(ip + 1) if ip + 1 < toks // 2 else None
-        for i2 in range(2):
-            i = 2 * ip + i2
-            x = jnp.concatenate([state_ref[i, pl.ds(spot, toks), :] for spot in spots], axis=0)
-            x = x.astype(F32) + acc[:, i2 * channels : (i2 + 1) * channels] * inverse[:, i : i + 1]
-            x = x.astype(BF16)
-            for n, spot in enumerate(spots):
-                pair_ref[i, pl.ds(spot, toks), :] = x[n * toks : (n + 1) * toks]
+    weights = jnp.concatenate([w_high, w_low], axis=0)
+    w_sum = jnp.sum(w_high.astype(F32) + w_low.astype(F32), axis=1, keepdims=True)
+    channels = turned_ref.shape[1]
+    group = even_scr.shape[0] // channels
+
+    def product(g, acc_scr):
+        rows = folded_ref[g * group : (g + 1) * group].reshape(group * channels, -1)
+        acc_scr[...] = dot(rows, rhs_scr[...].reshape(factor * seqs, tokens))
+
+    def finish(g, acc_scr):
+        for n in range(group):
+            i = g * group + n
+            for jb in range(tiles):
+                cols = slice(jb * 128, (jb + 1) * 128)
+                update = acc_scr[n * channels : (n + 1) * channels, cols] * inverse[i : i + 1, cols]
+                x = (turned_ref[i, :, cols].astype(F32) + update).astype(BF16)
+                logits = dot(weights, x)
+                x = x.astype(F32)
+                turned = x.T.astype(BF16)
+                for k in range(128 // toks):
+                    spot = spots[jb * (128 // toks) + k]
+                    pair_ref[i, pl.ds(spot, toks), :] = turned[k * toks : (k + 1) * toks]
+                mean = jnp.mean(x, axis=0, keepdims=True)
+                x = x - mean
+                scale = lax.rsqrt(jnp.mean(x * x, axis=0, keepdims=True) + 1e-05)
+                logits = (logits[:heads] + logits[heads:] - w_sum * mean) * scale
+                logits_scr[jb, pl.ds(i, heads, stride=toks), :] = logits
             pltpu.make_async_copy(pair_ref.at[i], pair_hbm.at[i], pair_sem.at[i]).start()
-            x = x.astype(F32)
-            x = x - jnp.mean(x, axis=-1, keepdims=True)
-            spread = jnp.mean(x * x, axis=-1, keepdims=True)
-            high, low = split(x * lax.rsqrt(spread + 1e-05))
-            logits = dot_nt(lhs, jnp.concatenate([high, low], axis=1))
-            logits = logits[:heads] + logits[heads:]
-            for jb in range(tokens // 128):
-                logits_scr[jb, pl.ds(i, heads, stride=toks), :] = logits[
-                    :, jb * 128 : jb * 128 + 128
-                ]
-        acc = later
-    logits = jnp.concatenate([logits_scr[jb] for jb in range(tokens // 128)], axis=1)
-    logits = jnp.where(real[:1] > 0.5, logits, -1000000000.0)
+
+    scratch = (even_scr, odd_scr)
+    product(0, even_scr)
+    for g in range(toks // group):
+        if g + 1 < toks // group:
+            product(g + 1, scratch[(g + 1) % 2])
+        finish(g, scratch[g % 2])
+    logits = jnp.concatenate([logits_scr[jb] for jb in range(tiles)], axis=1)
+    logits = jnp.where(real > 0.5, logits, -1000000000.0)
     top = jnp.max(logits, axis=-1, keepdims=True)
     power = jnp.exp(logits - top)
     probs = (power / jnp.sum(power, axis=-1, keepdims=True)).astype(BF16)
@@ -295,6 +324,7 @@
         gated = (gate_ref[hp] * average).astype(BF16)
         part = dot_nt(gated, result_ref[hp])
         total = part if total is None else total + part
+    copies[2].wait()
     width = rows_ref.shape[2]
     total = total.reshape(outer, 4, toks, lanes)
     base = rows_ref[...].astype(F32).reshape(outer, 2, 4, toks, width)
@@ -304,6 +334,11 @@
             out_ref[so * 8 + s2 * 4 : so * 8 + s2 * 4 + 4] = piece[so].astype(BF16)
     for i in range(toks):
         pltpu.make_async_copy(pair_ref.at[i], pair_hbm.at[i], pair_sem.at[i]).wait()
+
+
+def far_order(devs):
+    far = list(range(4, devs, 4))
+    return far[:1] + far[:0:-1]
 
 
 def shards(
@@ -329,7 +364,7 @@
     factor = former_factor_proj.shape[1]
     channels = outer_output_weight.shape[1]
     lanes = 2 * width
-    half, outer = seqs // 2, seqs // 8
+    half = seqs // 2
     params = pltpu.CompilerParams(vmem_limit_bytes=28 << 20)
 
     def keep(*arrays):
@@ -358,17 +393,18 @@
         return lax.ppermute(block, "row", [(n, n ^ shift) for n in range(devs)])
 
     held = {0: packed}
-    for shift in sorted(range(4, devs, 4), reverse=True):
+    far = far_order(devs)
+    for shift in far:
         held[shift] = swap(packed, shift)
     for bit in (2, 1):
-        for shift in sorted(held):
+        for shift in list(held):
             held[shift ^ bit] = swap(held[shift], bit)
     shifts = tuple(sorted(held))
 
     arrays = (
         former_factor_proj.T,
+        outer_output_weight,
         latter_factor_proj.T,
-        outer_output_weight,
         content_vector_proj,
         sigmoid_switch_proj,
         final_result_proj.T,
@@ -376,9 +412,9 @@
     folded, gate, right, value, result = pl.pallas_call(
         functools.partial(fold_kernel, seqs, heads),
         out_shape=(
-            jax.ShapeDtypeStruct((toks // 2, outer, 8 * factor, 2 * channels), BF16),
+            jax.ShapeDtypeStruct((toks, channels, factor * seqs), BF16),
             jax.ShapeDtypeStruct((heads // 2, half * toks, lanes), F32),
-            jax.ShapeDtypeStruct((8 * width, 8 * factor), BF16),
+            jax.ShapeDtypeStruct((8 * factor, 8 * width), BF16),
             jax.ShapeDtypeStruct((heads // 2, 4 * width, lanes), BF16),
             jax.ShapeDtypeStruct((heads // 2, lanes, lanes), BF16),
         ),
@@ -388,7 +424,8 @@
         + [
             pltpu.VMEM(outer_output_weight.shape, F32),
             pltpu.VMEM((seqs * toks, 128), F32),
-            pltpu.VMEM((seqs * toks, factor), BF16),
+            pltpu.VMEM((factor // 2 * channels, 2 * factor), BF16),
+            pltpu.VMEM((toks // 2, 2 * factor, 4 * seqs), BF16),
             pltpu.SemaphoreType.DMA((6,)),
         ],
         compiler_params=params,
@@ -397,29 +434,51 @@
         ),
         name="fold",
     )(packed, *keep(*arrays))
-    arrays = (homolog_embedding, pair_state_tiles, pair_logit_weight.T, pair_norm_gain[None])
+    turned = pl.pallas_call(
+        functools.partial(turn_kernel, shifts),
+        out_shape=jax.ShapeDtypeStruct((toks, channels, tokens), BF16),
+        in_specs=[HB],
+        out_specs=VM,
+        scratch_shapes=room(pair_state_tiles) + [pltpu.SemaphoreType.DMA((toks,))],
+        compiler_params=params,
+        cost_estimate=pl.CostEstimate(flops=10**7, bytes_accessed=10**6, transcendentals=0),
+        name="turn",
+    )(*keep(pair_state_tiles))
+    arrays = (homolog_embedding, pair_logit_weight.T, pair_norm_gain[None])
+    group = GROUP
     out, pair = pl.pallas_call(
         functools.partial(main_kernel, seqs, heads, shifts),
         out_shape=(
             jax.ShapeDtypeStruct(homolog_embedding.shape, BF16),
             jax.ShapeDtypeStruct(pair_state_tiles.shape, BF16),
         ),
-        in_specs=[VM] * devs + [HB] * 4 + [VM] * 5,
+        in_specs=[VM] * devs + [HB] * 3 + [VM] * 6,
         out_specs=(VM, HB),
         scratch_shapes=room(*arrays)
         + [
             pltpu.VMEM(pair_state_tiles.shape, BF16),
-            pltpu.VMEM((tokens, outer * 8 * factor), BF16),
-            pltpu.VMEM((tokens, outer * 8 * factor), BF16),
+            pltpu.VMEM((seqs + 8, tokens), F32),
+            pltpu.VMEM((factor, seqs, tokens), BF16),
             pltpu.VMEM((tokens // 128, heads * toks, 128), F32),
             pltpu.VMEM((half, heads * toks, lanes), BF16),
-            pltpu.SemaphoreType.DMA((4,)),
+            pltpu.VMEM((group * channels, tokens), F32),
+            pltpu.VMEM((group * channels, tokens), F32),
+            pltpu.SemaphoreType.DMA((3,)),
             pltpu.SemaphoreType.DMA((toks,)),
         ],
         compiler_params=params,
         cost_estimate=pl.CostEstimate(flops=4 * 10**9, bytes_accessed=10**7, transcendentals=10**6),
         name="main",
-    )(*[held[shift] for shift in shifts], *keep(*arrays), folded, gate, right, value, result)
+    )(
+        *[held[shift] for shift in shifts],
+        *keep(*arrays),
+        turned,
+        folded,
+        gate,
+        right,
+        value,
+        result,
+    )
     return out, pair
 
 

time: 43.8 us -> 43.2 us (0.986)
  Pallas kernels: 17.4 us -> 16.7 us
    pallas_call x1, Pallas kernels: 9.54 us -> 6.69 us  [shards(): pl.pallas_call(functools.partial(main_kernel, seqs, heads, shifts), out_s...]
    pallas_call x0 -> x1, Pallas kernels: none -> 2.67 us  [shards(): pl.pallas_call(functools.partial(turn_kernel, shifts), out_shape=jax.Shap...]
    pallas_call x1, Pallas kernels: 6.41 us -> 5.92 us  [shards(): pl.pallas_call(functools.partial(fold_kernel, seqs, heads), out_shape=(ja...]
  transfers between devices with their start and end apart: 15 -> 15, of which waited for: 4 -> 4; matrix products, arithmetic and copies ran while one was open for 0% -> 0% of each run, Pallas kernels for 15% -> 20%
where the time goes in v2:
time: 43.2 us; the launch traced here: 42.9 us
  Pallas kernels  16.7 us (39%)
  waiting for transfers between devices  13 us (30%)
  starting transfers between devices  12.4 us (29%)
  between operations  0.71 us (2%)
    ppermute x15, waiting for transfers between devices, swap(): return lax.ppermute(block, 'row', [(n, n ^ shift) for n in range(devs)])  13 us
    ppermute x15, starting transfers between devices, swap(): return lax.ppermute(block, 'row', [(n, n ^ shift) for n in range(devs)])  12.4 us
    pallas_call x1, Pallas kernels, shards(): pl.pallas_call(functools.partial(main_kernel, seqs, heads, shifts), out_s...  6.69 us
    pallas_call x1, Pallas kernels, shards(): pl.pallas_call(functools.partial(fold_kernel, seqs, heads), out_shape=(ja...  5.92 us
    pallas_call x1, Pallas kernels, shards(): pl.pallas_call(functools.partial(turn_kernel, shifts), out_shape=jax.Shap...  2.67 us
    pallas_call x1, Pallas kernels, shards(): pl.pallas_call(pack_kernel, out_shape=jax.ShapeDtypeStruct((half + 1, tok...  1.45 us
  transfers between devices with their start and end apart: 15, of which 4 were waited for; matrix products, arithmetic and copies ran while one was open for 0% of the time, Pallas kernels for 20%

profile of v2, /device:TPU:0, one launch (start us, length us, event | category | flops | bytes accessed | tf_op | source)
XLA Modules:
  0.0 42.9 jit_solution(12797787021806233272)
XLA Ops:
  0.6 1.4 %pack.1.pack_ref.refs_0_ = bf16[33,16,128]{2,1,0:T(8,128)(2,1)S(1)} custom-call(bf16[64,16,64]{2,1,0:T(8,128)(2,1)} %refs_16_.1, s32[16,64]{1,0:T(8,128)} %bitcast.8, f32[1,64]{1,0:T(1,128)} %bitcast.10, s32[1,256]{1,0:T(1,128)} %bitcast.9), custom_call_target="tpu_custom_call" | custom-call | tf_op jit(solution)/shard_map/pack/pallas_call | solution.py:382
  2.1 5.1 %collective-permute-start.11 = (bf16[33,16,128]{2,1,0:T(8,128)(2,1)S(1)}, bf16[33,16,128]{2,1,0:T(8,128)(2,1)S(1)}, u32[]{:S(2)}, u32[]{:S(2)}) collective-permute-start(bf16[33,16,128]{2,1,0:T(8,128)(2,1)S(1)} %pack.1.pack_ref.refs_0_), channel_id=1, source_target_pairs={{0,12},{1,13},{2,14},{3,15},{4,8},{5,9},{6,10},{7,11},{8,4},{9,5},... | collective-permute-start | bytes 405512 | tf_op jit(solution)/shard_map/ppermute | solution.py:393
  7.2 0.0 collective-permute-start.7
  7.2 0.6 %collective-permute-start.3 = (bf16[33,16,128]{2,1,0:T(8,128)(2,1)S(1)}, bf16[33,16,128]{2,1,0:T(8,128)(2,1)S(1)}, u32[]{:S(2)}, u32[]{:S(2)}) collective-permute-start(bf16[33,16,128]{2,1,0:T(8,128)(2,1)S(1)} %pack.1.pack_ref.refs_0_), channel_id=1, source_target_pairs={{0,4},{1,5},{2,6},{3,7},{4,0},{5,1},{6,2},{7,3},{8,12},{9,13},{10,... | collective-permute-start | bytes 405512 | tf_op jit(solution)/shard_map/ppermute | solution.py:393
  7.9 1.7 %collective-permute-start.1 = (bf16[33,16,128]{2,1,0:T(8,128)(2,1)S(1)}, bf16[33,16,128]{2,1,0:T(8,128)(2,1)S(1)}, u32[]{:S(2)}, u32[]{:S(2)}) collective-permute-start(bf16[33,16,128]{2,1,0:T(8,128)(2,1)S(1)} %pack.1.pack_ref.refs_0_), channel_id=1, source_target_pairs={{0,2},{1,3},{2,0},{3,1},{4,6},{5,7},{6,4},{7,5},{8,10},{9,11},{10,... | collective-permute-start | bytes 405512 | tf_op jit(solution)/shard_map/ppermute | solution.py:393
  9.5 0.0 collective-permute-start
  9.5 2.2 %collective-permute-done.11.refs_12_ = bf16[33,16,128]{2,1,0:T(8,128)(2,1)S(1)} collective-permute-done((bf16[33,16,128]{2,1,0:T(8,128)(2,1)S(1)}, bf16[33,16,128]{2,1,0:T(8,128)(2,1)S(1)}, u32[]{:S(2)}, u32[]{:S(2)}) %collective-permute-start.11) | collective-permute-done | bytes 135200 | tf_op jit(solution)/shard_map/ppermute | solution.py:393
  11.8 1.7 %collective-permute-start.13 = (bf16[33,16,128]{2,1,0:T(8,128)(2,1)S(1)}, bf16[33,16,128]{2,1,0:T(8,128)(2,1)S(1)}, u32[]{:S(2)}, u32[]{:S(2)}) collective-permute-start(bf16[33,16,128]{2,1,0:T(8,128)(2,1)S(1)} %collective-permute-done.11.refs_12_), channel_id=1, source_target_pairs={{0,2},{1,3},{2,0},{3,1},{4,6},{5,7},{6,4},{7,5},{8,10},{9,11},{10,... | collective-permute-start | bytes 405512 | tf_op jit(solution)/shard_map/ppermute | solution.py:393
  13.5 5.2 %collective-permute-done.7.refs_8_ = bf16[33,16,128]{2,1,0:T(8,128)(2,1)S(1)} collective-permute-done((bf16[33,16,128]{2,1,0:T(8,128)(2,1)S(1)}, bf16[33,16,128]{2,1,0:T(8,128)(2,1)S(1)}, u32[]{:S(2)}, u32[]{:S(2)}) %collective-permute-start.7) | collective-permute-done | bytes 135200 | tf_op jit(solution)/shard_map/ppermute | solution.py:393
  18.7 0.0 collective-permute-start.12
  18.7 0.0 collective-permute-done.3.refs_4_
  18.7 1.5 %collective-permute-start.9 = (bf16[33,16,128]{2,1,0:T(8,128)(2,1)S(1)}, bf16[33,16,128]{2,1,0:T(8,128)(2,1)S(1)}, u32[]{:S(2)}, u32[]{:S(2)}) collective-permute-start(bf16[33,16,128]{2,1,0:T(8,128)(2,1)S(1)} %collective-permute-done.7.refs_8_), channel_id=1, source_target_pairs={{0,2},{1,3},{2,0},{3,1},{4,6},{5,7},{6,4},{7,5},{8,10},{9,11},{10,... | collective-permute-start | bytes 405512 | tf_op jit(solution)/shard_map/ppermute | solution.py:393
  20.2 0.0 collective-permute-done.1.refs_2_
  20.2 0.2 collective-permute-start.8
  20.4 0.0 collective-permute-done.refs_1_
  20.4 0.5 %collective-permute-start.5 = (bf16[33,16,128]{2,1,0:T(8,128)(2,1)S(1)}, bf16[33,16,128]{2,1,0:T(8,128)(2,1)S(1)}, u32[]{:S(2)}, u32[]{:S(2)}) collective-permute-start(bf16[33,16,128]{2,1,0:T(8,128)(2,1)S(1)} %collective-permute-done.3.refs_4_), channel_id=1, source_target_pairs={{0,2},{1,3},{2,0},{3,1},{4,6},{5,7},{6,4},{7,5},{8,10},{9,11},{10,... | collective-permute-start | bytes 405512 | tf_op jit(solution)/shard_map/ppermute | solution.py:393
  20.9 0.0 collective-permute-done.13.refs_14_
  20.9 0.0 collective-permute-start.4
  20.9 0.0 collective-permute-done.12.refs_13_
  20.9 0.5 %collective-permute-start.2 = (bf16[33,16,128]{2,1,0:T(8,128)(2,1)S(1)}, bf16[33,16,128]{2,1,0:T(8,128)(2,1)S(1)}, u32[]{:S(2)}, u32[]{:S(2)}) collective-permute-start(bf16[33,16,128]{2,1,0:T(8,128)(2,1)S(1)} %collective-permute-done.1.refs_2_), channel_id=1, source_target_pairs={{0,1},{1,0},{2,3},{3,2},{4,5},{5,4},{6,7},{7,6},{8,9},{9,8},{10,11... | collective-permute-start | bytes 405512 | tf_op jit(solution)/shard_map/ppermute | solution.py:393
  21.4 3.7 %collective-permute-done.9.refs_10_ = bf16[33,16,128]{2,1,0:T(8,128)(2,1)S(1)} collective-permute-done((bf16[33,16,128]{2,1,0:T(8,128)(2,1)S(1)}, bf16[33,16,128]{2,1,0:T(8,128)(2,1)S(1)}, u32[]{:S(2)}, u32[]{:S(2)}) %collective-permute-start.9) | collective-permute-done | bytes 135200 | tf_op jit(solution)/shard_map/ppermute | solution.py:393
  25.1 0.0 collective-permute-start.14
  25.1 0.0 collective-permute-done.8.refs_9_
  25.1 0.5 %collective-permute-start.10 = (bf16[33,16,128]{2,1,0:T(8,128)(2,1)S(1)}, bf16[33,16,128]{2,1,0:T(8,128)(2,1)S(1)}, u32[]{:S(2)}, u32[]{:S(2)}) collective-permute-start(bf16[33,16,128]{2,1,0:T(8,128)(2,1)S(1)} %collective-permute-done.9.refs_10_), channel_id=1, source_target_pairs={{0,1},{1,0},{2,3},{3,2},{4,5},{5,4},{6,7},{7,6},{8,9},{9,8},{10,11... | collective-permute-start | bytes 405512 | tf_op jit(solution)/shard_map/ppermute | solution.py:393
  25.6 1.9 %collective-permute-done.5.refs_6_ = bf16[33,16,128]{2,1,0:T(8,128)(2,1)S(1)} collective-permute-done((bf16[33,16,128]{2,1,0:T(8,128)(2,1)S(1)}, bf16[33,16,128]{2,1,0:T(8,128)(2,1)S(1)}, u32[]{:S(2)}, u32[]{:S(2)}) %collective-permute-start.5) | collective-permute-done | bytes 135200 | tf_op jit(solution)/shard_map/ppermute | solution.py:393
  27.6 0.0 collective-permute-start.6
  27.6 2.7 %turn.1.refs_19_ = bf16[16,128,256]{2,1,0:T(8,128)(2,1)S(1)} custom-call(bf16[16,256,128]{2,1,0:T(8,128)(2,1)} %state_hbm.1), custom_call_target="tpu_custom_call" | custom-call | flops 10000000 | bytes 1000000 | tf_op jit(solution)/shard_map/turn/pallas_call | solution.py:437
  30.2 5.9 %fold.1 = (bf16[16,128,2048]{2,1,0:T(8,128)(2,1)S(1)}, f32[4,512,128]{2,1,0:T(8,128)S(1)}, bf16[256,512]{1,0:T(8,128)(2,1)S(1)}, bf16[4,256,128]{2,1,0:T(8,128)(2,1)S(1)}, bf16[4,128,128]{2,1,0:T(8,128)(2,1)S(1)}) custom-call(bf16[33,16,128]{2,1,0:T(8,128)(2,1)S(1)} %pack.1.pack_ref.refs_0_, bf16[32,64]{1,0:T(8,128)(2,1)} %bitcast.12, ...), custom_call_target="tpu_custom_call" | custom-call | flops 1000000000 | bytes 10000000 | tf_op jit(solution)/shard_map/fold/pallas_call | solution.py:412
  36.2 0.0 collective-permute-done.4.refs_5_
  36.2 0.0 collective-permute-done.2.refs_3_
  36.2 0.0 collective-permute-done.14.refs_15_
  36.2 0.0 collective-permute-done.10.refs_11_
  36.2 0.0 collective-permute-done.6.refs_7_
  36.2 6.7 %main.1 = (bf16[64,16,64]{2,1,0:T(8,128)(2,1)}, bf16[16,256,128]{2,1,0:T(8,128)(2,1)}) custom-call(bf16[33,16,128]{2,1,0:T(8,128)(2,1)S(1)} %pack.1.pack_ref.refs_0_, bf16[33,16,128]{2,1,0:T(8,128)(2,1)S(1)} %collective-permute-done.refs_1_, bf16[33,16,128]{2,1,0:T(8,128)(2,1)S(1)} %collective-permute-done.1.refs_2_, ...), custom_call_target="tpu_custom_call" | custom-call | flops 4000000000 | bytes 10000000 | tf_op jit(solution)/shard_map/main/pallas_call | solution.py:449
Async XLA Ops:
  2.1 9.7 %collective-permute-start.11 = (bf16[33,16,128]{2,1,0:T(8,128)(2,1)S(1)}, bf16[33,16,128]{2,1,0:T(8,128)(2,1)S(1)}, u32[]{:S(2)}, u32[]{:S(2)}) collective-permute-start(bf16[33,16,128]{2,1,0:T(8,128)(2,1)S(1)} %pack.1.pack_ref.refs_0_), channel_id=1, source_target_pairs={{0,12},{1,13},{2,14},{3,15},{4,8},{5,9},{6,10},{7,11},{8,4},{9,5},... | collective-permute-start | bytes 405512 | tf_op jit(solution)/shard_map/ppermute | solution.py:393
  7.2 11.4 %collective-permute-start.7 = (bf16[33,16,128]{2,1,0:T(8,128)(2,1)S(1)}, bf16[33,16,128]{2,1,0:T(8,128)(2,1)S(1)}, u32[]{:S(2)}, u32[]{:S(2)}) collective-permute-start(bf16[33,16,128]{2,1,0:T(8,128)(2,1)S(1)} %pack.1.pack_ref.refs_0_), channel_id=1, source_target_pairs={{0,8},{1,9},{2,10},{3,11},{4,12},{5,13},{6,14},{7,15},{8,0},{9,1},... | collective-permute-start | bytes 405512 | tf_op jit(solution)/shard_map/ppermute | solution.py:393
  7.2 11.4 %collective-permute-start.3 = (bf16[33,16,128]{2,1,0:T(8,128)(2,1)S(1)}, bf16[33,16,128]{2,1,0:T(8,128)(2,1)S(1)}, u32[]{:S(2)}, u32[]{:S(2)}) collective-permute-start(bf16[33,16,128]{2,1,0:T(8,128)(2,1)S(1)} %pack.1.pack_ref.refs_0_), channel_id=1, source_target_pairs={{0,4},{1,5},{2,6},{3,7},{4,0},{5,1},{6,2},{7,3},{8,12},{9,13},{10,... | collective-permute-start | bytes 405512 | tf_op jit(solution)/shard_map/ppermute | solution.py:393
  7.9 12.3 %collective-permute-start.1 = (bf16[33,16,128]{2,1,0:T(8,128)(2,1)S(1)}, bf16[33,16,128]{2,1,0:T(8,128)(2,1)S(1)}, u32[]{:S(2)}, u32[]{:S(2)}) collective-permute-start(bf16[33,16,128]{2,1,0:T(8,128)(2,1)S(1)} %pack.1.pack_ref.refs_0_), channel_id=1, source_target_pairs={{0,2},{1,3},{2,0},{3,1},{4,6},{5,7},{6,4},{7,5},{8,10},{9,11},{10,... | collective-permute-start | bytes 405512 | tf_op jit(solution)/shard_map/ppermute | solution.py:393
  9.5 10.9 %collective-permute-start = (bf16[33,16,128]{2,1,0:T(8,128)(2,1)S(1)}, bf16[33,16,128]{2,1,0:T(8,128)(2,1)S(1)}, u32[]{:S(2)}, u32[]{:S(2)}) collective-permute-start(bf16[33,16,128]{2,1,0:T(8,128)(2,1)S(1)} %pack.1.pack_ref.refs_0_), channel_id=1, source_target_pairs={{0,1},{1,0},{2,3},{3,2},{4,5},{5,4},{6,7},{7,6},{8,9},{9,8},{10,11... | collective-permute-start | bytes 405512 | tf_op jit(solution)/shard_map/ppermute | solution.py:393
  11.8 9.2 %collective-permute-start.13 = (bf16[33,16,128]{2,1,0:T(8,128)(2,1)S(1)}, bf16[33,16,128]{2,1,0:T(8,128)(2,1)S(1)}, u32[]{:S(2)}, u32[]{:S(2)}) collective-permute-start(bf16[33,16,128]{2,1,0:T(8,128)(2,1)S(1)} %collective-permute-done.11.refs_12_), channel_id=1, source_target_pairs={{0,2},{1,3},{2,0},{3,1},{4,6},{5,7},{6,4},{7,5},{8,10},{9,11},{10,... | collective-permute-start | bytes 405512 | tf_op jit(solution)/shard_map/ppermute | solution.py:393
  18.7 2.3 %collective-permute-start.12 = (bf16[33,16,128]{2,1,0:T(8,128)(2,1)S(1)}, bf16[33,16,128]{2,1,0:T(8,128)(2,1)S(1)}, u32[]{:S(2)}, u32[]{:S(2)}) collective-permute-start(bf16[33,16,128]{2,1,0:T(8,128)(2,1)S(1)} %collective-permute-done.11.refs_12_), channel_id=1, source_target_pairs={{0,1},{1,0},{2,3},{3,2},{4,5},{5,4},{6,7},{7,6},{8,9},{9,8},{10,11... | collective-permute-start | bytes 405512 | tf_op jit(solution)/shard_map/ppermute | solution.py:393
  18.7 6.5 %collective-permute-start.9 = (bf16[33,16,128]{2,1,0:T(8,128)(2,1)S(1)}, bf16[33,16,128]{2,1,0:T(8,128)(2,1)S(1)}, u32[]{:S(2)}, u32[]{:S(2)}) collective-permute-start(bf16[33,16,128]{2,1,0:T(8,128)(2,1)S(1)} %collective-permute-done.7.refs_8_), channel_id=1, source_target_pairs={{0,2},{1,3},{2,0},{3,1},{4,6},{5,7},{6,4},{7,5},{8,10},{9,11},{10,... | collective-permute-start | bytes 405512 | tf_op jit(solution)/shard_map/ppermute | solution.py:393
  20.2 4.9 %collective-permute-start.8 = (bf16[33,16,128]{2,1,0:T(8,128)(2,1)S(1)}, bf16[33,16,128]{2,1,0:T(8,128)(2,1)S(1)}, u32[]{:S(2)}, u32[]{:S(2)}) collective-permute-start(bf16[33,16,128]{2,1,0:T(8,128)(2,1)S(1)} %collective-permute-done.7.refs_8_), channel_id=1, source_target_pairs={{0,1},{1,0},{2,3},{3,2},{4,5},{5,4},{6,7},{7,6},{8,9},{9,8},{10,11... | collective-permute-start | bytes 405512 | tf_op jit(solution)/shard_map/ppermute | solution.py:393
  20.4 7.1 %collective-permute-start.5 = (bf16[33,16,128]{2,1,0:T(8,128)(2,1)S(1)}, bf16[33,16,128]{2,1,0:T(8,128)(2,1)S(1)}, u32[]{:S(2)}, u32[]{:S(2)}) collective-permute-start(bf16[33,16,128]{2,1,0:T(8,128)(2,1)S(1)} %collective-permute-done.3.refs_4_), channel_id=1, source_target_pairs={{0,2},{1,3},{2,0},{3,1},{4,6},{5,7},{6,4},{7,5},{8,10},{9,11},{10,... | collective-permute-start | bytes 405512 | tf_op jit(solution)/shard_map/ppermute | solution.py:393
  20.9 15.2 %collective-permute-start.4 = (bf16[33,16,128]{2,1,0:T(8,128)(2,1)S(1)}, bf16[33,16,128]{2,1,0:T(8,128)(2,1)S(1)}, u32[]{:S(2)}, u32[]{:S(2)}) collective-permute-start(bf16[33,16,128]{2,1,0:T(8,128)(2,1)S(1)} %collective-permute-done.3.refs_4_), channel_id=1, source_target_pairs={{0,1},{1,0},{2,3},{3,2},{4,5},{5,4},{6,7},{7,6},{8,9},{9,8},{10,11... | collective-permute-start | bytes 405512 | tf_op jit(solution)/shard_map/ppermute | solution.py:393
  20.9 15.2 %collective-permute-start.2 = (bf16[33,16,128]{2,1,0:T(8,128)(2,1)S(1)}, bf16[33,16,128]{2,1,0:T(8,128)(2,1)S(1)}, u32[]{:S(2)}, u32[]{:S(2)}) collective-permute-start(bf16[33,16,128]{2,1,0:T(8,128)(2,1)S(1)} %collective-permute-done.1.refs_2_), channel_id=1, source_target_pairs={{0,1},{1,0},{2,3},{3,2},{4,5},{5,4},{6,7},{7,6},{8,9},{9,8},{10,11... | collective-permute-start | bytes 405512 | tf_op jit(solution)/shard_map/ppermute | solution.py:393
  25.1 11.1 %collective-permute-start.14 = (bf16[33,16,128]{2,1,0:T(8,128)(2,1)S(1)}, bf16[33,16,128]{2,1,0:T(8,128)(2,1)S(1)}, u32[]{:S(2)}, u32[]{:S(2)}) collective-permute-start(bf16[33,16,128]{2,1,0:T(8,128)(2,1)S(1)} %collective-permute-done.13.refs_14_), channel_id=1, source_target_pairs={{0,1},{1,0},{2,3},{3,2},{4,5},{5,4},{6,7},{7,6},{8,9},{9,8},{10,11... | collective-permute-start | bytes 405512 | tf_op jit(solution)/shard_map/ppermute | solution.py:393
  25.1 11.1 %collective-permute-start.10 = (bf16[33,16,128]{2,1,0:T(8,128)(2,1)S(1)}, bf16[33,16,128]{2,1,0:T(8,128)(2,1)S(1)}, u32[]{:S(2)}, u32[]{:S(2)}) collective-permute-start(bf16[33,16,128]{2,1,0:T(8,128)(2,1)S(1)} %collective-permute-done.9.refs_10_), channel_id=1, source_target_pairs={{0,1},{1,0},{2,3},{3,2},{4,5},{5,4},{6,7},{7,6},{8,9},{9,8},{10,11... | collective-permute-start | bytes 405512 | tf_op jit(solution)/shard_map/ppermute | solution.py:393
  27.6 8.7 %collective-permute-start.6 = (bf16[33,16,128]{2,1,0:T(8,128)(2,1)S(1)}, bf16[33,16,128]{2,1,0:T(8,128)(2,1)S(1)}, u32[]{:S(2)}, u32[]{:S(2)}) collective-permute-start(bf16[33,16,128]{2,1,0:T(8,128)(2,1)S(1)} %collective-permute-done.5.refs_6_), channel_id=1, source_target_pairs={{0,1},{1,0},{2,3},{3,2},{4,5},{5,4},{6,7},{7,6},{8,9},{9,8},{10,11... | collective-permute-start | bytes 405512 | tf_op jit(solution)/shard_map/ppermute | solution.py:393

commit v3 on v2

--- a/solution.py
+++ b/solution.py
@@ -46,9 +46,24 @@
     return copies
 
 
-def pack_kernel(rows_hbm, mask_hbm, gain_hbm, real_hbm, out_ref, rows_ref, mask_ref, gain_ref, real_ref, sems):
+def pack_kernel(
+    rows_hbm,
+    mask_hbm,
+    gain_hbm,
+    real_hbm,
+    former_hbm,
+    out_ref,
+    former_ref,
+    rows_ref,
+    mask_ref,
+    gain_ref,
+    real_ref,
+    sems,
+):
     copies = fetch(
-        (rows_hbm, mask_hbm, gain_hbm, real_hbm), (rows_ref, mask_ref, gain_ref, real_ref), sems
+        (rows_hbm, mask_hbm, gain_hbm, real_hbm, former_hbm),
+        (rows_ref, mask_ref, gain_ref, real_ref, former_ref),
+        sems,
     )
     for copy in copies:
         copy.wait()
@@ -89,17 +104,11 @@
     return spots
 
 
-def turn_kernel(shifts, state_hbm, turned_ref, state_ref, sems):
+def turn_kernel(shifts, state_ref, turned_ref):
     toks = state_ref.shape[0]
-    copies = [
-        pltpu.make_async_copy(state_hbm.at[i], state_ref.at[i], sems.at[i]) for i in range(toks)
-    ]
-    for copy in copies:
-        copy.start()
     spots = positions(len(shifts), toks, shifts)
     group = 128 // toks
     for i in range(toks):
-        copies[i].wait()
         for jb in range(len(shifts) // group):
             rows = [
                 state_ref[i, pl.ds(spot, toks), :] for spot in spots[jb * group : (jb + 1) * group]
@@ -110,41 +119,24 @@
 
 def fold_kernel(
     seqs,
-    heads,
     pack_ref,
-    former_hbm,
+    former_ref,
     outer_hbm,
-    latter_hbm,
-    content_hbm,
-    switch_hbm,
-    final_hbm,
+    state_hbm,
     folded_ref,
-    gate_ref,
-    right_ref,
-    value_ref,
-    result_ref,
-    former_ref,
+    state_ref,
     outer_ref,
-    latter_ref,
-    content_ref,
-    switch_ref,
-    final_ref,
     weight_scr,
     left_scr,
     lhs_scr,
     rhs_scr,
     sems,
 ):
-    copies = fetch(
-        (former_hbm, outer_hbm, latter_hbm, content_hbm, switch_hbm, final_hbm),
-        (former_ref, outer_ref, latter_ref, content_ref, switch_ref, final_ref),
-        sems,
-    )
+    copies = fetch((outer_hbm, state_hbm), (outer_ref, state_ref), sems)
     half, toks, lanes = seqs // 2, pack_ref.shape[1], pack_ref.shape[2]
-    factor, width = former_ref.shape
+    factor, _ = former_ref.shape
     outer = seqs // 8
     rows = pack_ref[:half].reshape(half * toks, lanes)
-    copies[0].wait()
     left = dot_nt(rows, twice(former_ref[...]))
     for so in range(outer):
         for s2 in range(2):
@@ -159,7 +151,7 @@
         rhs_scr[i // 2, :, i % 2 * 2 * seqs : (i % 2 + 1) * 2 * seqs] = twice(
             dot(rows_i, picked.astype(BF16))
         ).astype(BF16)
-    copies[1].wait()
+    copies[0].wait()
     weight_scr[...] = outer_ref[...].astype(F32)
     channels = outer_ref.shape[1]
     for ep in range(factor // 2):
@@ -179,7 +171,36 @@
         return carry
 
     lax.fori_loop(0, toks // 2, step, 0)
-    for copy in copies[2:]:
+    copies[1].wait()
+
+
+def gate_kernel(
+    seqs,
+    heads,
+    pack_ref,
+    latter_hbm,
+    content_hbm,
+    switch_hbm,
+    final_hbm,
+    gate_ref,
+    right_ref,
+    value_ref,
+    result_ref,
+    latter_ref,
+    content_ref,
+    switch_ref,
+    final_ref,
+    sems,
+):
+    copies = fetch(
+        (latter_hbm, content_hbm, switch_hbm, final_hbm),
+        (latter_ref, content_ref, switch_ref, final_ref),
+        sems,
+    )
+    half, toks, lanes = seqs // 2, pack_ref.shape[1], pack_ref.shape[2]
+    factor, width = latter_ref.shape
+    rows = pack_ref[:half].reshape(half * toks, lanes)
+    for copy in copies:
         copy.wait()
     spread = jnp.where(
         iota((8 * factor, factor), 0) // 8 == iota((8 * factor, factor), 1), 1.0, 0.0
@@ -379,15 +400,18 @@
         lineup_standardize_scaling[None],
         token_real_mask[None],
     )
-    packed = pl.pallas_call(
+    packed, former = pl.pallas_call(
         pack_kernel,
-        out_shape=jax.ShapeDtypeStruct((half + 1, toks, lanes), BF16),
-        in_specs=[HB] * 4,
-        out_specs=VM,
-        scratch_shapes=room(*arrays) + [pltpu.SemaphoreType.DMA((4,))],
+        out_shape=(
+            jax.ShapeDtypeStruct((half + 1, toks, lanes), BF16),
+            jax.ShapeDtypeStruct((factor, width), BF16),
+        ),
+        in_specs=[HB] * 5,
+        out_specs=(VM,) * 2,
+        scratch_shapes=room(*arrays) + [pltpu.SemaphoreType.DMA((5,))],
         compiler_params=params,
         name="pack",
-    )(*keep(*arrays))
+    )(*keep(*arrays, former_factor_proj.T))
 
     def swap(block, shift):
         return lax.ppermute(block, "row", [(n, n ^ shift) for n in range(devs)])
@@ -401,49 +425,58 @@
             held[shift ^ bit] = swap(held[shift], bit)
     shifts = tuple(sorted(held))
 
+    folded, state = pl.pallas_call(
+        functools.partial(fold_kernel, seqs),
+        out_shape=(
+            jax.ShapeDtypeStruct((toks, channels, factor * seqs), BF16),
+            jax.ShapeDtypeStruct(pair_state_tiles.shape, BF16),
+        ),
+        in_specs=[VM] * 2 + [HB] * 2,
+        out_specs=(VM,) * 2,
+        scratch_shapes=room(outer_output_weight)
+        + [
+            pltpu.VMEM(outer_output_weight.shape, F32),
+            pltpu.VMEM((seqs * toks, 128), F32),
+            pltpu.VMEM((factor // 2 * channels, 2 * factor), BF16),
+            pltpu.VMEM((toks // 2, 2 * factor, 4 * seqs), BF16),
+            pltpu.SemaphoreType.DMA((2,)),
+        ],
+        compiler_params=params,
+        cost_estimate=pl.CostEstimate(flops=10**9, bytes_accessed=10**7, transcendentals=0),
+        name="fold",
+    )(packed, former, *keep(outer_output_weight, pair_state_tiles))
     arrays = (
-        former_factor_proj.T,
-        outer_output_weight,
         latter_factor_proj.T,
         content_vector_proj,
         sigmoid_switch_proj,
         final_result_proj.T,
     )
-    folded, gate, right, value, result = pl.pallas_call(
-        functools.partial(fold_kernel, seqs, heads),
+    gate, right, value, result = pl.pallas_call(
+        functools.partial(gate_kernel, seqs, heads),
         out_shape=(
-            jax.ShapeDtypeStruct((toks, channels, factor * seqs), BF16),
             jax.ShapeDtypeStruct((heads // 2, half * toks, lanes), F32),
             jax.ShapeDtypeStruct((8 * factor, 8 * width), BF16),
             jax.ShapeDtypeStruct((heads // 2, 4 * width, lanes), BF16),
             jax.ShapeDtypeStruct((heads // 2, lanes, lanes), BF16),
         ),
-        in_specs=[VM] + [HB] * 6,
-        out_specs=(VM,) * 5,
-        scratch_shapes=room(*arrays)
-        + [
-            pltpu.VMEM(outer_output_weight.shape, F32),
-            pltpu.VMEM((seqs * toks, 128), F32),
-            pltpu.VMEM((factor // 2 * channels, 2 * factor), BF16),
-            pltpu.VMEM((toks // 2, 2 * factor, 4 * seqs), BF16),
-            pltpu.SemaphoreType.DMA((6,)),
-        ],
+        in_specs=[VM] + [HB] * 4,
+        out_specs=(VM,) * 4,
+        scratch_shapes=room(*arrays) + [pltpu.SemaphoreType.DMA((4,))],
         compiler_params=params,
         cost_estimate=pl.CostEstimate(
-            flops=10**9, bytes_accessed=10**7, transcendentals=10**6
+            flops=10**8, bytes_accessed=10**6, transcendentals=10**6
         ),
-        name="fold",
+        name="gate",
     )(packed, *keep(*arrays))
     turned = pl.pallas_call(
         functools.partial(turn_kernel, shifts),
         out_shape=jax.ShapeDtypeStruct((toks, channels, tokens), BF16),
-        in_specs=[HB],
+        in_specs=[VM],
         out_specs=VM,
-        scratch_shapes=room(pair_state_tiles) + [pltpu.SemaphoreType.DMA((toks,))],
         compiler_params=params,
         cost_estimate=pl.CostEstimate(flops=10**7, bytes_accessed=10**6, transcendentals=0),
         name="turn",
-    )(*keep(pair_state_tiles))
+    )(state)
     arrays = (homolog_embedding, pair_logit_weight.T, pair_norm_gain[None])
     group = GROUP
     out, pair = pl.pallas_call(

time: 43.2 us -> 41.6 us (0.963)
  Pallas kernels: 16.7 us -> 15.1 us
    pallas_call x1, Pallas kernels: 2.67 us -> 0.38 us  [shards(): pl.pallas_call(functools.partial(turn_kernel, shifts), out_shape=jax.Shap...]
    pallas_call x2 -> x3, Pallas kernels: 7.36 us -> 7.99 us  [the longest x1 5.29 us: shards(): pl.pallas_call(functools.partial(fold_kernel, seqs), out_shape=(jax.Shape...]
  transfers between devices with their start and end apart: 15 -> 15, of which waited for: 4 -> 4; matrix products, arithmetic and copies ran while one was open for 0% -> 0% of each run, Pallas kernels for 20% -> 17%
where the time goes in v3:
time: 41.6 us; the launch traced here: 41.3 us
  Pallas kernels  15.1 us (36%)
  waiting for transfers between devices  13 us (31%)
  starting transfers between devices  12.4 us (30%)
  between operations  0.72 us (2%)
    ppermute x15, waiting for transfers between devices, swap(): return lax.ppermute(block, 'row', [(n, n ^ shift) for n in range(devs)])  13 us
    ppermute x15, starting transfers between devices, swap(): return lax.ppermute(block, 'row', [(n, n ^ shift) for n in range(devs)])  12.4 us
    pallas_call x1, Pallas kernels, shards(): pl.pallas_call(functools.partial(main_kernel, seqs, heads, shifts), out_s...  6.72 us
    pallas_call x1, Pallas kernels, shards(): pl.pallas_call(functools.partial(fold_kernel, seqs), out_shape=(jax.Shape...  5.29 us
    pallas_call x1, Pallas kernels, shards(): pl.pallas_call(pack_kernel, out_shape=(jax.ShapeDtypeStruct((half + 1, to...  1.46 us
    pallas_call x1, Pallas kernels, shards(): pl.pallas_call(functools.partial(gate_kernel, seqs, heads), out_shape=(ja...  1.25 us
  transfers between devices with their start and end apart: 15, of which 4 were waited for; matrix products, arithmetic and copies ran while one was open for 0% of the time, Pallas kernels for 17%

profile of v3, /device:TPU:0, one launch (start us, length us, event | category | flops | bytes accessed | tf_op | source)
XLA Modules:
  0.0 41.3 jit_solution(3579163279291773243)
XLA Ops:
  0.6 1.5 %pack.1 = (bf16[33,16,128]{2,1,0:T(8,128)(2,1)S(1)}, bf16[32,64]{1,0:T(8,128)(2,1)S(1)}) custom-call(bf16[64,16,64]{2,1,0:T(8,128)(2,1)} %refs_16_.1, s32[16,64]{1,0:T(8,128)} %bitcast.8, f32[1,64]{1,0:T(1,128)} %bitcast.11, s32[1,256]{1,0:T(1,128)} %bitcast.10, bf16[32,64]{1,0:T(8,128)(2,1)} %bitcast.9), custom_call_target="tpu_custom_call" | custom-call | tf_op jit(solution)/shard_map/pack/pallas_call | solution.py:403
  2.1 5.1 %collective-permute-start.11 = (bf16[33,16,128]{2,1,0:T(8,128)(2,1)S(1)}, bf16[33,16,128]{2,1,0:T(8,128)(2,1)S(1)}, u32[]{:S(2)}, u32[]{:S(2)}) collective-permute-start(bf16[33,16,128]{2,1,0:T(8,128)(2,1)S(1)} %get-tuple-element.10.pack_ref.refs_0_), channel_id=1, source_target_pairs={{0,12},{1,13},{2,14},{3,15},{4,8},{5,9},{6,10},{7,11},{8,4},{9,5},... | collective-permute-start | bytes 405512 | tf_op jit(solution)/shard_map/ppermute | solution.py:417
  7.2 0.0 collective-permute-start.7
  7.2 0.6 %collective-permute-start.3 = (bf16[33,16,128]{2,1,0:T(8,128)(2,1)S(1)}, bf16[33,16,128]{2,1,0:T(8,128)(2,1)S(1)}, u32[]{:S(2)}, u32[]{:S(2)}) collective-permute-start(bf16[33,16,128]{2,1,0:T(8,128)(2,1)S(1)} %get-tuple-element.10.pack_ref.refs_0_), channel_id=1, source_target_pairs={{0,4},{1,5},{2,6},{3,7},{4,0},{5,1},{6,2},{7,3},{8,12},{9,13},{10,... | collective-permute-start | bytes 405512 | tf_op jit(solution)/shard_map/ppermute | solution.py:417
  7.9 1.7 %collective-permute-start.1 = (bf16[33,16,128]{2,1,0:T(8,128)(2,1)S(1)}, bf16[33,16,128]{2,1,0:T(8,128)(2,1)S(1)}, u32[]{:S(2)}, u32[]{:S(2)}) collective-permute-start(bf16[33,16,128]{2,1,0:T(8,128)(2,1)S(1)} %get-tuple-element.10.pack_ref.refs_0_), channel_id=1, source_target_pairs={{0,2},{1,3},{2,0},{3,1},{4,6},{5,7},{6,4},{7,5},{8,10},{9,11},{10,... | collective-permute-start | bytes 405512 | tf_op jit(solution)/shard_map/ppermute | solution.py:417
  9.5 0.0 collective-permute-start
  9.6 2.2 %collective-permute-done.11.refs_12_ = bf16[33,16,128]{2,1,0:T(8,128)(2,1)S(1)} collective-permute-done((bf16[33,16,128]{2,1,0:T(8,128)(2,1)S(1)}, bf16[33,16,128]{2,1,0:T(8,128)(2,1)S(1)}, u32[]{:S(2)}, u32[]{:S(2)}) %collective-permute-start.11) | collective-permute-done | bytes 135200 | tf_op jit(solution)/shard_map/ppermute | solution.py:417
  11.8 1.7 %collective-permute-start.13 = (bf16[33,16,128]{2,1,0:T(8,128)(2,1)S(1)}, bf16[33,16,128]{2,1,0:T(8,128)(2,1)S(1)}, u32[]{:S(2)}, u32[]{:S(2)}) collective-permute-start(bf16[33,16,128]{2,1,0:T(8,128)(2,1)S(1)} %collective-permute-done.11.refs_12_), channel_id=1, source_target_pairs={{0,2},{1,3},{2,0},{3,1},{4,6},{5,7},{6,4},{7,5},{8,10},{9,11},{10,... | collective-permute-start | bytes 405512 | tf_op jit(solution)/shard_map/ppermute | solution.py:417
  13.5 5.2 %collective-permute-done.7.refs_8_ = bf16[33,16,128]{2,1,0:T(8,128)(2,1)S(1)} collective-permute-done((bf16[33,16,128]{2,1,0:T(8,128)(2,1)S(1)}, bf16[33,16,128]{2,1,0:T(8,128)(2,1)S(1)}, u32[]{:S(2)}, u32[]{:S(2)}) %collective-permute-start.7) | collective-permute-done | bytes 135200 | tf_op jit(solution)/shard_map/ppermute | solution.py:417
  18.7 0.0 collective-permute-start.12
  18.7 0.0 collective-permute-done.3.refs_4_
  18.7 1.5 %collective-permute-start.9 = (bf16[33,16,128]{2,1,0:T(8,128)(2,1)S(1)}, bf16[33,16,128]{2,1,0:T(8,128)(2,1)S(1)}, u32[]{:S(2)}, u32[]{:S(2)}) collective-permute-start(bf16[33,16,128]{2,1,0:T(8,128)(2,1)S(1)} %collective-permute-done.7.refs_8_), channel_id=1, source_target_pairs={{0,2},{1,3},{2,0},{3,1},{4,6},{5,7},{6,4},{7,5},{8,10},{9,11},{10,... | collective-permute-start | bytes 405512 | tf_op jit(solution)/shard_map/ppermute | solution.py:417
  20.2 0.0 collective-permute-done.1.refs_2_
  20.2 0.2 collective-permute-start.8
  20.4 0.0 collective-permute-done.refs_1_
  20.4 0.5 %collective-permute-start.5 = (bf16[33,16,128]{2,1,0:T(8,128)(2,1)S(1)}, bf16[33,16,128]{2,1,0:T(8,128)(2,1)S(1)}, u32[]{:S(2)}, u32[]{:S(2)}) collective-permute-start(bf16[33,16,128]{2,1,0:T(8,128)(2,1)S(1)} %collective-permute-done.3.refs_4_), channel_id=1, source_target_pairs={{0,2},{1,3},{2,0},{3,1},{4,6},{5,7},{6,4},{7,5},{8,10},{9,11},{10,... | collective-permute-start | bytes 405512 | tf_op jit(solution)/shard_map/ppermute | solution.py:417
  20.9 0.0 collective-permute-done.13.refs_14_
  20.9 0.0 collective-permute-start.4
  20.9 0.0 collective-permute-done.12.refs_13_
  20.9 0.5 %collective-permute-start.2 = (bf16[33,16,128]{2,1,0:T(8,128)(2,1)S(1)}, bf16[33,16,128]{2,1,0:T(8,128)(2,1)S(1)}, u32[]{:S(2)}, u32[]{:S(2)}) collective-permute-start(bf16[33,16,128]{2,1,0:T(8,128)(2,1)S(1)} %collective-permute-done.1.refs_2_), channel_id=1, source_target_pairs={{0,1},{1,0},{2,3},{3,2},{4,5},{5,4},{6,7},{7,6},{8,9},{9,8},{10,11... | collective-permute-start | bytes 405512 | tf_op jit(solution)/shard_map/ppermute | solution.py:417
  21.5 3.7 %collective-permute-done.9.refs_10_ = bf16[33,16,128]{2,1,0:T(8,128)(2,1)S(1)} collective-permute-done((bf16[33,16,128]{2,1,0:T(8,128)(2,1)S(1)}, bf16[33,16,128]{2,1,0:T(8,128)(2,1)S(1)}, u32[]{:S(2)}, u32[]{:S(2)}) %collective-permute-start.9) | collective-permute-done | bytes 135200 | tf_op jit(solution)/shard_map/ppermute | solution.py:417
  25.1 0.0 collective-permute-start.14
  25.1 0.0 collective-permute-done.8.refs_9_
  25.1 0.5 %collective-permute-start.10 = (bf16[33,16,128]{2,1,0:T(8,128)(2,1)S(1)}, bf16[33,16,128]{2,1,0:T(8,128)(2,1)S(1)}, u32[]{:S(2)}, u32[]{:S(2)}) collective-permute-start(bf16[33,16,128]{2,1,0:T(8,128)(2,1)S(1)} %collective-permute-done.9.refs_10_), channel_id=1, source_target_pairs={{0,1},{1,0},{2,3},{3,2},{4,5},{5,4},{6,7},{7,6},{8,9},{9,8},{10,11... | collective-permute-start | bytes 405512 | tf_op jit(solution)/shard_map/ppermute | solution.py:417
  25.6 1.9 %collective-permute-done.5.refs_6_ = bf16[33,16,128]{2,1,0:T(8,128)(2,1)S(1)} collective-permute-done((bf16[33,16,128]{2,1,0:T(8,128)(2,1)S(1)}, bf16[33,16,128]{2,1,0:T(8,128)(2,1)S(1)}, u32[]{:S(2)}, u32[]{:S(2)}) %collective-permute-start.5) | collective-permute-done | bytes 135200 | tf_op jit(solution)/shard_map/ppermute | solution.py:417
  27.6 0.0 collective-permute-start.6
  27.6 5.3 %fold.1 = (bf16[16,128,2048]{2,1,0:T(8,128)(2,1)S(1)}, bf16[16,256,128]{2,1,0:T(8,128)(2,1)S(1)}) custom-call(bf16[33,16,128]{2,1,0:T(8,128)(2,1)S(1)} %get-tuple-element.10.pack_ref.refs_0_, bf16[32,64]{1,0:T(8,128)(2,1)S(1)} %get-tuple-element.11.former_ref, bf16[1024,128]{1,0:T(8,128)(2,1)} %outer_hbm.1, bf16[16,256,128]{2,1,0:T(8,128)(2,1)} %state_hbm.1), custom_call_target="tpu_custom_call" | custom-call | flops 1000000000 | bytes 10000000 | tf_op jit(solution)/shard_map/fold/pallas_call | solution.py:428
  32.9 0.4 turn.1.refs_19_
  33.2 1.2 %gate.1 = (f32[4,512,128]{2,1,0:T(8,128)S(1)}, bf16[256,512]{1,0:T(8,128)(2,1)S(1)}, bf16[4,256,128]{2,1,0:T(8,128)(2,1)S(1)}, bf16[4,128,128]{2,1,0:T(8,128)(2,1)S(1)}) custom-call(bf16[33,16,128]{2,1,0:T(8,128)(2,1)S(1)} %get-tuple-element.10.pack_ref.refs_0_, bf16[32,64]{1,0:T(8,128)(2,1)} %bitcast.13, bf16[64,256]{1,0:T(8,128)(2,1)} %content_hbm.1, ...), custom_call_target="tpu_custom_call" | custom-call | flops 100000000 | bytes 1000000 | tf_op jit(solution)/shard_map/gate/pallas_call | solution.py:454
  34.5 0.0 collective-permute-done.4.refs_5_
  34.5 0.0 collective-permute-done.2.refs_3_
  34.5 0.0 collective-permute-done.14.refs_15_
  34.5 0.0 collective-permute-done.10.refs_11_
  34.5 0.0 collective-permute-done.6.refs_7_
  34.6 6.7 %main.1 = (bf16[64,16,64]{2,1,0:T(8,128)(2,1)}, bf16[16,256,128]{2,1,0:T(8,128)(2,1)}) custom-call(bf16[33,16,128]{2,1,0:T(8,128)(2,1)S(1)} %get-tuple-element.10.pack_ref.refs_0_, bf16[33,16,128]{2,1,0:T(8,128)(2,1)S(1)} %collective-permute-done.refs_1_, bf16[33,16,128]{2,1,0:T(8,128)(2,1)S(1)} %collective-permute-done.1.refs_2_, ...), custom_call_target="tpu_custom_call" | custom-call | flops 4000000000 | bytes 10000000 | tf_op jit(solution)/shard_map/main/pallas_call | solution.py:482
Async XLA Ops:
  2.1 9.7 %collective-permute-start.11 = (bf16[33,16,128]{2,1,0:T(8,128)(2,1)S(1)}, bf16[33,16,128]{2,1,0:T(8,128)(2,1)S(1)}, u32[]{:S(2)}, u32[]{:S(2)}) collective-permute-start(bf16[33,16,128]{2,1,0:T(8,128)(2,1)S(1)} %get-tuple-element.10.pack_ref.refs_0_), channel_id=1, source_target_pairs={{0,12},{1,13},{2,14},{3,15},{4,8},{5,9},{6,10},{7,11},{8,4},{9,5},... | collective-permute-start | bytes 405512 | tf_op jit(solution)/shard_map/ppermute | solution.py:417
  7.2 11.4 %collective-permute-start.7 = (bf16[33,16,128]{2,1,0:T(8,128)(2,1)S(1)}, bf16[33,16,128]{2,1,0:T(8,128)(2,1)S(1)}, u32[]{:S(2)}, u32[]{:S(2)}) collective-permute-start(bf16[33,16,128]{2,1,0:T(8,128)(2,1)S(1)} %get-tuple-element.10.pack_ref.refs_0_), channel_id=1, source_target_pairs={{0,8},{1,9},{2,10},{3,11},{4,12},{5,13},{6,14},{7,15},{8,0},{9,1},... | collective-permute-start | bytes 405512 | tf_op jit(solution)/shard_map/ppermute | solution.py:417
  7.2 11.4 %collective-permute-start.3 = (bf16[33,16,128]{2,1,0:T(8,128)(2,1)S(1)}, bf16[33,16,128]{2,1,0:T(8,128)(2,1)S(1)}, u32[]{:S(2)}, u32[]{:S(2)}) collective-permute-start(bf16[33,16,128]{2,1,0:T(8,128)(2,1)S(1)} %get-tuple-element.10.pack_ref.refs_0_), channel_id=1, source_target_pairs={{0,4},{1,5},{2,6},{3,7},{4,0},{5,1},{6,2},{7,3},{8,12},{9,13},{10,... | collective-permute-start | bytes 405512 | tf_op jit(solution)/shard_map/ppermute | solution.py:417
  7.9 12.3 %collective-permute-start.1 = (bf16[33,16,128]{2,1,0:T(8,128)(2,1)S(1)}, bf16[33,16,128]{2,1,0:T(8,128)(2,1)S(1)}, u32[]{:S(2)}, u32[]{:S(2)}) collective-permute-start(bf16[33,16,128]{2,1,0:T(8,128)(2,1)S(1)} %get-tuple-element.10.pack_ref.refs_0_), channel_id=1, source_target_pairs={{0,2},{1,3},{2,0},{3,1},{4,6},{5,7},{6,4},{7,5},{8,10},{9,11},{10,... | collective-permute-start | bytes 405512 | tf_op jit(solution)/shard_map/ppermute | solution.py:417
  9.5 10.9 %collective-permute-start = (bf16[33,16,128]{2,1,0:T(8,128)(2,1)S(1)}, bf16[33,16,128]{2,1,0:T(8,128)(2,1)S(1)}, u32[]{:S(2)}, u32[]{:S(2)}) collective-permute-start(bf16[33,16,128]{2,1,0:T(8,128)(2,1)S(1)} %get-tuple-element.10.pack_ref.refs_0_), channel_id=1, source_target_pairs={{0,1},{1,0},{2,3},{3,2},{4,5},{5,4},{6,7},{7,6},{8,9},{9,8},{10,11... | collective-permute-start | bytes 405512 | tf_op jit(solution)/shard_map/ppermute | solution.py:417
  11.8 9.2 %collective-permute-start.13 = (bf16[33,16,128]{2,1,0:T(8,128)(2,1)S(1)}, bf16[33,16,128]{2,1,0:T(8,128)(2,1)S(1)}, u32[]{:S(2)}, u32[]{:S(2)}) collective-permute-start(bf16[33,16,128]{2,1,0:T(8,128)(2,1)S(1)} %collective-permute-done.11.refs_12_), channel_id=1, source_target_pairs={{0,2},{1,3},{2,0},{3,1},{4,6},{5,7},{6,4},{7,5},{8,10},{9,11},{10,... | collective-permute-start | bytes 405512 | tf_op jit(solution)/shard_map/ppermute | solution.py:417
  18.7 2.3 %collective-permute-start.12 = (bf16[33,16,128]{2,1,0:T(8,128)(2,1)S(1)}, bf16[33,16,128]{2,1,0:T(8,128)(2,1)S(1)}, u32[]{:S(2)}, u32[]{:S(2)}) collective-permute-start(bf16[33,16,128]{2,1,0:T(8,128)(2,1)S(1)} %collective-permute-done.11.refs_12_), channel_id=1, source_target_pairs={{0,1},{1,0},{2,3},{3,2},{4,5},{5,4},{6,7},{7,6},{8,9},{9,8},{10,11... | collective-permute-start | bytes 405512 | tf_op jit(solution)/shard_map/ppermute | solution.py:417
  18.7 6.5 %collective-permute-start.9 = (bf16[33,16,128]{2,1,0:T(8,128)(2,1)S(1)}, bf16[33,16,128]{2,1,0:T(8,128)(2,1)S(1)}, u32[]{:S(2)}, u32[]{:S(2)}) collective-permute-start(bf16[33,16,128]{2,1,0:T(8,128)(2,1)S(1)} %collective-permute-done.7.refs_8_), channel_id=1, source_target_pairs={{0,2},{1,3},{2,0},{3,1},{4,6},{5,7},{6,4},{7,5},{8,10},{9,11},{10,... | collective-permute-start | bytes 405512 | tf_op jit(solution)/shard_map/ppermute | solution.py:417
  20.2 4.9 %collective-permute-start.8 = (bf16[33,16,128]{2,1,0:T(8,128)(2,1)S(1)}, bf16[33,16,128]{2,1,0:T(8,128)(2,1)S(1)}, u32[]{:S(2)}, u32[]{:S(2)}) collective-permute-start(bf16[33,16,128]{2,1,0:T(8,128)(2,1)S(1)} %collective-permute-done.7.refs_8_), channel_id=1, source_target_pairs={{0,1},{1,0},{2,3},{3,2},{4,5},{5,4},{6,7},{7,6},{8,9},{9,8},{10,11... | collective-permute-start | bytes 405512 | tf_op jit(solution)/shard_map/ppermute | solution.py:417
  20.4 7.1 %collective-permute-start.5 = (bf16[33,16,128]{2,1,0:T(8,128)(2,1)S(1)}, bf16[33,16,128]{2,1,0:T(8,128)(2,1)S(1)}, u32[]{:S(2)}, u32[]{:S(2)}) collective-permute-start(bf16[33,16,128]{2,1,0:T(8,128)(2,1)S(1)} %collective-permute-done.3.refs_4_), channel_id=1, source_target_pairs={{0,2},{1,3},{2,0},{3,1},{4,6},{5,7},{6,4},{7,5},{8,10},{9,11},{10,... | collective-permute-start | bytes 405512 | tf_op jit(solution)/shard_map/ppermute | solution.py:417
  20.9 13.6 %collective-permute-start.4 = (bf16[33,16,128]{2,1,0:T(8,128)(2,1)S(1)}, bf16[33,16,128]{2,1,0:T(8,128)(2,1)S(1)}, u32[]{:S(2)}, u32[]{:S(2)}) collective-permute-start(bf16[33,16,128]{2,1,0:T(8,128)(2,1)S(1)} %collective-permute-done.3.refs_4_), channel_id=1, source_target_pairs={{0,1},{1,0},{2,3},{3,2},{4,5},{5,4},{6,7},{7,6},{8,9},{9,8},{10,11... | collective-permute-start | bytes 405512 | tf_op jit(solution)/shard_map/ppermute | solution.py:417
  20.9 13.6 %collective-permute-start.2 = (bf16[33,16,128]{2,1,0:T(8,128)(2,1)S(1)}, bf16[33,16,128]{2,1,0:T(8,128)(2,1)S(1)}, u32[]{:S(2)}, u32[]{:S(2)}) collective-permute-start(bf16[33,16,128]{2,1,0:T(8,128)(2,1)S(1)} %collective-permute-done.1.refs_2_), channel_id=1, source_target_pairs={{0,1},{1,0},{2,3},{3,2},{4,5},{5,4},{6,7},{7,6},{8,9},{9,8},{10,11... | collective-permute-start | bytes 405512 | tf_op jit(solution)/shard_map/ppermute | solution.py:417
  25.1 9.4 %collective-permute-start.14 = (bf16[33,16,128]{2,1,0:T(8,128)(2,1)S(1)}, bf16[33,16,128]{2,1,0:T(8,128)(2,1)S(1)}, u32[]{:S(2)}, u32[]{:S(2)}) collective-permute-start(bf16[33,16,128]{2,1,0:T(8,128)(2,1)S(1)} %collective-permute-done.13.refs_14_), channel_id=1, source_target_pairs={{0,1},{1,0},{2,3},{3,2},{4,5},{5,4},{6,7},{7,6},{8,9},{9,8},{10,11... | collective-permute-start | bytes 405512 | tf_op jit(solution)/shard_map/ppermute | solution.py:417
  25.1 9.4 %collective-permute-start.10 = (bf16[33,16,128]{2,1,0:T(8,128)(2,1)S(1)}, bf16[33,16,128]{2,1,0:T(8,128)(2,1)S(1)}, u32[]{:S(2)}, u32[]{:S(2)}) collective-permute-start(bf16[33,16,128]{2,1,0:T(8,128)(2,1)S(1)} %collective-permute-done.9.refs_10_), channel_id=1, source_target_pairs={{0,1},{1,0},{2,3},{3,2},{4,5},{5,4},{6,7},{7,6},{8,9},{9,8},{10,11... | collective-permute-start | bytes 405512 | tf_op jit(solution)/shard_map/ppermute | solution.py:417
  27.6 7.0 %collective-permute-start.6 = (bf16[33,16,128]{2,1,0:T(8,128)(2,1)S(1)}, bf16[33,16,128]{2,1,0:T(8,128)(2,1)S(1)}, u32[]{:S(2)}, u32[]{:S(2)}) collective-permute-start(bf16[33,16,128]{2,1,0:T(8,128)(2,1)S(1)} %collective-permute-done.5.refs_6_), channel_id=1, source_target_pairs={{0,1},{1,0},{2,3},{3,2},{4,5},{5,4},{6,7},{7,6},{8,9},{9,8},{10,11... | collective-permute-start | bytes 405512 | tf_op jit(solution)/shard_map/ppermute | solution.py:417

commit v4 on v3

--- a/solution.py
+++ b/solution.py
@@ -238,11 +238,12 @@
         right_ref,
         value_ref,
         result_ref,
-        out_ref,
+        out_hbm,
         pair_hbm,
         rows_ref,
         weight_ref,
         gain_ref,
+        out_ref,
         pair_ref,
         mask_scr,
         rhs_scr,
@@ -349,12 +350,21 @@
     width = rows_ref.shape[2]
     total = total.reshape(outer, 4, toks, lanes)
     base = rows_ref[...].astype(F32).reshape(outer, 2, 4, toks, width)
-    for s2 in range(2):
-        piece = base[:, s2] + total[..., s2 * width : (s2 + 1) * width]
-        for so in range(outer):
-            out_ref[so * 8 + s2 * 4 : so * 8 + s2 * 4 + 4] = piece[so].astype(BF16)
+    stores = []
+    for so in range(outer):
+        for s2 in range(2):
+            piece = base[so, s2] + total[so, ..., s2 * width : (s2 + 1) * width]
+            out_ref[so * 8 + s2 * 4 : so * 8 + s2 * 4 + 4] = piece.astype(BF16)
+        if so % 2:
+            here = pl.ds(so // 2 * 16, 16)
+            stores.append(
+                pltpu.make_async_copy(out_ref.at[here], out_hbm.at[here], sems.at[3 + so // 2])
+            )
+            stores[-1].start()
     for i in range(toks):
         pltpu.make_async_copy(pair_ref.at[i], pair_hbm.at[i], pair_sem.at[i]).wait()
+    for store in stores:
+        store.wait()
 
 
 def far_order(devs):
@@ -385,7 +395,7 @@
     factor = former_factor_proj.shape[1]
     channels = outer_output_weight.shape[1]
     lanes = 2 * width
-    half = seqs // 2
+    half, outer = seqs // 2, seqs // 8
     params = pltpu.CompilerParams(vmem_limit_bytes=28 << 20)
 
     def keep(*arrays):
@@ -486,8 +496,8 @@
             jax.ShapeDtypeStruct(pair_state_tiles.shape, BF16),
         ),
         in_specs=[VM] * devs + [HB] * 3 + [VM] * 6,
-        out_specs=(VM, HB),
-        scratch_shapes=room(*arrays)
+        out_specs=(HB, HB),
+        scratch_shapes=room(*arrays, homolog_embedding)
         + [
             pltpu.VMEM(pair_state_tiles.shape, BF16),
             pltpu.VMEM((seqs + 8, tokens), F32),
@@ -496,7 +506,7 @@
             pltpu.VMEM((half, heads * toks, lanes), BF16),
             pltpu.VMEM((group * channels, tokens), F32),
             pltpu.VMEM((group * channels, tokens), F32),
-            pltpu.SemaphoreType.DMA((3,)),
+            pltpu.SemaphoreType.DMA((3 + outer // 2,)),
             pltpu.SemaphoreType.DMA((toks,)),
         ],
         compiler_params=params,

time: 41.6 us -> 40.8 us (0.981)
  Pallas kernels: 15.1 us -> 14.3 us
    pallas_call x1, Pallas kernels: 6.72 us -> 5.95 us  [shards(): pl.pallas_call(functools.partial(main_kernel, seqs, heads, shifts), out_s...]
where the time goes in v4:
time: 40.8 us; the launch traced here: 40.5 us
  Pallas kernels  14.3 us (35%)
  waiting for transfers between devices  13 us (32%)
  starting transfers between devices  12.4 us (30%)
  between operations  0.72 us (2%)
    ppermute x15, waiting for transfers between devices, swap(): return lax.ppermute(block, 'row', [(n, n ^ shift) for n in range(devs)])  13 us
    ppermute x15, starting transfers between devices, swap(): return lax.ppermute(block, 'row', [(n, n ^ shift) for n in range(devs)])  12.4 us
    pallas_call x1, Pallas kernels, shards(): pl.pallas_call(functools.partial(main_kernel, seqs, heads, shifts), out_s...  5.95 us
    pallas_call x1, Pallas kernels, shards(): pl.pallas_call(functools.partial(fold_kernel, seqs), out_shape=(jax.Shape...  5.29 us
    pallas_call x1, Pallas kernels, shards(): pl.pallas_call(pack_kernel, out_shape=(jax.ShapeDtypeStruct((half + 1, to...  1.46 us
    pallas_call x1, Pallas kernels, shards(): pl.pallas_call(functools.partial(gate_kernel, seqs, heads), out_shape=(ja...  1.25 us
  transfers between devices with their start and end apart: 15, of which 4 were waited for; matrix products, arithmetic and copies ran while one was open for 0% of the time, Pallas kernels for 17%

profile of v4, /device:TPU:0, one launch (start us, length us, event | category | flops | bytes accessed | tf_op | source)
XLA Modules:
  0.0 40.5 jit_solution(13244307727856262039)
XLA Ops:
  0.6 1.5 %pack.1 = (bf16[33,16,128]{2,1,0:T(8,128)(2,1)S(1)}, bf16[32,64]{1,0:T(8,128)(2,1)S(1)}) custom-call(bf16[64,16,64]{2,1,0:T(8,128)(2,1)} %refs_16_.1, s32[16,64]{1,0:T(8,128)} %bitcast.8, f32[1,64]{1,0:T(1,128)} %bitcast.11, s32[1,256]{1,0:T(1,128)} %bitcast.10, bf16[32,64]{1,0:T(8,128)(2,1)} %bitcast.9), custom_call_target="tpu_custom_call" | custom-call | tf_op jit(solution)/shard_map/pack/pallas_call | solution.py:413
  2.1 5.1 %collective-permute-start.11 = (bf16[33,16,128]{2,1,0:T(8,128)(2,1)S(1)}, bf16[33,16,128]{2,1,0:T(8,128)(2,1)S(1)}, u32[]{:S(2)}, u32[]{:S(2)}) collective-permute-start(bf16[33,16,128]{2,1,0:T(8,128)(2,1)S(1)} %get-tuple-element.10.pack_ref.refs_0_), channel_id=1, source_target_pairs={{0,12},{1,13},{2,14},{3,15},{4,8},{5,9},{6,10},{7,11},{8,4},{9,5},... | collective-permute-start | bytes 405512 | tf_op jit(solution)/shard_map/ppermute | solution.py:427
  7.2 0.0 collective-permute-start.7
  7.2 0.6 %collective-permute-start.3 = (bf16[33,16,128]{2,1,0:T(8,128)(2,1)S(1)}, bf16[33,16,128]{2,1,0:T(8,128)(2,1)S(1)}, u32[]{:S(2)}, u32[]{:S(2)}) collective-permute-start(bf16[33,16,128]{2,1,0:T(8,128)(2,1)S(1)} %get-tuple-element.10.pack_ref.refs_0_), channel_id=1, source_target_pairs={{0,4},{1,5},{2,6},{3,7},{4,0},{5,1},{6,2},{7,3},{8,12},{9,13},{10,... | collective-permute-start | bytes 405512 | tf_op jit(solution)/shard_map/ppermute | solution.py:427
  7.9 1.7 %collective-permute-start.1 = (bf16[33,16,128]{2,1,0:T(8,128)(2,1)S(1)}, bf16[33,16,128]{2,1,0:T(8,128)(2,1)S(1)}, u32[]{:S(2)}, u32[]{:S(2)}) collective-permute-start(bf16[33,16,128]{2,1,0:T(8,128)(2,1)S(1)} %get-tuple-element.10.pack_ref.refs_0_), channel_id=1, source_target_pairs={{0,2},{1,3},{2,0},{3,1},{4,6},{5,7},{6,4},{7,5},{8,10},{9,11},{10,... | collective-permute-start | bytes 405512 | tf_op jit(solution)/shard_map/ppermute | solution.py:427
  9.5 0.0 collective-permute-start
  9.6 2.2 %collective-permute-done.11.refs_12_ = bf16[33,16,128]{2,1,0:T(8,128)(2,1)S(1)} collective-permute-done((bf16[33,16,128]{2,1,0:T(8,128)(2,1)S(1)}, bf16[33,16,128]{2,1,0:T(8,128)(2,1)S(1)}, u32[]{:S(2)}, u32[]{:S(2)}) %collective-permute-start.11) | collective-permute-done | bytes 135200 | tf_op jit(solution)/shard_map/ppermute | solution.py:427
  11.8 1.7 %collective-permute-start.13 = (bf16[33,16,128]{2,1,0:T(8,128)(2,1)S(1)}, bf16[33,16,128]{2,1,0:T(8,128)(2,1)S(1)}, u32[]{:S(2)}, u32[]{:S(2)}) collective-permute-start(bf16[33,16,128]{2,1,0:T(8,128)(2,1)S(1)} %collective-permute-done.11.refs_12_), channel_id=1, source_target_pairs={{0,2},{1,3},{2,0},{3,1},{4,6},{5,7},{6,4},{7,5},{8,10},{9,11},{10,... | collective-permute-start | bytes 405512 | tf_op jit(solution)/shard_map/ppermute | solution.py:427
  13.5 5.2 %collective-permute-done.7.refs_8_ = bf16[33,16,128]{2,1,0:T(8,128)(2,1)S(1)} collective-permute-done((bf16[33,16,128]{2,1,0:T(8,128)(2,1)S(1)}, bf16[33,16,128]{2,1,0:T(8,128)(2,1)S(1)}, u32[]{:S(2)}, u32[]{:S(2)}) %collective-permute-start.7) | collective-permute-done | bytes 135200 | tf_op jit(solution)/shard_map/ppermute | solution.py:427
  18.7 0.0 collective-permute-start.12
  18.7 0.0 collective-permute-done.3.refs_4_
  18.7 1.5 %collective-permute-start.9 = (bf16[33,16,128]{2,1,0:T(8,128)(2,1)S(1)}, bf16[33,16,128]{2,1,0:T(8,128)(2,1)S(1)}, u32[]{:S(2)}, u32[]{:S(2)}) collective-permute-start(bf16[33,16,128]{2,1,0:T(8,128)(2,1)S(1)} %collective-permute-done.7.refs_8_), channel_id=1, source_target_pairs={{0,2},{1,3},{2,0},{3,1},{4,6},{5,7},{6,4},{7,5},{8,10},{9,11},{10,... | collective-permute-start | bytes 405512 | tf_op jit(solution)/shard_map/ppermute | solution.py:427
  20.2 0.0 collective-permute-done.1.refs_2_
  20.2 0.2 collective-permute-start.8
  20.4 0.0 collective-permute-done.refs_1_
  20.4 0.5 %collective-permute-start.5 = (bf16[33,16,128]{2,1,0:T(8,128)(2,1)S(1)}, bf16[33,16,128]{2,1,0:T(8,128)(2,1)S(1)}, u32[]{:S(2)}, u32[]{:S(2)}) collective-permute-start(bf16[33,16,128]{2,1,0:T(8,128)(2,1)S(1)} %collective-permute-done.3.refs_4_), channel_id=1, source_target_pairs={{0,2},{1,3},{2,0},{3,1},{4,6},{5,7},{6,4},{7,5},{8,10},{9,11},{10,... | collective-permute-start | bytes 405512 | tf_op jit(solution)/shard_map/ppermute | solution.py:427
  20.9 0.0 collective-permute-done.13.refs_14_
  20.9 0.0 collective-permute-start.4
  20.9 0.0 collective-permute-done.12.refs_13_
  20.9 0.5 %collective-permute-start.2 = (bf16[33,16,128]{2,1,0:T(8,128)(2,1)S(1)}, bf16[33,16,128]{2,1,0:T(8,128)(2,1)S(1)}, u32[]{:S(2)}, u32[]{:S(2)}) collective-permute-start(bf16[33,16,128]{2,1,0:T(8,128)(2,1)S(1)} %collective-permute-done.1.refs_2_), channel_id=1, source_target_pairs={{0,1},{1,0},{2,3},{3,2},{4,5},{5,4},{6,7},{7,6},{8,9},{9,8},{10,11... | collective-permute-start | bytes 405512 | tf_op jit(solution)/shard_map/ppermute | solution.py:427
  21.5 3.7 %collective-permute-done.9.refs_10_ = bf16[33,16,128]{2,1,0:T(8,128)(2,1)S(1)} collective-permute-done((bf16[33,16,128]{2,1,0:T(8,128)(2,1)S(1)}, bf16[33,16,128]{2,1,0:T(8,128)(2,1)S(1)}, u32[]{:S(2)}, u32[]{:S(2)}) %collective-permute-start.9) | collective-permute-done | bytes 135200 | tf_op jit(solution)/shard_map/ppermute | solution.py:427
  25.1 0.0 collective-permute-start.14
  25.1 0.0 collective-permute-done.8.refs_9_
  25.1 0.5 %collective-permute-start.10 = (bf16[33,16,128]{2,1,0:T(8,128)(2,1)S(1)}, bf16[33,16,128]{2,1,0:T(8,128)(2,1)S(1)}, u32[]{:S(2)}, u32[]{:S(2)}) collective-permute-start(bf16[33,16,128]{2,1,0:T(8,128)(2,1)S(1)} %collective-permute-done.9.refs_10_), channel_id=1, source_target_pairs={{0,1},{1,0},{2,3},{3,2},{4,5},{5,4},{6,7},{7,6},{8,9},{9,8},{10,11... | collective-permute-start | bytes 405512 | tf_op jit(solution)/shard_map/ppermute | solution.py:427
  25.6 1.9 %collective-permute-done.5.refs_6_ = bf16[33,16,128]{2,1,0:T(8,128)(2,1)S(1)} collective-permute-done((bf16[33,16,128]{2,1,0:T(8,128)(2,1)S(1)}, bf16[33,16,128]{2,1,0:T(8,128)(2,1)S(1)}, u32[]{:S(2)}, u32[]{:S(2)}) %collective-permute-start.5) | collective-permute-done | bytes 135200 | tf_op jit(solution)/shard_map/ppermute | solution.py:427
  27.6 0.0 collective-permute-start.6
  27.6 5.3 %fold.1 = (bf16[16,128,2048]{2,1,0:T(8,128)(2,1)S(1)}, bf16[16,256,128]{2,1,0:T(8,128)(2,1)S(1)}) custom-call(bf16[33,16,128]{2,1,0:T(8,128)(2,1)S(1)} %get-tuple-element.10.pack_ref.refs_0_, bf16[32,64]{1,0:T(8,128)(2,1)S(1)} %get-tuple-element.11.former_ref, bf16[1024,128]{1,0:T(8,128)(2,1)} %outer_hbm.1, bf16[16,256,128]{2,1,0:T(8,128)(2,1)} %state_hbm.1), custom_call_target="tpu_custom_call" | custom-call | flops 1000000000 | bytes 10000000 | tf_op jit(solution)/shard_map/fold/pallas_call | solution.py:438
  32.9 0.4 turn.1.refs_19_
  33.2 1.2 %gate.1 = (f32[4,512,128]{2,1,0:T(8,128)S(1)}, bf16[256,512]{1,0:T(8,128)(2,1)S(1)}, bf16[4,256,128]{2,1,0:T(8,128)(2,1)S(1)}, bf16[4,128,128]{2,1,0:T(8,128)(2,1)S(1)}) custom-call(bf16[33,16,128]{2,1,0:T(8,128)(2,1)S(1)} %get-tuple-element.10.pack_ref.refs_0_, bf16[32,64]{1,0:T(8,128)(2,1)} %bitcast.13, bf16[64,256]{1,0:T(8,128)(2,1)} %content_hbm.1, ...), custom_call_target="tpu_custom_call" | custom-call | flops 100000000 | bytes 1000000 | tf_op jit(solution)/shard_map/gate/pallas_call | solution.py:464
  34.5 0.0 collective-permute-done.4.refs_5_
  34.5 0.0 collective-permute-done.2.refs_3_
  34.5 0.0 collective-permute-done.14.refs_15_
  34.5 0.0 collective-permute-done.10.refs_11_
  34.5 0.0 collective-permute-done.6.refs_7_
  34.6 6.0 %main.1 = (bf16[64,16,64]{2,1,0:T(8,128)(2,1)}, bf16[16,256,128]{2,1,0:T(8,128)(2,1)}) custom-call(bf16[33,16,128]{2,1,0:T(8,128)(2,1)S(1)} %get-tuple-element.10.pack_ref.refs_0_, bf16[33,16,128]{2,1,0:T(8,128)(2,1)S(1)} %collective-permute-done.refs_1_, bf16[33,16,128]{2,1,0:T(8,128)(2,1)S(1)} %collective-permute-done.1.refs_2_, ...), custom_call_target="tpu_custom_call" | custom-call | flops 4000000000 | bytes 10000000 | tf_op jit(solution)/shard_map/main/pallas_call | solution.py:492
Async XLA Ops:
  2.1 9.7 %collective-permute-start.11 = (bf16[33,16,128]{2,1,0:T(8,128)(2,1)S(1)}, bf16[33,16,128]{2,1,0:T(8,128)(2,1)S(1)}, u32[]{:S(2)}, u32[]{:S(2)}) collective-permute-start(bf16[33,16,128]{2,1,0:T(8,128)(2,1)S(1)} %get-tuple-element.10.pack_ref.refs_0_), channel_id=1, source_target_pairs={{0,12},{1,13},{2,14},{3,15},{4,8},{5,9},{6,10},{7,11},{8,4},{9,5},... | collective-permute-start | bytes 405512 | tf_op jit(solution)/shard_map/ppermute | solution.py:427
  7.2 11.4 %collective-permute-start.7 = (bf16[33,16,128]{2,1,0:T(8,128)(2,1)S(1)}, bf16[33,16,128]{2,1,0:T(8,128)(2,1)S(1)}, u32[]{:S(2)}, u32[]{:S(2)}) collective-permute-start(bf16[33,16,128]{2,1,0:T(8,128)(2,1)S(1)} %get-tuple-element.10.pack_ref.refs_0_), channel_id=1, source_target_pairs={{0,8},{1,9},{2,10},{3,11},{4,12},{5,13},{6,14},{7,15},{8,0},{9,1},... | collective-permute-start | bytes 405512 | tf_op jit(solution)/shard_map/ppermute | solution.py:427
  7.2 11.4 %collective-permute-start.3 = (bf16[33,16,128]{2,1,0:T(8,128)(2,1)S(1)}, bf16[33,16,128]{2,1,0:T(8,128)(2,1)S(1)}, u32[]{:S(2)}, u32[]{:S(2)}) collective-permute-start(bf16[33,16,128]{2,1,0:T(8,128)(2,1)S(1)} %get-tuple-element.10.pack_ref.refs_0_), channel_id=1, source_target_pairs={{0,4},{1,5},{2,6},{3,7},{4,0},{5,1},{6,2},{7,3},{8,12},{9,13},{10,... | collective-permute-start | bytes 405512 | tf_op jit(solution)/shard_map/ppermute | solution.py:427
  7.9 12.3 %collective-permute-start.1 = (bf16[33,16,128]{2,1,0:T(8,128)(2,1)S(1)}, bf16[33,16,128]{2,1,0:T(8,128)(2,1)S(1)}, u32[]{:S(2)}, u32[]{:S(2)}) collective-permute-start(bf16[33,16,128]{2,1,0:T(8,128)(2,1)S(1)} %get-tuple-element.10.pack_ref.refs_0_), channel_id=1, source_target_pairs={{0,2},{1,3},{2,0},{3,1},{4,6},{5,7},{6,4},{7,5},{8,10},{9,11},{10,... | collective-permute-start | bytes 405512 | tf_op jit(solution)/shard_map/ppermute | solution.py:427
  9.5 10.9 %collective-permute-start = (bf16[33,16,128]{2,1,0:T(8,128)(2,1)S(1)}, bf16[33,16,128]{2,1,0:T(8,128)(2,1)S(1)}, u32[]{:S(2)}, u32[]{:S(2)}) collective-permute-start(bf16[33,16,128]{2,1,0:T(8,128)(2,1)S(1)} %get-tuple-element.10.pack_ref.refs_0_), channel_id=1, source_target_pairs={{0,1},{1,0},{2,3},{3,2},{4,5},{5,4},{6,7},{7,6},{8,9},{9,8},{10,11... | collective-permute-start | bytes 405512 | tf_op jit(solution)/shard_map/ppermute | solution.py:427
  11.8 9.2 %collective-permute-start.13 = (bf16[33,16,128]{2,1,0:T(8,128)(2,1)S(1)}, bf16[33,16,128]{2,1,0:T(8,128)(2,1)S(1)}, u32[]{:S(2)}, u32[]{:S(2)}) collective-permute-start(bf16[33,16,128]{2,1,0:T(8,128)(2,1)S(1)} %collective-permute-done.11.refs_12_), channel_id=1, source_target_pairs={{0,2},{1,3},{2,0},{3,1},{4,6},{5,7},{6,4},{7,5},{8,10},{9,11},{10,... | collective-permute-start | bytes 405512 | tf_op jit(solution)/shard_map/ppermute | solution.py:427
  18.7 2.3 %collective-permute-start.12 = (bf16[33,16,128]{2,1,0:T(8,128)(2,1)S(1)}, bf16[33,16,128]{2,1,0:T(8,128)(2,1)S(1)}, u32[]{:S(2)}, u32[]{:S(2)}) collective-permute-start(bf16[33,16,128]{2,1,0:T(8,128)(2,1)S(1)} %collective-permute-done.11.refs_12_), channel_id=1, source_target_pairs={{0,1},{1,0},{2,3},{3,2},{4,5},{5,4},{6,7},{7,6},{8,9},{9,8},{10,11... | collective-permute-start | bytes 405512 | tf_op jit(solution)/shard_map/ppermute | solution.py:427
  18.7 6.5 %collective-permute-start.9 = (bf16[33,16,128]{2,1,0:T(8,128)(2,1)S(1)}, bf16[33,16,128]{2,1,0:T(8,128)(2,1)S(1)}, u32[]{:S(2)}, u32[]{:S(2)}) collective-permute-start(bf16[33,16,128]{2,1,0:T(8,128)(2,1)S(1)} %collective-permute-done.7.refs_8_), channel_id=1, source_target_pairs={{0,2},{1,3},{2,0},{3,1},{4,6},{5,7},{6,4},{7,5},{8,10},{9,11},{10,... | collective-permute-start | bytes 405512 | tf_op jit(solution)/shard_map/ppermute | solution.py:427
  20.2 4.9 %collective-permute-start.8 = (bf16[33,16,128]{2,1,0:T(8,128)(2,1)S(1)}, bf16[33,16,128]{2,1,0:T(8,128)(2,1)S(1)}, u32[]{:S(2)}, u32[]{:S(2)}) collective-permute-start(bf16[33,16,128]{2,1,0:T(8,128)(2,1)S(1)} %collective-permute-done.7.refs_8_), channel_id=1, source_target_pairs={{0,1},{1,0},{2,3},{3,2},{4,5},{5,4},{6,7},{7,6},{8,9},{9,8},{10,11... | collective-permute-start | bytes 405512 | tf_op jit(solution)/shard_map/ppermute | solution.py:427
  20.4 7.1 %collective-permute-start.5 = (bf16[33,16,128]{2,1,0:T(8,128)(2,1)S(1)}, bf16[33,16,128]{2,1,0:T(8,128)(2,1)S(1)}, u32[]{:S(2)}, u32[]{:S(2)}) collective-permute-start(bf16[33,16,128]{2,1,0:T(8,128)(2,1)S(1)} %collective-permute-done.3.refs_4_), channel_id=1, source_target_pairs={{0,2},{1,3},{2,0},{3,1},{4,6},{5,7},{6,4},{7,5},{8,10},{9,11},{10,... | collective-permute-start | bytes 405512 | tf_op jit(solution)/shard_map/ppermute | solution.py:427
  20.9 13.6 %collective-permute-start.4 = (bf16[33,16,128]{2,1,0:T(8,128)(2,1)S(1)}, bf16[33,16,128]{2,1,0:T(8,128)(2,1)S(1)}, u32[]{:S(2)}, u32[]{:S(2)}) collective-permute-start(bf16[33,16,128]{2,1,0:T(8,128)(2,1)S(1)} %collective-permute-done.3.refs_4_), channel_id=1, source_target_pairs={{0,1},{1,0},{2,3},{3,2},{4,5},{5,4},{6,7},{7,6},{8,9},{9,8},{10,11... | collective-permute-start | bytes 405512 | tf_op jit(solution)/shard_map/ppermute | solution.py:427
  20.9 13.6 %collective-permute-start.2 = (bf16[33,16,128]{2,1,0:T(8,128)(2,1)S(1)}, bf16[33,16,128]{2,1,0:T(8,128)(2,1)S(1)}, u32[]{:S(2)}, u32[]{:S(2)}) collective-permute-start(bf16[33,16,128]{2,1,0:T(8,128)(2,1)S(1)} %collective-permute-done.1.refs_2_), channel_id=1, source_target_pairs={{0,1},{1,0},{2,3},{3,2},{4,5},{5,4},{6,7},{7,6},{8,9},{9,8},{10,11... | collective-permute-start | bytes 405512 | tf_op jit(solution)/shard_map/ppermute | solution.py:427
  25.1 9.4 %collective-permute-start.14 = (bf16[33,16,128]{2,1,0:T(8,128)(2,1)S(1)}, bf16[33,16,128]{2,1,0:T(8,128)(2,1)S(1)}, u32[]{:S(2)}, u32[]{:S(2)}) collective-permute-start(bf16[33,16,128]{2,1,0:T(8,128)(2,1)S(1)} %collective-permute-done.13.refs_14_), channel_id=1, source_target_pairs={{0,1},{1,0},{2,3},{3,2},{4,5},{5,4},{6,7},{7,6},{8,9},{9,8},{10,11... | collective-permute-start | bytes 405512 | tf_op jit(solution)/shard_map/ppermute | solution.py:427
  25.1 9.4 %collective-permute-start.10 = (bf16[33,16,128]{2,1,0:T(8,128)(2,1)S(1)}, bf16[33,16,128]{2,1,0:T(8,128)(2,1)S(1)}, u32[]{:S(2)}, u32[]{:S(2)}) collective-permute-start(bf16[33,16,128]{2,1,0:T(8,128)(2,1)S(1)} %collective-permute-done.9.refs_10_), channel_id=1, source_target_pairs={{0,1},{1,0},{2,3},{3,2},{4,5},{5,4},{6,7},{7,6},{8,9},{9,8},{10,11... | collective-permute-start | bytes 405512 | tf_op jit(solution)/shard_map/ppermute | solution.py:427
  27.6 7.0 %collective-permute-start.6 = (bf16[33,16,128]{2,1,0:T(8,128)(2,1)S(1)}, bf16[33,16,128]{2,1,0:T(8,128)(2,1)S(1)}, u32[]{:S(2)}, u32[]{:S(2)}) collective-permute-start(bf16[33,16,128]{2,1,0:T(8,128)(2,1)S(1)} %collective-permute-done.5.refs_6_), channel_id=1, source_target_pairs={{0,1},{1,0},{2,3},{3,2},{4,5},{5,4},{6,7},{7,6},{8,9},{9,8},{10,11... | collective-permute-start | bytes 405512 | tf_op jit(solution)/shard_map/ppermute | solution.py:427

commit v5 on v4

--- a/solution.py
+++ b/solution.py
@@ -182,10 +182,16 @@
     content_hbm,
     switch_hbm,
     final_hbm,
+    weight_hbm,
+    gain_hbm,
+    rows_hbm,
     gate_ref,
     right_ref,
     value_ref,
     result_ref,
+    weight_ref,
+    gain_ref,
+    rows_ref,
     latter_ref,
     content_ref,
     switch_ref,
@@ -193,14 +199,14 @@
     sems,
 ):
     copies = fetch(
-        (latter_hbm, content_hbm, switch_hbm, final_hbm),
-        (latter_ref, content_ref, switch_ref, final_ref),
+        (latter_hbm, content_hbm, switch_hbm, final_hbm, weight_hbm, gain_hbm, rows_hbm),
+        (latter_ref, content_ref, switch_ref, final_ref, weight_ref, gain_ref, rows_ref),
         sems,
     )
     half, toks, lanes = seqs // 2, pack_ref.shape[1], pack_ref.shape[2]
     factor, width = latter_ref.shape
     rows = pack_ref[:half].reshape(half * toks, lanes)
-    for copy in copies:
+    for copy in copies[:4]:
         copy.wait()
     spread = jnp.where(
         iota((8 * factor, factor), 0) // 8 == iota((8 * factor, factor), 1), 1.0, 0.0
@@ -224,14 +230,16 @@
                 row = [mine, zero] if s2 == 0 else [zero, mine]
                 value_ref[hp, base : base + width, :] = jnp.concatenate(row, 1).astype(BF16)
         result_ref[hp] = twice(final_ref[:, cols])
+    for copy in copies[4:]:
+        copy.wait()
 
 
 def main_kernel(seqs, heads, shifts, *refs):
     blocks = refs[: len(shifts)]
     (
-        rows_hbm,
-        weight_hbm,
-        gain_hbm,
+        rows_ref,
+        weight_ref,
+        gain_ref,
         turned_ref,
         folded_ref,
         gate_ref,
@@ -240,9 +248,6 @@
         result_ref,
         out_hbm,
         pair_hbm,
-        rows_ref,
-        weight_ref,
-        gain_ref,
         out_ref,
         pair_ref,
         mask_scr,
@@ -254,11 +259,6 @@
         sems,
         pair_sem,
     ) = refs[len(shifts) :]
-    copies = fetch(
-        (weight_hbm, gain_hbm, rows_hbm),
-        (weight_ref, gain_ref, rows_ref),
-        sems,
-    )
     half = seqs // 2
     outer = seqs // 8
     devs = len(shifts)
@@ -284,8 +284,6 @@
             right = dot_nt(right_ref[...], rows).reshape(factor, 8, tokens)
             pieces.append(right * mask_scr[n * 8 : n * 8 + 8, :])
         rhs_scr[:, so * 8 : so * 8 + 16, :] = jnp.concatenate(pieces, axis=1).astype(BF16)
-    for copy in copies[:2]:
-        copy.wait()
     w_high, w_low = split(weight_ref[...] * gain_ref[...])
     weights = jnp.concatenate([w_high, w_low], axis=0)
     w_sum = jnp.sum(w_high.astype(F32) + w_low.astype(F32), axis=1, keepdims=True)
@@ -346,7 +344,6 @@
         gated = (gate_ref[hp] * average).astype(BF16)
         part = dot_nt(gated, result_ref[hp])
         total = part if total is None else total + part
-    copies[2].wait()
     width = rows_ref.shape[2]
     total = total.reshape(outer, 4, toks, lanes)
     base = rows_ref[...].astype(F32).reshape(outer, 2, 4, toks, width)
@@ -358,7 +355,7 @@
         if so % 2:
             here = pl.ds(so // 2 * 16, 16)
             stores.append(
-                pltpu.make_async_copy(out_ref.at[here], out_hbm.at[here], sems.at[3 + so // 2])
+                pltpu.make_async_copy(out_ref.at[here], out_hbm.at[here], sems.at[so // 2])
             )
             stores[-1].start()
     for i in range(toks):
@@ -461,23 +458,25 @@
         sigmoid_switch_proj,
         final_result_proj.T,
     )
-    gate, right, value, result = pl.pallas_call(
+    others = (pair_logit_weight.T, pair_norm_gain[None], homolog_embedding)
+    gate, right, value, result, *extra = pl.pallas_call(
         functools.partial(gate_kernel, seqs, heads),
         out_shape=(
             jax.ShapeDtypeStruct((heads // 2, half * toks, lanes), F32),
             jax.ShapeDtypeStruct((8 * factor, 8 * width), BF16),
             jax.ShapeDtypeStruct((heads // 2, 4 * width, lanes), BF16),
             jax.ShapeDtypeStruct((heads // 2, lanes, lanes), BF16),
-        ),
-        in_specs=[VM] + [HB] * 4,
-        out_specs=(VM,) * 4,
-        scratch_shapes=room(*arrays) + [pltpu.SemaphoreType.DMA((4,))],
+        )
+        + tuple(jax.ShapeDtypeStruct(a.shape, a.dtype) for a in others),
+        in_specs=[VM] + [HB] * 7,
+        out_specs=(VM,) * 7,
+        scratch_shapes=room(*arrays) + [pltpu.SemaphoreType.DMA((7,))],
         compiler_params=params,
         cost_estimate=pl.CostEstimate(
             flops=10**8, bytes_accessed=10**6, transcendentals=10**6
         ),
         name="gate",
-    )(packed, *keep(*arrays))
+    )(packed, *keep(*arrays, *others))
     turned = pl.pallas_call(
         functools.partial(turn_kernel, shifts),
         out_shape=jax.ShapeDtypeStruct((toks, channels, tokens), BF16),
@@ -487,7 +486,6 @@
         cost_estimate=pl.CostEstimate(flops=10**7, bytes_accessed=10**6, transcendentals=0),
         name="turn",
     )(state)
-    arrays = (homolog_embedding, pair_logit_weight.T, pair_norm_gain[None])
     group = GROUP
     out, pair = pl.pallas_call(
         functools.partial(main_kernel, seqs, heads, shifts),
@@ -495,9 +493,9 @@
             jax.ShapeDtypeStruct(homolog_embedding.shape, BF16),
             jax.ShapeDtypeStruct(pair_state_tiles.shape, BF16),
         ),
-        in_specs=[VM] * devs + [HB] * 3 + [VM] * 6,
+        in_specs=[VM] * (devs + 9),
         out_specs=(HB, HB),
-        scratch_shapes=room(*arrays, homolog_embedding)
+        scratch_shapes=room(homolog_embedding)
         + [
             pltpu.VMEM(pair_state_tiles.shape, BF16),
             pltpu.VMEM((seqs + 8, tokens), F32),
@@ -506,7 +504,7 @@
             pltpu.VMEM((half, heads * toks, lanes), BF16),
             pltpu.VMEM((group * channels, tokens), F32),
             pltpu.VMEM((group * channels, tokens), F32),
-            pltpu.SemaphoreType.DMA((3 + outer // 2,)),
+            pltpu.SemaphoreType.DMA((outer // 2,)),
             pltpu.SemaphoreType.DMA((toks,)),
         ],
         compiler_params=params,
@@ -514,7 +512,9 @@
         name="main",
     )(
         *[held[shift] for shift in shifts],
-        *keep(*arrays),
+        extra[2],
+        extra[0],
+        extra[1],
         turned,
         folded,
         gate,

time: 40.8 us -> 40.6 us (level)
  no operation moved by 1% of the time
where the time goes in v5:
time: 40.6 us; the launch traced here: 40.3 us
  Pallas kernels  14.1 us (35%)
  waiting for transfers between devices  13 us (32%)
  starting transfers between devices  12.4 us (31%)
  between operations  0.72 us (2%)
    ppermute x15, waiting for transfers between devices, swap(): return lax.ppermute(block, 'row', [(n, n ^ shift) for n in range(devs)])  13 us
    ppermute x15, starting transfers between devices, swap(): return lax.ppermute(block, 'row', [(n, n ^ shift) for n in range(devs)])  12.4 us
    pallas_call x1, Pallas kernels, shards(): pl.pallas_call(functools.partial(main_kernel, seqs, heads, shifts), out_s...  5.74 us
    pallas_call x1, Pallas kernels, shards(): pl.pallas_call(functools.partial(fold_kernel, seqs), out_shape=(jax.Shape...  5.28 us
    pallas_call x1, Pallas kernels, shards(): pl.pallas_call(pack_kernel, out_shape=(jax.ShapeDtypeStruct((half + 1, to...  1.46 us
    pallas_call x1, Pallas kernels, shards(): pl.pallas_call(functools.partial(gate_kernel, seqs, heads), out_shape=(ja...  1.28 us
  transfers between devices with their start and end apart: 15, of which 4 were waited for; matrix products, arithmetic and copies ran while one was open for 0% of the time, Pallas kernels for 17%

profile of v5, /device:TPU:0, one launch (start us, length us, event | category | flops | bytes accessed | tf_op | source)
XLA Modules:
  0.0 40.3 jit_solution(8569156265733392769)
XLA Ops:
  0.6 1.5 %pack.1 = (bf16[33,16,128]{2,1,0:T(8,128)(2,1)S(1)}, bf16[32,64]{1,0:T(8,128)(2,1)S(1)}) custom-call(bf16[64,16,64]{2,1,0:T(8,128)(2,1)} %rows_hbm.3, s32[16,64]{1,0:T(8,128)} %bitcast.8, f32[1,64]{1,0:T(1,128)} %bitcast.11, s32[1,256]{1,0:T(1,128)} %bitcast.10, bf16[32,64]{1,0:T(8,128)(2,1)} %bitcast.9), custom_call_target="tpu_custom_call" | custom-call | tf_op jit(solution)/shard_map/pack/pallas_call | solution.py:410
  2.1 5.1 %collective-permute-start.11 = (bf16[33,16,128]{2,1,0:T(8,128)(2,1)S(1)}, bf16[33,16,128]{2,1,0:T(8,128)(2,1)S(1)}, u32[]{:S(2)}, u32[]{:S(2)}) collective-permute-start(bf16[33,16,128]{2,1,0:T(8,128)(2,1)S(1)} %get-tuple-element.13.pack_ref.refs_0_), channel_id=1, source_target_pairs={{0,12},{1,13},{2,14},{3,15},{4,8},{5,9},{6,10},{7,11},{8,4},{9,5},... | collective-permute-start | bytes 405512 | tf_op jit(solution)/shard_map/ppermute | solution.py:424
  7.2 0.0 collective-permute-start.7
  7.2 0.6 %collective-permute-start.3 = (bf16[33,16,128]{2,1,0:T(8,128)(2,1)S(1)}, bf16[33,16,128]{2,1,0:T(8,128)(2,1)S(1)}, u32[]{:S(2)}, u32[]{:S(2)}) collective-permute-start(bf16[33,16,128]{2,1,0:T(8,128)(2,1)S(1)} %get-tuple-element.13.pack_ref.refs_0_), channel_id=1, source_target_pairs={{0,4},{1,5},{2,6},{3,7},{4,0},{5,1},{6,2},{7,3},{8,12},{9,13},{10,... | collective-permute-start | bytes 405512 | tf_op jit(solution)/shard_map/ppermute | solution.py:424
  7.9 1.7 %collective-permute-start.1 = (bf16[33,16,128]{2,1,0:T(8,128)(2,1)S(1)}, bf16[33,16,128]{2,1,0:T(8,128)(2,1)S(1)}, u32[]{:S(2)}, u32[]{:S(2)}) collective-permute-start(bf16[33,16,128]{2,1,0:T(8,128)(2,1)S(1)} %get-tuple-element.13.pack_ref.refs_0_), channel_id=1, source_target_pairs={{0,2},{1,3},{2,0},{3,1},{4,6},{5,7},{6,4},{7,5},{8,10},{9,11},{10,... | collective-permute-start | bytes 405512 | tf_op jit(solution)/shard_map/ppermute | solution.py:424
  9.5 0.0 collective-permute-start
  9.6 2.2 %collective-permute-done.11.refs_12_ = bf16[33,16,128]{2,1,0:T(8,128)(2,1)S(1)} collective-permute-done((bf16[33,16,128]{2,1,0:T(8,128)(2,1)S(1)}, bf16[33,16,128]{2,1,0:T(8,128)(2,1)S(1)}, u32[]{:S(2)}, u32[]{:S(2)}) %collective-permute-start.11) | collective-permute-done | bytes 135200 | tf_op jit(solution)/shard_map/ppermute | solution.py:424
  11.8 1.7 %collective-permute-start.13 = (bf16[33,16,128]{2,1,0:T(8,128)(2,1)S(1)}, bf16[33,16,128]{2,1,0:T(8,128)(2,1)S(1)}, u32[]{:S(2)}, u32[]{:S(2)}) collective-permute-start(bf16[33,16,128]{2,1,0:T(8,128)(2,1)S(1)} %collective-permute-done.11.refs_12_), channel_id=1, source_target_pairs={{0,2},{1,3},{2,0},{3,1},{4,6},{5,7},{6,4},{7,5},{8,10},{9,11},{10,... | collective-permute-start | bytes 405512 | tf_op jit(solution)/shard_map/ppermute | solution.py:424
  13.5 5.2 %collective-permute-done.7.refs_8_ = bf16[33,16,128]{2,1,0:T(8,128)(2,1)S(1)} collective-permute-done((bf16[33,16,128]{2,1,0:T(8,128)(2,1)S(1)}, bf16[33,16,128]{2,1,0:T(8,128)(2,1)S(1)}, u32[]{:S(2)}, u32[]{:S(2)}) %collective-permute-start.7) | collective-permute-done | bytes 135200 | tf_op jit(solution)/shard_map/ppermute | solution.py:424
  18.7 0.0 collective-permute-start.12
  18.7 0.0 collective-permute-done.3.refs_4_
  18.7 1.5 %collective-permute-start.9 = (bf16[33,16,128]{2,1,0:T(8,128)(2,1)S(1)}, bf16[33,16,128]{2,1,0:T(8,128)(2,1)S(1)}, u32[]{:S(2)}, u32[]{:S(2)}) collective-permute-start(bf16[33,16,128]{2,1,0:T(8,128)(2,1)S(1)} %collective-permute-done.7.refs_8_), channel_id=1, source_target_pairs={{0,2},{1,3},{2,0},{3,1},{4,6},{5,7},{6,4},{7,5},{8,10},{9,11},{10,... | collective-permute-start | bytes 405512 | tf_op jit(solution)/shard_map/ppermute | solution.py:424
  20.2 0.0 collective-permute-done.1.refs_2_
  20.2 0.2 collective-permute-start.8
  20.4 0.0 collective-permute-done.refs_1_
  20.4 0.5 %collective-permute-start.5 = (bf16[33,16,128]{2,1,0:T(8,128)(2,1)S(1)}, bf16[33,16,128]{2,1,0:T(8,128)(2,1)S(1)}, u32[]{:S(2)}, u32[]{:S(2)}) collective-permute-start(bf16[33,16,128]{2,1,0:T(8,128)(2,1)S(1)} %collective-permute-done.3.refs_4_), channel_id=1, source_target_pairs={{0,2},{1,3},{2,0},{3,1},{4,6},{5,7},{6,4},{7,5},{8,10},{9,11},{10,... | collective-permute-start | bytes 405512 | tf_op jit(solution)/shard_map/ppermute | solution.py:424
  20.9 0.0 collective-permute-done.13.refs_14_
  20.9 0.0 collective-permute-start.4
  20.9 0.0 collective-permute-done.12.refs_13_
  20.9 0.5 %collective-permute-start.2 = (bf16[33,16,128]{2,1,0:T(8,128)(2,1)S(1)}, bf16[33,16,128]{2,1,0:T(8,128)(2,1)S(1)}, u32[]{:S(2)}, u32[]{:S(2)}) collective-permute-start(bf16[33,16,128]{2,1,0:T(8,128)(2,1)S(1)} %collective-permute-done.1.refs_2_), channel_id=1, source_target_pairs={{0,1},{1,0},{2,3},{3,2},{4,5},{5,4},{6,7},{7,6},{8,9},{9,8},{10,11... | collective-permute-start | bytes 405512 | tf_op jit(solution)/shard_map/ppermute | solution.py:424
  21.5 3.7 %collective-permute-done.9.refs_10_ = bf16[33,16,128]{2,1,0:T(8,128)(2,1)S(1)} collective-permute-done((bf16[33,16,128]{2,1,0:T(8,128)(2,1)S(1)}, bf16[33,16,128]{2,1,0:T(8,128)(2,1)S(1)}, u32[]{:S(2)}, u32[]{:S(2)}) %collective-permute-start.9) | collective-permute-done | bytes 135200 | tf_op jit(solution)/shard_map/ppermute | solution.py:424
  25.1 0.0 collective-permute-start.14
  25.1 0.0 collective-permute-done.8.refs_9_
  25.1 0.5 %collective-permute-start.10 = (bf16[33,16,128]{2,1,0:T(8,128)(2,1)S(1)}, bf16[33,16,128]{2,1,0:T(8,128)(2,1)S(1)}, u32[]{:S(2)}, u32[]{:S(2)}) collective-permute-start(bf16[33,16,128]{2,1,0:T(8,128)(2,1)S(1)} %collective-permute-done.9.refs_10_), channel_id=1, source_target_pairs={{0,1},{1,0},{2,3},{3,2},{4,5},{5,4},{6,7},{7,6},{8,9},{9,8},{10,11... | collective-permute-start | bytes 405512 | tf_op jit(solution)/shard_map/ppermute | solution.py:424
  25.6 1.9 %collective-permute-done.5.refs_6_ = bf16[33,16,128]{2,1,0:T(8,128)(2,1)S(1)} collective-permute-done((bf16[33,16,128]{2,1,0:T(8,128)(2,1)S(1)}, bf16[33,16,128]{2,1,0:T(8,128)(2,1)S(1)}, u32[]{:S(2)}, u32[]{:S(2)}) %collective-permute-start.5) | collective-permute-done | bytes 135200 | tf_op jit(solution)/shard_map/ppermute | solution.py:424
  27.6 0.0 collective-permute-start.6
  27.6 5.3 %fold.1 = (bf16[16,128,2048]{2,1,0:T(8,128)(2,1)S(1)}, bf16[16,256,128]{2,1,0:T(8,128)(2,1)S(1)}) custom-call(bf16[33,16,128]{2,1,0:T(8,128)(2,1)S(1)} %get-tuple-element.13.pack_ref.refs_0_, bf16[32,64]{1,0:T(8,128)(2,1)S(1)} %get-tuple-element.17.former_ref, bf16[1024,128]{1,0:T(8,128)(2,1)} %outer_hbm.1, bf16[16,256,128]{2,1,0:T(8,128)(2,1)} %state_hbm.1), custom_call_target="tpu_custom_call" | custom-call | flops 1000000000 | bytes 10000000 | tf_op jit(solution)/shard_map/fold/pallas_call | solution.py:435
  32.9 0.4 turn.1.refs_19_
  33.2 1.3 %gate.1 = (f32[4,512,128]{2,1,0:T(8,128)S(1)}, bf16[256,512]{1,0:T(8,128)(2,1)S(1)}, bf16[4,256,128]{2,1,0:T(8,128)(2,1)S(1)}, bf16[4,128,128]{2,1,0:T(8,128)(2,...) custom-call(bf16[33,16,128]{2,1,0:T(8,128)(2,1)S(1)} %get-tuple-element.13.pack_ref.refs_0_, ...), custom_call_target="tpu_custom_call" | custom-call | flops 100000000 | bytes 1000000 | tf_op jit(solution)/shard_map/gate/pallas_call | solution.py:462
  34.5 0.0 collective-permute-done.4.refs_5_
  34.5 0.0 collective-permute-done.2.refs_3_
  34.6 0.0 collective-permute-done.14.refs_15_
  34.6 0.0 collective-permute-done.10.refs_11_
  34.6 0.0 collective-permute-done.6.refs_7_
  34.6 5.7 %main.1 = (bf16[64,16,64]{2,1,0:T(8,128)(2,1)}, bf16[16,256,128]{2,1,0:T(8,128)(2,1)}) custom-call(bf16[33,16,128]{2,1,0:T(8,128)(2,1)S(1)} %get-tuple-element.13.pack_ref.refs_0_, bf16[33,16,128]{2,1,0:T(8,128)(2,1)S(1)} %collective-permute-done.refs_1_, bf16[33,16,128]{2,1,0:T(8,128)(2,1)S(1)} %collective-permute-done.1.refs_2_, ...), custom_call_target="tpu_custom_call" | custom-call | flops 4000000000 | bytes 10000000 | tf_op jit(solution)/shard_map/main/pallas_call | solution.py:490
Async XLA Ops:
  2.1 9.7 %collective-permute-start.11 = (bf16[33,16,128]{2,1,0:T(8,128)(2,1)S(1)}, bf16[33,16,128]{2,1,0:T(8,128)(2,1)S(1)}, u32[]{:S(2)}, u32[]{:S(2)}) collective-permute-start(bf16[33,16,128]{2,1,0:T(8,128)(2,1)S(1)} %get-tuple-element.13.pack_ref.refs_0_), channel_id=1, source_target_pairs={{0,12},{1,13},{2,14},{3,15},{4,8},{5,9},{6,10},{7,11},{8,4},{9,5},... | collective-permute-start | bytes 405512 | tf_op jit(solution)/shard_map/ppermute | solution.py:424
  7.2 11.4 %collective-permute-start.7 = (bf16[33,16,128]{2,1,0:T(8,128)(2,1)S(1)}, bf16[33,16,128]{2,1,0:T(8,128)(2,1)S(1)}, u32[]{:S(2)}, u32[]{:S(2)}) collective-permute-start(bf16[33,16,128]{2,1,0:T(8,128)(2,1)S(1)} %get-tuple-element.13.pack_ref.refs_0_), channel_id=1, source_target_pairs={{0,8},{1,9},{2,10},{3,11},{4,12},{5,13},{6,14},{7,15},{8,0},{9,1},... | collective-permute-start | bytes 405512 | tf_op jit(solution)/shard_map/ppermute | solution.py:424
  7.2 11.4 %collective-permute-start.3 = (bf16[33,16,128]{2,1,0:T(8,128)(2,1)S(1)}, bf16[33,16,128]{2,1,0:T(8,128)(2,1)S(1)}, u32[]{:S(2)}, u32[]{:S(2)}) collective-permute-start(bf16[33,16,128]{2,1,0:T(8,128)(2,1)S(1)} %get-tuple-element.13.pack_ref.refs_0_), channel_id=1, source_target_pairs={{0,4},{1,5},{2,6},{3,7},{4,0},{5,1},{6,2},{7,3},{8,12},{9,13},{10,... | collective-permute-start | bytes 405512 | tf_op jit(solution)/shard_map/ppermute | solution.py:424
  7.9 12.3 %collective-permute-start.1 = (bf16[33,16,128]{2,1,0:T(8,128)(2,1)S(1)}, bf16[33,16,128]{2,1,0:T(8,128)(2,1)S(1)}, u32[]{:S(2)}, u32[]{:S(2)}) collective-permute-start(bf16[33,16,128]{2,1,0:T(8,128)(2,1)S(1)} %get-tuple-element.13.pack_ref.refs_0_), channel_id=1, source_target_pairs={{0,2},{1,3},{2,0},{3,1},{4,6},{5,7},{6,4},{7,5},{8,10},{9,11},{10,... | collective-permute-start | bytes 405512 | tf_op jit(solution)/shard_map/ppermute | solution.py:424
  9.5 10.9 %collective-permute-start = (bf16[33,16,128]{2,1,0:T(8,128)(2,1)S(1)}, bf16[33,16,128]{2,1,0:T(8,128)(2,1)S(1)}, u32[]{:S(2)}, u32[]{:S(2)}) collective-permute-start(bf16[33,16,128]{2,1,0:T(8,128)(2,1)S(1)} %get-tuple-element.13.pack_ref.refs_0_), channel_id=1, source_target_pairs={{0,1},{1,0},{2,3},{3,2},{4,5},{5,4},{6,7},{7,6},{8,9},{9,8},{10,11... | collective-permute-start | bytes 405512 | tf_op jit(solution)/shard_map/ppermute | solution.py:424
  11.8 9.2 %collective-permute-start.13 = (bf16[33,16,128]{2,1,0:T(8,128)(2,1)S(1)}, bf16[33,16,128]{2,1,0:T(8,128)(2,1)S(1)}, u32[]{:S(2)}, u32[]{:S(2)}) collective-permute-start(bf16[33,16,128]{2,1,0:T(8,128)(2,1)S(1)} %collective-permute-done.11.refs_12_), channel_id=1, source_target_pairs={{0,2},{1,3},{2,0},{3,1},{4,6},{5,7},{6,4},{7,5},{8,10},{9,11},{10,... | collective-permute-start | bytes 405512 | tf_op jit(solution)/shard_map/ppermute | solution.py:424
  18.7 2.3 %collective-permute-start.12 = (bf16[33,16,128]{2,1,0:T(8,128)(2,1)S(1)}, bf16[33,16,128]{2,1,0:T(8,128)(2,1)S(1)}, u32[]{:S(2)}, u32[]{:S(2)}) collective-permute-start(bf16[33,16,128]{2,1,0:T(8,128)(2,1)S(1)} %collective-permute-done.11.refs_12_), channel_id=1, source_target_pairs={{0,1},{1,0},{2,3},{3,2},{4,5},{5,4},{6,7},{7,6},{8,9},{9,8},{10,11... | collective-permute-start | bytes 405512 | tf_op jit(solution)/shard_map/ppermute | solution.py:424
  18.7 6.5 %collective-permute-start.9 = (bf16[33,16,128]{2,1,0:T(8,128)(2,1)S(1)}, bf16[33,16,128]{2,1,0:T(8,128)(2,1)S(1)}, u32[]{:S(2)}, u32[]{:S(2)}) collective-permute-start(bf16[33,16,128]{2,1,0:T(8,128)(2,1)S(1)} %collective-permute-done.7.refs_8_), channel_id=1, source_target_pairs={{0,2},{1,3},{2,0},{3,1},{4,6},{5,7},{6,4},{7,5},{8,10},{9,11},{10,... | collective-permute-start | bytes 405512 | tf_op jit(solution)/shard_map/ppermute | solution.py:424
  20.2 4.9 %collective-permute-start.8 = (bf16[33,16,128]{2,1,0:T(8,128)(2,1)S(1)}, bf16[33,16,128]{2,1,0:T(8,128)(2,1)S(1)}, u32[]{:S(2)}, u32[]{:S(2)}) collective-permute-start(bf16[33,16,128]{2,1,0:T(8,128)(2,1)S(1)} %collective-permute-done.7.refs_8_), channel_id=1, source_target_pairs={{0,1},{1,0},{2,3},{3,2},{4,5},{5,4},{6,7},{7,6},{8,9},{9,8},{10,11... | collective-permute-start | bytes 405512 | tf_op jit(solution)/shard_map/ppermute | solution.py:424
  20.4 7.1 %collective-permute-start.5 = (bf16[33,16,128]{2,1,0:T(8,128)(2,1)S(1)}, bf16[33,16,128]{2,1,0:T(8,128)(2,1)S(1)}, u32[]{:S(2)}, u32[]{:S(2)}) collective-permute-start(bf16[33,16,128]{2,1,0:T(8,128)(2,1)S(1)} %collective-permute-done.3.refs_4_), channel_id=1, source_target_pairs={{0,2},{1,3},{2,0},{3,1},{4,6},{5,7},{6,4},{7,5},{8,10},{9,11},{10,... | collective-permute-start | bytes 405512 | tf_op jit(solution)/shard_map/ppermute | solution.py:424
  20.9 13.6 %collective-permute-start.4 = (bf16[33,16,128]{2,1,0:T(8,128)(2,1)S(1)}, bf16[33,16,128]{2,1,0:T(8,128)(2,1)S(1)}, u32[]{:S(2)}, u32[]{:S(2)}) collective-permute-start(bf16[33,16,128]{2,1,0:T(8,128)(2,1)S(1)} %collective-permute-done.3.refs_4_), channel_id=1, source_target_pairs={{0,1},{1,0},{2,3},{3,2},{4,5},{5,4},{6,7},{7,6},{8,9},{9,8},{10,11... | collective-permute-start | bytes 405512 | tf_op jit(solution)/shard_map/ppermute | solution.py:424
  20.9 13.6 %collective-permute-start.2 = (bf16[33,16,128]{2,1,0:T(8,128)(2,1)S(1)}, bf16[33,16,128]{2,1,0:T(8,128)(2,1)S(1)}, u32[]{:S(2)}, u32[]{:S(2)}) collective-permute-start(bf16[33,16,128]{2,1,0:T(8,128)(2,1)S(1)} %collective-permute-done.1.refs_2_), channel_id=1, source_target_pairs={{0,1},{1,0},{2,3},{3,2},{4,5},{5,4},{6,7},{7,6},{8,9},{9,8},{10,11... | collective-permute-start | bytes 405512 | tf_op jit(solution)/shard_map/ppermute | solution.py:424
  25.1 9.4 %collective-permute-start.14 = (bf16[33,16,128]{2,1,0:T(8,128)(2,1)S(1)}, bf16[33,16,128]{2,1,0:T(8,128)(2,1)S(1)}, u32[]{:S(2)}, u32[]{:S(2)}) collective-permute-start(bf16[33,16,128]{2,1,0:T(8,128)(2,1)S(1)} %collective-permute-done.13.refs_14_), channel_id=1, source_target_pairs={{0,1},{1,0},{2,3},{3,2},{4,5},{5,4},{6,7},{7,6},{8,9},{9,8},{10,11... | collective-permute-start | bytes 405512 | tf_op jit(solution)/shard_map/ppermute | solution.py:424
  25.1 9.4 %collective-permute-start.10 = (bf16[33,16,128]{2,1,0:T(8,128)(2,1)S(1)}, bf16[33,16,128]{2,1,0:T(8,128)(2,1)S(1)}, u32[]{:S(2)}, u32[]{:S(2)}) collective-permute-start(bf16[33,16,128]{2,1,0:T(8,128)(2,1)S(1)} %collective-permute-done.9.refs_10_), channel_id=1, source_target_pairs={{0,1},{1,0},{2,3},{3,2},{4,5},{5,4},{6,7},{7,6},{8,9},{9,8},{10,11... | collective-permute-start | bytes 405512 | tf_op jit(solution)/shard_map/ppermute | solution.py:424
  27.6 7.0 %collective-permute-start.6 = (bf16[33,16,128]{2,1,0:T(8,128)(2,1)S(1)}, bf16[33,16,128]{2,1,0:T(8,128)(2,1)S(1)}, u32[]{:S(2)}, u32[]{:S(2)}) collective-permute-start(bf16[33,16,128]{2,1,0:T(8,128)(2,1)S(1)} %collective-permute-done.5.refs_6_), channel_id=1, source_target_pairs={{0,1},{1,0},{2,3},{3,2},{4,5},{5,4},{6,7},{7,6},{8,9},{9,8},{10,11... | collective-permute-start | bytes 405512 | tf_op jit(solution)/shard_map/ppermute | solution.py:424
